TPU v7x, 32 devices: a whole 2x2x4 slice. The times are simulated.
32 devices in a mesh: dp: 2 (over x), ctx: 2 (over y), exp: 8 (over z, core).
Axes of the slice: x: 2, y: 2, z: 4, core: 2. Of those that a mesh axis runs over, the one named last changes fastest.
Arguments:
- tokens: float32 [16, 1536, 512], P(('dp', 'exp'), 'ctx'), may hold values from -6 to 6
- lengths: int32 [16, 3], P(('dp', 'exp')), may hold values from 1 to 1536, as said below
- routes: int32 [16, 1536, 8], P(('dp', 'exp'), 'ctx'), may hold values from 0 to 23, all different within a row; in each aligned block of 768 rows (0 to 767, 768 to 1535, ..., all dimensions but the last counted through in order) at most 320 rows name the same one
- route_gates: float32 [16, 1536, 8], P(('dp', 'exp'), 'ctx'), may hold values from 0.06 to 0.2
- cotangent: float32 [16, 1536, 512], P(('dp', 'exp'), 'ctx'), may hold values from -6 to 6
- gain_one: float32 [512], replicated, may hold values from 0.25 to 1.75
- shift_one: float32 [512], replicated, may hold values from -1 to 1
- kv_weight: float32 [512, 128], replicated, may hold values from -0.25 to 0.25
- query_weight: float32 [24, 512, 64], P('exp'), may hold values from -0.25 to 0.25
- out_weight: float32 [24, 64, 512], P('exp'), may hold values from -18 to 18
- gain_two: float32 [512], replicated, may hold values from 0.25 to 1.75
- shift_two: float32 [512], replicated, may hold values from -1 to 1
- up_weight: float32 [512, 2048], replicated, may hold values from -0.25 to 0.25
- up_bias: float32 [2048], replicated, may hold values from -1 to 1
- down_weight: float32 [2048, 512], replicated, may hold values from -0.125 to 0.125
- down_bias: float32 [512], replicated, may hold values from -1 to 1
Outputs:
- output: float32 [16, 1536, 512], P(('dp', 'exp'), 'ctx')
- grad_tokens: float32 [16, 1536, 512], P(('dp', 'exp'), 'ctx')
- grad_gain_one: float32 [512], replicated
- grad_shift_one: float32 [512], replicated
- grad_kv_weight: float32 [512, 128], replicated
- grad_query_weight: float32 [24, 512, 64], P('exp')
- grad_out_weight: float32 [24, 64, 512], P('exp')
- grad_gain_two: float32 [512], replicated
- grad_shift_two: float32 [512], replicated
- grad_up_weight: float32 [512, 2048], replicated
- grad_up_bias: float32 [2048], replicated
- grad_down_weight: float32 [2048, 512], replicated
- grad_down_bias: float32 [512], replicated
Inputs may be any that keep to these rules, and one draw needn't show every extreme that they name: Each row lists the lengths of 3 documents that lie end to end in this order and fill the 1536 tokens of the group. `routes`: each row names 8 different head experts; in the 768 rows of one device no head expert is named by more than 320 rows.
All inputs are finite; a program needn't handle non-finite values.
Results may differ from a plain program's by a relative error of at most 0.012.
Values may be sent and summed in bfloat16 or wider, within the bound.
A program may use at most 192 MiB of HBM per device.

v0:
```python
import jax
import jax.numpy as jnp
from jax import lax
from jax.sharding import PartitionSpec as P

D = 512
HEAD = 64
TOP = 8
EXP_DEV = 3
QT = 64


def layer_norm(values, ln_gain, ln_shift):
    center_val = values - jnp.mean(values, axis=-1, keepdims=True)
    var_val = jnp.mean(center_val * center_val, axis=-1, keepdims=True)
    return center_val * lax.rsqrt(var_val + 1e-05) * ln_gain + ln_shift


def local(
    tokens,
    lengths,
    routes,
    route_gates,
    cotangent,
    gain_one,
    shift_one,
    kv_weight,
    query_weight,
    out_weight,
    gain_two,
    shift_two,
    up_weight,
    up_bias,
    down_weight,
    down_bias,
):
    f32 = jnp.float32
    bf16 = jnp.bfloat16
    inputs = tokens[0]
    tok_count = inputs.shape[0]
    exp_size = lax.axis_size("exp")
    experts_all = EXP_DEV * exp_size
    capacity = tok_count * TOP * 5 // (4 * experts_all)
    route_flat = routes[0].reshape(-1)
    onehot = (route_flat[:, None] == jnp.arange(experts_all, dtype=jnp.int32)[None, :]).astype(
        jnp.int32
    )
    slot_rank = jnp.sum((jnp.cumsum(onehot, axis=0) - 1) * onehot, axis=1)
    slot_index = route_flat * capacity + slot_rank
    token_ids = jnp.arange(route_flat.shape[0], dtype=jnp.int32) // TOP
    slot_token = jnp.zeros((experts_all * capacity,), jnp.int32).at[slot_index].set(token_ids)
    slot_live = jnp.zeros((experts_all * capacity,), jnp.bool_).at[slot_index].set(True)

    def to_slots(row_data):
        row_width = row_data.shape[-1]
        flat_rows = row_data.reshape(-1, row_width) if row_data.ndim == 3 else row_data
        if row_data.ndim == 3:
            picked = flat_rows[route_of_slot]
        else:
            picked = flat_rows[slot_token]
        picked = jnp.where(slot_live[:, None], picked, jnp.zeros_like(picked))
        return picked.reshape(exp_size, EXP_DEV, capacity, row_width)

    route_of_slot = (
        jnp.zeros((experts_all * capacity,), jnp.int32)
        .at[slot_index]
        .set(jnp.arange(route_flat.shape[0], dtype=jnp.int32))
    )

    def from_slots(slot_data):
        row_width = slot_data.shape[-1]
        return slot_data.reshape(-1, row_width)[slot_index].reshape(tok_count, TOP, row_width)

    normed_one = layer_norm(inputs, gain_one, shift_one)
    act_one = normed_one.astype(bf16)
    kv_low = kv_weight.astype(bf16)
    keyval = jnp.dot(act_one, kv_low, preferred_element_type=f32).astype(bf16)
    keyval_all = lax.all_gather(keyval, "ctx", axis=0, tiled=True)
    row_slots = to_slots(act_one)
    query_low = query_weight.astype(bf16)
    outw_low = out_weight.astype(bf16)
    query_full, outw_full = (
        lax.all_gather(query_low, "exp", axis=0, tiled=True),
        lax.all_gather(outw_low, "exp", axis=0, tiled=True),
    )
    query_full = query_full.reshape(exp_size, EXP_DEV, D, HEAD)
    outw_full = outw_full.reshape(exp_size, EXP_DEV, HEAD, D)
    query_slots = jnp.einsum(
        "secd,sedh->sech", row_slots, query_full, preferred_element_type=f32
    ).astype(bf16)
    queries = from_slots(query_slots)
    ctx_index = lax.axis_index("ctx")
    group_len = keyval_all.shape[0]
    key_pos = jnp.arange(group_len, dtype=jnp.int32)
    doc_ends = jnp.cumsum(lengths[0])
    key_doc = jnp.sum((key_pos[:, None] >= doc_ends[None, :]).astype(jnp.int32), axis=1)
    query_pos = ctx_index * tok_count + jnp.arange(tok_count, dtype=jnp.int32)
    query_doc = lax.dynamic_slice_in_dim(key_doc, ctx_index * tok_count, tok_count)
    keys_part = keyval_all[:, :HEAD]
    values_part = keyval_all[:, HEAD:]
    num_blocks = tok_count // QT
    pos_blocks = query_pos.reshape(num_blocks, QT)
    doc_blocks = query_doc.reshape(num_blocks, QT)
    query_blocks = queries.reshape(num_blocks, QT, TOP, HEAD)

    def block_probs(query_blk, pos_blk, doc_blk):
        scores = jnp.einsum("tkh,jh->tkj", query_blk, keys_part, preferred_element_type=f32) * 0.125
        allowed = (key_pos[None, :] <= pos_blk[:, None]) & (key_doc[None, :] == doc_blk[:, None])
        scores = jnp.where(allowed[:, None, :], scores, -1e30)
        return jax.nn.softmax(scores, axis=-1)

    def attend(block_in):
        query_blk, pos_blk, doc_blk = block_in
        attn_probs = block_probs(query_blk, pos_blk, doc_blk)
        return jnp.einsum(
            "tkj,jh->tkh", attn_probs.astype(bf16), values_part, preferred_element_type=f32
        ).astype(bf16)

    context = lax.map(attend, (query_blocks, pos_blocks, doc_blocks)).reshape(tok_count, TOP, HEAD)
    context_slots = to_slots(context)
    branch_slots = jnp.einsum(
        "sech,sehd->secd", context_slots, outw_full, preferred_element_type=f32
    ).astype(bf16)
    branch = from_slots(branch_slots)
    gates_tok = route_gates[0]
    attn_out = jnp.einsum("tk,tkd->td", gates_tok, branch, preferred_element_type=f32)
    mid_stream = inputs + attn_out
    act_two = layer_norm(mid_stream, gain_two, shift_two).astype(bf16)
    up_low = up_weight.astype(bf16)
    down_low = down_weight.astype(bf16)
    hidden_pre = jnp.dot(act_two, up_low, preferred_element_type=f32) + up_bias
    hidden = jax.nn.gelu(hidden_pre).astype(bf16)
    output = mid_stream + jnp.dot(hidden, down_low, preferred_element_type=f32) + down_bias
    grad_out = cotangent[0]
    grad_ffn = grad_out.astype(bf16)
    grad_down_bias = jnp.sum(grad_ffn, axis=0, dtype=f32)
    grad_down = jnp.einsum("tf,td->fd", hidden, grad_ffn, preferred_element_type=f32)
    grad_hidden = jnp.einsum("td,fd->tf", grad_ffn, down_low, preferred_element_type=f32)
    gelu_pull = jax.vjp(jax.nn.gelu, hidden_pre)[1]
    grad_pre = gelu_pull(grad_hidden)[0].astype(bf16)
    grad_up_bias = jnp.sum(grad_pre, axis=0, dtype=f32)
    grad_up = jnp.einsum("td,tf->df", act_two, grad_pre, preferred_element_type=f32)
    grad_act_two = jnp.einsum("tf,df->td", grad_pre, up_low, preferred_element_type=f32)
    norm_two_pull = jax.vjp(layer_norm, mid_stream, gain_two, shift_two)[1]
    grad_mid_ln, grad_gain_two, grad_shift_two = norm_two_pull(grad_act_two)
    grad_mid = grad_out + grad_mid_ln
    grad_branch = (gates_tok[:, :, None] * grad_mid[:, None, :]).astype(bf16)
    grad_branch_slots = to_slots(grad_branch)
    grad_out_full = jnp.einsum(
        "sech,secd->sehd", context_slots, grad_branch_slots, preferred_element_type=f32
    )
    grad_context_slots = jnp.einsum(
        "secd,sehd->sech", grad_branch_slots, outw_full, preferred_element_type=f32
    ).astype(bf16)
    grad_context = from_slots(grad_context_slots)

    def attend_back(key_acc, block_in):
        query_blk, pos_blk, doc_blk, grad_blk = block_in
        attn_probs = block_probs(query_blk, pos_blk, doc_blk)
        grad_probs = jnp.einsum("tkh,jh->tkj", grad_blk, values_part, preferred_element_type=f32)
        grad_scores = (
            attn_probs * (grad_probs - jnp.sum(attn_probs * grad_probs, axis=-1, keepdims=True))
        ).astype(bf16)
        grad_query = (
            jnp.einsum("tkj,jh->tkh", grad_scores, keys_part, preferred_element_type=f32) * 0.125
        ).astype(bf16)
        grad_keys = (
            jnp.einsum("tkj,tkh->jh", grad_scores, query_blk, preferred_element_type=f32) * 0.125
        )
        grad_values = jnp.einsum(
            "tkj,tkh->jh", attn_probs.astype(bf16), grad_blk, preferred_element_type=f32
        )
        return (key_acc + jnp.concatenate([grad_keys, grad_values], axis=1), grad_query)

    key_init = jnp.zeros((group_len, 2 * HEAD), f32)
    grad_keyval_full, grad_query_blocks = lax.scan(
        attend_back,
        key_init,
        (query_blocks, pos_blocks, doc_blocks, grad_context.reshape(num_blocks, QT, TOP, HEAD)),
    )
    grad_queries = grad_query_blocks.reshape(tok_count, TOP, HEAD)
    grad_keyval = lax.psum_scatter(grad_keyval_full, "ctx", scatter_dimension=0, tiled=True).astype(
        bf16
    )
    grad_kv_weight = jnp.einsum("td,tc->dc", act_one, grad_keyval, preferred_element_type=f32)
    grad_act_one = jnp.einsum("tc,dc->td", grad_keyval, kv_low, preferred_element_type=f32)
    grad_query_slots = to_slots(grad_queries)
    grad_query_full = jnp.einsum(
        "secd,sech->sedh", row_slots, grad_query_slots, preferred_element_type=f32
    )
    grad_rows_slots = jnp.einsum(
        "sech,sedh->secd", grad_query_slots, query_full, preferred_element_type=f32
    ).astype(bf16)
    grad_query_weight, grad_out_weight = (
        lax.psum_scatter(
            grad_query_full.reshape(experts_all, D, HEAD), "exp", scatter_dimension=0, tiled=True
        ),
        lax.psum_scatter(
            grad_out_full.reshape(experts_all, HEAD, D), "exp", scatter_dimension=0, tiled=True
        ),
    )
    grad_query_weight, grad_out_weight = lax.psum(
        (grad_query_weight, grad_out_weight), ("dp", "ctx")
    )
    grad_rows = from_slots(grad_rows_slots)
    grad_act_one = grad_act_one + jnp.sum(grad_rows, axis=1, dtype=f32)
    norm_one_pull = jax.vjp(layer_norm, inputs, gain_one, shift_one)[1]
    grad_in_ln, grad_gain_one, grad_shift_one = norm_one_pull(grad_act_one)
    grad_inputs = grad_mid + grad_in_ln
    dense_sums = lax.psum(
        (
            grad_gain_one,
            grad_shift_one,
            grad_kv_weight,
            grad_gain_two,
            grad_shift_two,
            grad_up,
            grad_up_bias,
            grad_down,
            grad_down_bias,
        ),
        ("dp", "ctx", "exp"),
    )
    (
        sum_gain_one,
        sum_shift_one,
        sum_kv_weight,
        sum_gain_two,
        sum_shift_two,
        sum_up,
        sum_up_bias,
        sum_down,
        sum_down_bias,
    ) = dense_sums
    return (
        output[None],
        grad_inputs[None],
        sum_gain_one,
        sum_shift_one,
        sum_kv_weight,
        grad_query_weight,
        grad_out_weight,
        sum_gain_two,
        sum_shift_two,
        sum_up,
        sum_up_bias,
        sum_down,
        sum_down_bias,
    )


def solution(mesh):
    in_specs = (
        P(("dp", "exp"), "ctx", None),
        P(("dp", "exp"), None),
        P(("dp", "exp"), "ctx", None),
        P(("dp", "exp"), "ctx", None),
        P(("dp", "exp"), "ctx", None),
        P(),
        P(),
        P(),
        P("exp", None, None),
        P("exp", None, None),
        P(),
        P(),
        P(),
        P(),
        P(),
        P(),
    )
    out_specs = (
        P(("dp", "exp"), "ctx", None),
        P(("dp", "exp"), "ctx", None),
        P(),
        P(),
        P(),
        P("exp", None, None),
        P("exp", None, None),
        P(),
        P(),
        P(),
        P(),
        P(),
        P(),
    )
    return jax.shard_map(local, mesh=mesh, in_specs=in_specs, out_specs=out_specs, check_vma=False)
```

profile of v0, /device:TPU:0, one launch (start us, length us, event | category | flops | bytes accessed | tf_op | source)
XLA Modules:
  0.0 896.8 jit_solution(12855102576403496717)
XLA Ops:
  12.9 7.1 reduce-window.18
  22.4 23.0 %scatter_custom_fusion.1 = s32[7680]{0:T(1024)S(1)} fusion(s32[6144]{0:T(1024)S(1)} %bitcast.241, s32[6144]{0:T(1024)S(1)} %add_select_fusion, s32[]{:T(128)} %constant.104.clone.1), kind=kCustom, calls=%fused_computation.177 | custom fusion | bytes 30724 | tf_op jit(solution)/shard_map/scatter | solution.py:51
  45.5 26.1 %scatter_custom_fusion = pred[7680]{0:T(1024)(128)(4,1)S(1)} fusion(s32[6144]{0:T(1024)S(1)} %bitcast.242, pred[6144]{0:T(1024)(128)(4,1)S(1)} %broadcast.276, pred[]{:T(512)} %constant.102.clone.1), kind=kCustom, calls=%fused_computation.179 | custom fusion | bytes 7681 | tf_op jit(solution)/shard_map/scatter | solution.py:52
  72.1 22.2 %gather_fusion = bf16[7680,512]{1,0:T(8,128)(2,1)} fusion(bf16[768,512]{1,0:T(8,128)(2,1)S(1)} %add_convert_fusion.1, s32[8192]{0:T(1024)S(1)} %pad_clamp_fusion.1), kind=kCustom, calls=%fused_computation | custom fusion | bytes 15759360 | tf_op jit(solution)/shard_map/gather | solution.py:60
  94.7 8.5 all_gather.10
  106.1 23.2 %scatter_custom_fusion.2 = s32[7680]{0:T(1024)S(1)} fusion(s32[6144]{0:T(1024)S(1)} %bitcast.243, s32[6144]{0:T(1024)S(1)} %iota.43, s32[]{:T(128)} %constant.104.clone.1), kind=kCustom, calls=%fused_computation.175 | custom fusion | bytes 30724 | tf_op jit(solution)/shard_map/scatter | solution.py:67
  132.0 5.8 fusion.93
  139.9 24.3 %gather_fusion.1 = bf16[6144,64]{1,0:T(8,128)(2,1)} fusion(bf16[7680,64]{1,0:T(8,128)(2,1)S(1)} %bitcast.221, s32[6144]{0:T(1024)} %broadcast_clamp_fusion), kind=kCustom, calls=%fused_computation.1 | custom fusion | bytes 1597440 | tf_op jit(solution)/shard_map/gather | solution.py:72
  164.4 87.2 %while.24 = (s32[]{:T(128)}, bf16[12,64,8,64]{3,2,1,0:T(8,128)(2,1)S(1)}, s32[12,64]{1,0:T(8,128)S(1)}, s32[1536]{0:T(1024)S(1)}, s32[12,64]{1,0:T(8,128)}, /*in...) while((s32[]{:T(128)}, ...), condition=%wide.region_12.13_spmd.clone, body=%wide.region_9.12_spmd.clone.sunk | while | flops 206374400 | bytes 7186533 | solution.py:119
  165.3 3.8 fusion.191
  172.6 3.8 fusion.191
  179.8 3.8 fusion.191
  187.1 3.8 fusion.191
  194.4 3.8 fusion.191
  201.6 3.8 fusion.191
  208.9 3.8 fusion.191
  216.2 3.8 fusion.191
  223.4 3.8 fusion.191
  230.7 3.8 fusion.191
  238.0 3.8 fusion.191
  245.2 3.8 fusion.191
  251.7 16.3 %gather_fusion.2 = bf16[7680,64]{1,0:T(8,128)(2,1)} fusion(bf16[6144,64]{1,0:T(8,128)(2,1)S(1)} %bitcast.220, s32[8192]{0:T(1024)S(1)} %copy-done.29), kind=kCustom, calls=%fused_computation.2 | custom fusion | bytes 1996800 | tf_op jit(solution)/shard_map/gather | solution.py:58
  270.1 7.2 convolution_convert_fusion.1
  277.3 30.3 %gather_fusion.3 = bf16[6144,512]{1,0:T(8,128)(2,1)} fusion(bf16[7680,512]{1,0:T(8,128)(2,1)} %bitcast.218, s32[6144]{0:T(1024)S(1)} %copy-done.26), kind=kCustom, calls=%fused_computation.3 | custom fusion | bytes 12607488 | tf_op jit(solution)/shard_map/gather | solution.py:72
  307.7 4.6 fusion.86
  317.7 6.3 convert_reduce_fusion.1
  332.9 26.3 %gather_fusion.4 = bf16[7680,512]{1,0:T(8,128)(2,1)} fusion(bf16[6144,512]{1,0:T(8,128)(2,1)} %fusion.74, s32[8192]{0:T(1024)S(1)} %copy-done.29), kind=kCustom, calls=%fused_computation.4 | custom fusion | bytes 15759360 | tf_op jit(solution)/shard_map/gather | solution.py:58
  359.1 5.6 fusion.92
  365.8 22.2 %gather_fusion.5 = bf16[6144,64]{1,0:T(8,128)(2,1)} fusion(bf16[7680,64]{1,0:T(8,128)(2,1)S(1)} %bitcast.222, s32[6144]{0:T(1024)S(1)} %copy-done.27), kind=kCustom, calls=%fused_computation.5 | custom fusion | bytes 1597440 | tf_op jit(solution)/shard_map/gather | solution.py:72
  388.4 141.4 %while.25 = (s32[]{:T(128)}, f32[1536,128]{0,1:T(8,128)S(1)}, bf16[12,64,8,64]{3,2,1,0:T(8,128)(2,1)S(1)}, s32[12,64]{1,0:T(8,128)}, s32[1536]{0:T(1024)S(1)}, /...) while((s32[]{:T(128)}, f32[1536,128]{0,1:T(8,128)S(1)}, ...), condition=%wide.region_22.23_spmd.clone, body=%wide.region_18.22_spmd.clone.sunk | while | flops 514589696 | bytes 40785568 | solution.py:176
  401.0 3.7 fusion.203
  424.6 3.7 fusion.203
  459.9 3.7 fusion.203
  483.5 3.7 fusion.203
  495.3 3.7 fusion.203
  530.7 5.9 fusion.77
  536.7 16.4 %gather_fusion.6 = bf16[7680,64]{1,0:T(8,128)(2,1)S(1)} fusion(bf16[6144,64]{1,0:T(8,128)(2,1)S(1)} %bitcast.219, s32[8192]{0:T(1024)} %pad_clamp_fusion), kind=kCustom, calls=%fused_computation.6 | custom fusion | bytes 1996800 | tf_op jit(solution)/shard_map/gather | solution.py:58
  554.2 7.3 fusion.75
  562.9 6.0 fusion.130
  569.0 8.3 fusion.123
  580.7 6.7 convolution_convert_fusion
  587.5 30.0 %gather_fusion.7 = bf16[6144,512]{1,0:T(8,128)(2,1)} fusion(bf16[7680,512]{1,0:T(8,128)(2,1)} %bitcast.217, s32[6144]{0:T(1024)S(1)} %copy-done.28), kind=kCustom, calls=%fused_computation.7 | custom fusion | bytes 12607488 | tf_op jit(solution)/shard_map/gather | solution.py:72
  617.5 7.2 convert_reduce_fusion
  624.8 6.7 add_bitcast_fusion.1
  632.5 42.6 %all-reduce = (f32[512]{0:T(512)}, f32[512]{0:T(512)}, f32[512]{0:T(512)}, f32[512]{0:T(512)}, f32[2048]{0:T(1024)}, /*index=5*/f32[512]{0:T(512)}) all-reduce(f32[512]{0:T(512)S(1)} %get-tuple-element.248, f32[512]{0:T(512)S(1)} %get-tuple-element.251, ...), channel_id=1, replica_groups=mesh['dp'=2,'ctx'=2,'exp'=8] {'dp','ctx','exp'}, use_global_device_ids=true, to_apply=%region_28.29 | all-reduce | flops 4608 | bytes 36864 | tf_op jit(solution)/shard_map/psum | solution.py:210
  677.9 147.2 %all-reduce.6.cloned.1.call-done = (f32[512,128]{1,0:T(8,128)}, f32[512,2048]{1,0:T(8,128)}, f32[2048,512]{1,0:T(8,128)}) async-done(((f32[512,128]{1,0:T(8,128)}, f32[512,2048]{1,0:T(8,128)}, f32[2048,512]{1,0:T(8,128)}), (f32[512,128]{1,0:T(8,128)}, f32[512,2048]{1,0:T(8,128)}, f32[2048,512]{1,0:T(8,128)})) %all-reduce.6.cloned.1.call-update) | async-done | bytes 8650768 | tf_op jit(solution)/shard_map/psum | solution.py:210
  825.1 52.4 %all-reduce.8.cloned.1.call-done = (f32[3,512,64]{1,2,0:T(8,128)}, f32[3,64,512]{2,1,0:T(8,128)}) async-done(((f32[3,512,64]{1,2,0:T(8,128)}, f32[3,64,512]{2,1,0:T(8,128)}), (f32[3,512,64]{1,2,0:T(8,128)}, f32[3,64,512]{2,1,0:T(8,128)})) %all-reduce.8.cloned.1.call-update) | async-done | bytes 786448 | tf_op jit(solution)/shard_map/psum | solution.py:202
  882.7 4.8 copy.120
  (370 shorter events, 214.9 us)
Async XLA Ops:
  7.2 5.0 copy-start.40
  7.2 5.1 copy-start.3
  7.2 124.8 %all-gather.3.cloned.1.call-start = ((), (), s32[]{:S(2)}) async-start(), calls=%async_computation.3 | async-start | bytes 1769472 | tf_op jit(solution)/shard_map/all_gather | solution.py:83
  9.1 261.0 %all-gather.5.cloned.1.call-start = ((), (), s32[]{:S(2)}) async-start(), calls=%async_computation.4 | async-start | bytes 1769472 | tf_op jit(solution)/shard_map/all_gather | solution.py:84
  10.9 566.4 %reduce-scatter.4.cloned.1.call-start = ((), (), s32[]{:S(2)}) async-start(), calls=%async_computation.5 | async-start | bytes 1179648 | tf_op jit(solution)/shard_map/reduce_scatter | solution.py:182
  12.5 59.2 %copy-start.34 = (f32[768]{0:T(1024)}, f32[768]{0:T(1024)S(1)}, u32[]{:S(2)}) copy-start(f32[768]{0:T(1024)S(1)} %broadcast_multiply_fusion.2) | copy-start | bytes 9220
  12.8 7.1 copy-start.45
  12.8 58.9 %copy-start.43 = (f32[768]{0:T(1024)}, f32[768]{0:T(1024)S(1)}, u32[]{:S(2)}) copy-start(f32[768]{0:T(1024)S(1)} %fusion.121) | copy-start | bytes 9220
  20.0 51.7 %copy-start.48 = (f32[512]{0:T(512)S(1)}, f32[512]{0:T(512)}, u32[]{:S(2)}) copy-start(f32[512]{0:T(512)} %param.25) | copy-start | bytes 6148
  20.0 51.7 %copy-start.52 = (f32[512]{0:T(512)S(1)}, f32[512]{0:T(512)}, u32[]{:S(2)}) copy-start(f32[512]{0:T(512)} %param.26) | copy-start | bytes 6148
  71.7 60.3 %copy-start.30 = (pred[8,3,320]{2,1,0:T(4,128)(4,1)}, pred[8,3,320]{2,1,0:T(4,128)(4,1)S(1)}, u32[]{:S(2)}) copy-start(pred[8,3,320]{2,1,0:T(4,128)(4,1)S(1)} %broadcast_in_dim.90) | copy-start | bytes 23044
  72.1 22.2 %copy-start = (bf16[768,512]{1,0:T(8,128)(2,1)}, bf16[768,512]{1,0:T(8,128)(2,1)S(1)}, u32[]{:S(2)}) copy-start(bf16[768,512]{1,0:T(8,128)(2,1)S(1)} %add_convert_fusion.1) | copy-start | bytes 2359300
  72.1 22.2 %copy-start.24 = (f32[512,128]{1,0:T(8,128)S(1)}, f32[512,128]{1,0:T(8,128)}, u32[]{:S(2)}) copy-start(f32[512,128]{1,0:T(8,128)} %param.27) | copy-start | bytes 786436
  94.7 10.4 %copy-start.60 = (s32[1,3]{1,0:T(1,128)S(1)}, s32[1,3]{1,0:T(1,128)}, u32[]{:S(2)}) copy-start(s32[1,3]{1,0:T(1,128)} %param.21) | copy-start | bytes 40
  94.7 35.3 %copy-start.39 = (f32[1,768,8]{1,2,0:T(8,128)S(1)}, f32[1,768,8]{1,2,0:T(8,128)}, u32[]{:S(2)}) copy-start(f32[1,768,8]{1,2,0:T(8,128)} %param.23) | copy-start | bytes 73732
  164.4 87.3 %copy-start.29 = (s32[8192]{0:T(1024)S(1)}, s32[8192]{0:T(1024)}, u32[]{:S(2)}) copy-start(s32[8192]{0:T(1024)} %pad_clamp_fusion) | copy-start | bytes 98308
  251.6 16.3 %copy-start.47 = (s32[12,64]{1,0:T(8,128)}, s32[12,64]{1,0:T(8,128)S(1)}, u32[]{:S(2)}) copy-start(s32[12,64]{1,0:T(8,128)S(1)} %get-tuple-element.576) | copy-start | bytes 9220
  270.1 7.3 copy-start.13
  270.1 7.2 copy-start.26
  277.3 30.4 %copy-start.19 = (bf16[768,8,1]{1,2,0:T(2,128)(2,1)S(1)}, bf16[768,8,1]{1,2,0:T(2,128)(2,1)}, u32[]{:S(2)}) copy-start(bf16[768,8,1]{1,2,0:T(2,128)(2,1)} %copy.85) | copy-start | bytes 36868
  312.6 14.3 %copy-start.5 = (f32[768,512]{1,0:T(8,128)}, f32[768,512]{1,0:T(8,128)S(1)}, u32[]{:S(2)}) copy-start(f32[768,512]{1,0:T(8,128)S(1)} %get-tuple-element.304) | copy-start | bytes 4718596
  317.7 6.3 copy-start.11
  332.9 26.3 %copy-start.23 = (bf16[24,64,512]{2,1,0:T(8,128)(2,1)S(1)}, bf16[24,64,512]{2,1,0:T(8,128)(2,1)}, u32[]{:S(2)}) copy-start(bf16[24,64,512]{2,1,0:T(8,128)(2,1)} %all-gather.5.cloned.1.call-done) | copy-start | bytes 4718596
  365.8 22.5 %copy-start.7 = (f32[1536,128]{0,1:T(8,128)S(1)}, f32[1536,128]{0,1:T(8,128)}, u32[]{:S(2)}) copy-start(f32[1536,128]{0,1:T(8,128)} %custom-call) | copy-start | bytes 2359300
  365.8 22.5 %copy-start.12 = (bf16[1536,64]{0,1:T(8,128)(2,1)S(1)}, bf16[1536,64]{0,1:T(8,128)(2,1)}, u32[]{:S(2)}) copy-start(bf16[1536,64]{0,1:T(8,128)(2,1)} %get-tuple-element.548) | copy-start | bytes 589828
  388.4 142.4 %copy-start.32 = (pred[8,3,320]{2,1,0:T(4,128)(4,1)S(1)}, pred[8,3,320]{2,1,0:T(4,128)(4,1)}, u32[]{:S(2)}) copy-start(pred[8,3,320]{2,1,0:T(4,128)(4,1)} %copy-done.30) | copy-start | bytes 23044
  393.0 3.0 copy-start.2
  404.8 3.0 copy-start.2
  416.6 3.0 copy-start.2
  530.7 144.4 %reduce-scatter.8.cloned.1.call-start = ((), (), s32[]{:S(2)}) async-start(), calls=%async_computation.7 | async-start | bytes 3538944 | tf_op jit(solution)/shard_map/reduce_scatter | solution.py:198
  536.7 138.4 %reduce-scatter.6.cloned.1.call-start = ((), (), s32[]{:S(2)}) async-start(), calls=%async_computation.6 | async-start | bytes 3538944 | tf_op jit(solution)/shard_map/reduce_scatter | solution.py:195
  554.2 7.3 copy-start.14
  561.5 7.4 copy-start.58
  561.5 263.6 %all-reduce.6.cloned.1.call-start = ((), (), s32[]{:S(2)}) async-start(), calls=%async_computation.8 | async-start | bytes 17301504 | tf_op jit(solution)/shard_map/psum | solution.py:210
  562.9 6.1 copy-start.21
  569.0 8.3 copy-start.1
  579.4 8.0 copy-start.28
  579.5 298.1 %all-reduce.8.cloned.1.call-start = ((), (), s32[]{:S(2)}) async-start(), calls=%async_computation.9 | async-start | bytes 1572864 | tf_op jit(solution)/shard_map/psum | solution.py:202
  617.5 7.3 copy-start.56
  617.5 7.3 copy-start.59
  624.7 6.7 copy-start.4
  624.7 6.7 copy-start.22
  624.8 6.7 copy-start.25
  624.8 6.7 copy-start.35
  624.8 6.7 copy-start.44
  624.8 6.7 copy-start.49
  631.6 43.5 %copy-start.46 = (f32[768]{0:T(1024)S(1)}, f32[768]{0:T(1024)}, u32[]{:S(2)}) copy-start(f32[768]{0:T(1024)} %copy-done.45) | copy-start | bytes 9220
  882.7 4.9 copy-start.17
  (31 other events, 64.2 us)
Sparse Core Ops, SparseCore 0:
  10.2 27.7 all-gather.2
  40.3 24.4 all-gather.4
  530.8 18.8 reduce-scatter.3
  552.0 40.3 reduce-scatter.7
  594.7 39.4 reduce-scatter.5
  642.4 182.7 all-reduce.5
  828.5 48.9 all-reduce.7
where the time goes:
time: 908 us; the launch traced here: 897 us
  local copies, waits for them, and re-layouts  313 us (34%)
  matrix products  274 us (30%)
  waiting for transfers between devices  200 us (22%)
  blocking collectives  51.1 us (6%)
  other arithmetic  41.2 us (5%)
  between operations  15.5 us (2%)
    psum x1, waiting for transfers between devices, local(): lax.psum((grad_gain_one, grad_shift_one, grad_kv_weight, grad_gain_two, g...  147 us
    gather x4, local copies, waits for them, and re-layouts, from_slots(): slot_data.reshape(-1, row_width)[slot_index]  107 us
    sub x24, matrix products, block_probs(): return jax.nn.softmax(scores, axis=-1)  90.9 us
    gather x5, local copies, waits for them, and re-layouts, to_slots(): picked = flat_rows[route_of_slot]  62.1 us
    psum x1, waiting for transfers between devices, local(): lax.psum((grad_query_weight, grad_out_weight), ('dp', 'ctx'))  52.4 us
    psum x1, blocking collectives, local(): lax.psum((grad_gain_one, grad_shift_one, grad_kv_weight, grad_gain_two, g...  42.6 us
    dot_general x12, matrix products, attend_back(): jnp.einsum('tkh,jh->tkj', grad_blk, values_part, preferred_element_type=f32)  34 us
    dot_general x12, matrix products, attend(): jnp.einsum('tkj,jh->tkh', attn_probs.astype(bf16), values_part, preferred...  30.8 us
  transfers between devices with their start and end apart: 7, of which 2 were waited for; matrix products, arithmetic and copies ran while one was open for 39% of the time, Pallas kernels for 0%

commit v1 on v0

v1 whole, which is shorter than its diff:
```python
import functools
import math

import jax
import jax.numpy as jnp
from jax import lax
from jax.experimental import pallas as pl
from jax.experimental.pallas import tpu as pltpu
from jax.sharding import PartitionSpec as P

f32 = jnp.float32
bf16 = jnp.bfloat16
D = 512
HEAD = 64
TOP = 8
TB = 128
W = TOP * TB
NEG = -1e30
LOG2E = math.log2(math.e)
LN2 = math.log(2.0)
SAFE = 50.0
NN = (((1,), (0,)), ((), ()))
NT = (((1,), (1,)), ((), ()))
TN = (((0,), (0,)), ((), ()))
C0 = math.sqrt(2 / math.pi)
C1 = 0.044715


def attn_fwd_kernel(cidx_ref, act_ref, wq_ref, routes_ref, gates_ref, qdoc_ref, kaug_ref, vt_ref, kn_ref,
                    cd_ref, q_ref, ctx_ref, lse_ref,
                    qt, qaug, s, acc, *, experts, tok, KB):
    i=pl.program_id(0)
    c=cidx_ref[0]
    qt[...]=lax.dot_general(wq_ref[...], act_ref[...], NT, preferred_element_type=f32)*(0.125*LOG2E)
    n2=[]
    for k0 in range(0,TOP,4):
        r=[jnp.broadcast_to(routes_ref[k0+k:k0+k+1,:],(8,TB))[None] for k in range(4)]
        sel=[jnp.zeros((HEAD//8,8,TB),f32) for _ in range(4)]
        for e in range(experts):
            v=qt[e*HEAD:(e+1)*HEAD,:].reshape(HEAD//8,8,TB)
            sel=[jnp.where(r[k]==e,v,sel[k]) for k in range(4)]
        for k in range(4):
            sk=sel[k].reshape(HEAD,TB)
            n2.append(jnp.max(jnp.sum(sk*sk,axis=0,keepdims=True)))
            qaug[0:HEAD,(k0+k)*TB:(k0+k+1)*TB]=sk.astype(bf16)
    n2=functools.reduce(jnp.maximum,n2)*kn_ref[0]
    fast=n2<=SAFE*SAFE
    q_ref[0]=qaug[0:HEAD,:]
    qd=qdoc_ref[...]
    qaug[HEAD:HEAD+16,:]=jnp.concatenate([jnp.concatenate([qd,jnp.zeros_like(qd)],0)]*TOP,1).astype(bf16)
    qaug[HEAD+16:,:]=jnp.zeros((128-HEAD-16,W),bf16)
    q0=c*tok+i*TB
    nfull=q0//KB
    kd=pl.multiple_of(nfull*KB,KB)
    kp=lax.broadcasted_iota(jnp.int32,(KB,TB),0)+(kd-q0)
    tp=lax.broadcasted_iota(jnp.int32,(KB,TB),1)
    mask=kp<=tp
    acc[...]=jnp.zeros_like(acc)
    def scores(k0,n):
        return jnp.dot(kaug_ref[pl.ds(k0,n),:],qaug[...],preferred_element_type=f32)
    def masked(x):
        return jnp.concatenate([jnp.where(mask,x[:,k*TB:(k+1)*TB],NEG) for k in range(TOP)],1)
    def pv(k0,n,p):
        acc[...]+=jnp.dot(vt_ref[:,pl.ds(k0,n)],p,preferred_element_type=f32)
    def finish(m):
        l=acc[HEAD:HEAD+1,:]
        lse_ref[0]=m+jnp.log2(l)
        acc[0:HEAD,:]=acc[0:HEAD,:]*(1.0/l)
    @pl.when(fast)
    def _():
        def body(b,_):
            k0=pl.multiple_of(b*KB,KB)
            pv(k0,KB,jnp.exp2(scores(k0,KB)).astype(bf16))
            return 0
        lax.fori_loop(0,nfull,body,0)
        pv(kd,KB,jnp.exp2(masked(scores(kd,KB))).astype(bf16))
        finish(0.0)
    @pl.when(jnp.logical_not(fast))
    def _():
        def spass(b,m):
            k0=pl.multiple_of(b*KB,KB)
            x=scores(k0,KB)
            s[pl.ds(k0,KB),:]=x
            return jnp.maximum(m,jnp.max(x.reshape(KB//8,8,W),axis=0))
        m=lax.fori_loop(0,nfull,spass,jnp.full((8,W),NEG*2,f32))
        x=masked(scores(kd,KB))
        s[pl.ds(kd,KB),:]=x
        m=jnp.maximum(m,jnp.max(x.reshape(KB//8,8,W),axis=0))
        m=jnp.max(m,axis=0,keepdims=True)
        def ppass(b,_):
            k0=pl.multiple_of(b*KB,KB)
            pv(k0,KB,jnp.exp2(s[pl.ds(k0,KB),:]-m).astype(bf16))
            return 0
        lax.fori_loop(0,nfull+1,ppass,0)
        finish(m)
    ctx_ref[0]=acc[0:HEAD,:]
    for k in range(TOP):
        acc[0:HEAD,k*TB:(k+1)*TB]*=gates_ref[k:k+1,:]
    r=[jnp.broadcast_to(routes_ref[k:k+1,:],(8,TB))[None] for k in range(TOP)]
    for h0 in range(0,HEAD,32):
        g=[acc[h0:h0+32,k*TB:(k+1)*TB].reshape(4,8,TB) for k in range(TOP)]
        for e in range(experts):
            o=jnp.zeros((4,8,TB),f32)
            for k in range(TOP):
                o=jnp.where(r[k]==e,g[k],o)
            cd_ref[e*HEAD+h0:e*HEAD+h0+32,:]=o.reshape(32,TB).astype(bf16)

def attn_fwd(cidx, act, wq, routesT, gatesT, qdoc, kaug, vt, kn, KB=256):
    tok=act.shape[0]; experts=wq.shape[0]//HEAD; keys=kaug.shape[0]; n=tok//TB; vr=vt.shape[0]
    full=lambda a: pl.BlockSpec(a.shape,lambda i,*_:(0,)*a.ndim)
    return pl.pallas_call(
        functools.partial(attn_fwd_kernel,experts=experts,tok=tok,KB=KB),
        grid_spec=pltpu.PrefetchScalarGridSpec(num_scalar_prefetch=1,grid=(n,),
          in_specs=[pl.BlockSpec((TB,D),lambda i,*_:(i,0)),full(wq),
            pl.BlockSpec((TOP,TB),lambda i,*_:(0,i)),pl.BlockSpec((TOP,TB),lambda i,*_:(0,i)),
            pl.BlockSpec((8,TB),lambda i,*_:(0,i)),full(kaug),full(vt),pl.BlockSpec(memory_space=pltpu.SMEM)],
          out_specs=[pl.BlockSpec((experts*HEAD,TB),lambda i,*_:(0,i)),
            pl.BlockSpec((1,HEAD,W),lambda i,*_:(i,0,0)),
            pl.BlockSpec((1,HEAD,W),lambda i,*_:(i,0,0)),
            pl.BlockSpec((1,1,W),lambda i,*_:(i,0,0))],
          scratch_shapes=[pltpu.VMEM((experts*HEAD,TB),f32),pltpu.VMEM((128,W),bf16),
            pltpu.VMEM((keys,W),f32),pltpu.VMEM((vr,W),f32)]),
        out_shape=[jax.ShapeDtypeStruct((experts*HEAD,tok),bf16),
          jax.ShapeDtypeStruct((n,HEAD,W),bf16),jax.ShapeDtypeStruct((n,HEAD,W),f32),
          jax.ShapeDtypeStruct((n,1,W),f32)],
        compiler_params=pltpu.CompilerParams(vmem_limit_bytes=60*2**20),
        name="attn_fwd",
    )(cidx,act,wq,routesT,gatesT,qdoc,kaug,vt,kn)


def split3(x):
    hi=x.astype(bf16).astype(f32); r=x-hi
    mid=r.astype(bf16).astype(f32); lo=r-mid
    return hi,mid,lo

def attn_bwd_kernel(cidx_ref, dct_ref, q_ref, ctx_ref, lse_ref, routes_ref, gates_ref, qdoc_ref,
                    kaug_ref, vaug_ref, kt_ref,
                    dqd_ref, dkv_ref,
                    qaug, daug, rhs, pds, dq, *, experts, tok, KB):
    i=pl.program_id(0)
    c=cidx_ref[0]
    @pl.when(i==0)
    def _():
        dkv_ref[...]=jnp.zeros_like(dkv_ref)
        rhs[...]=jnp.zeros_like(rhs)
    q=q_ref[0]
    qaug[0:HEAD,:]=q
    rhs[0:HEAD,0:W]=q
    hi,mid,lo=split3(-lse_ref[0])
    qd=qdoc_ref[...]
    qaug[HEAD:HEAD+16,:]=jnp.concatenate([jnp.concatenate([qd[0:3,:]]*TOP,1),hi,mid,lo,jnp.zeros((10,W),f32)],0).astype(bf16)
    qaug[HEAD+16:,:]=jnp.zeros((128-HEAD-16,W),bf16)
    r=[jnp.broadcast_to(routes_ref[k:k+1,:],(8,TB))[None] for k in range(TOP)]
    for k0 in range(0,TOP,4):
        sel=[jnp.zeros((HEAD//8,8,TB),f32) for _ in range(4)]
        for e in range(experts):
            v=dct_ref[e*HEAD:(e+1)*HEAD,:].astype(f32).reshape(HEAD//8,8,TB)
            sel=[jnp.where(r[k0+k]==e,v,sel[k]) for k in range(4)]
        for k in range(4):
            sl=slice((k0+k)*TB,(k0+k+1)*TB)
            dc=(sel[k].reshape(HEAD,TB)*gates_ref[k0+k:k0+k+1,:]).astype(bf16)
            daug[0:HEAD,sl]=dc
            rhs[HEAD:,W+(k0+k)*TB:W+(k0+k+1)*TB]=dc
            dq[0:1,sl]=jnp.sum(dc.astype(f32)*ctx_ref[0,:,sl].astype(f32),axis=0,keepdims=True)
    hi,mid,lo=split3(-dq[0:1,:])
    daug[HEAD:HEAD+16,:]=jnp.concatenate([hi,mid,lo,jnp.zeros((13,W),f32)],0).astype(bf16)
    daug[HEAD+16:,:]=jnp.zeros((128-HEAD-16,W),bf16)
    dq[...]=jnp.zeros_like(dq)
    q0=c*tok+i*TB
    nfull=q0//KB
    kd=pl.multiple_of(nfull*KB,KB)
    def block(k0,mask):
        p=jnp.exp2(jnp.dot(kaug_ref[pl.ds(k0,KB),:],qaug[...],preferred_element_type=f32))
        if mask is not None:
            p=jnp.concatenate([jnp.where(mask,p[:,k*TB:(k+1)*TB],0.0) for k in range(TOP)],1)
        dp=jnp.dot(vaug_ref[pl.ds(k0,KB),:],daug[...],preferred_element_type=f32)
        pds[:,W:]=p.astype(bf16)
        pds[:,:W]=(p*dp).astype(bf16)
        dq[...]+=jnp.dot(kt_ref[:,pl.ds(k0,KB)],pds[:,:W],preferred_element_type=f32)
        dkv_ref[pl.ds(k0,KB),:]+=lax.dot_general(pds[...],rhs[...],NT,preferred_element_type=f32)
    def body(b,_):
        block(pl.multiple_of(b*KB,KB),None)
        return 0
    lax.fori_loop(0,nfull,body,0)
    kp=lax.broadcasted_iota(jnp.int32,(KB,TB),0)+(kd-q0)
    tp=lax.broadcasted_iota(jnp.int32,(KB,TB),1)
    block(kd,kp<=tp)
    dq[...]*=0.125
    for h0 in range(0,HEAD,32):
        g=[dq[h0:h0+32,k*TB:(k+1)*TB].reshape(4,8,TB) for k in range(TOP)]
        for e in range(experts):
            o=jnp.zeros((4,8,TB),f32)
            for k in range(TOP):
                o=jnp.where(r[k]==e,g[k],o)
            dqd_ref[e*HEAD+h0:e*HEAD+h0+32,:]=o.reshape(32,TB).astype(bf16)
    @pl.when(i==pl.num_programs(0)-1)
    def _():
        lane=lax.broadcasted_iota(jnp.int32,(1,128),1)
        dkv_ref[...]*=jnp.where(lane<HEAD,LN2,1.0)

def attn_bwd(cidx, dct, q, ctx, lse, routesT, gatesT, qdoc, kaug, vaug, kt, KB=256):
    tok=routesT.shape[1]; experts=dct.shape[0]//HEAD; keys=kaug.shape[0]; n=tok//TB
    full=lambda a: pl.BlockSpec(a.shape,lambda i,*_:(0,)*a.ndim)
    blk=lambda rows: pl.BlockSpec((rows,TB),lambda i,*_:(0,i))
    return pl.pallas_call(
        functools.partial(attn_bwd_kernel,experts=experts,tok=tok,KB=KB),
        grid_spec=pltpu.PrefetchScalarGridSpec(num_scalar_prefetch=1,grid=(n,),
          in_specs=[blk(experts*HEAD),
            pl.BlockSpec((1,HEAD,W),lambda i,*_:(i,0,0)),
            pl.BlockSpec((1,HEAD,W),lambda i,*_:(i,0,0)),
            pl.BlockSpec((1,1,W),lambda i,*_:(i,0,0)),
            blk(TOP),blk(TOP),blk(8),full(kaug),full(vaug),full(kt)],
          out_specs=[blk(experts*HEAD),pl.BlockSpec((keys,128),lambda i,*_:(0,0))],
          scratch_shapes=[pltpu.VMEM((128,W),bf16),pltpu.VMEM((128,W),bf16),pltpu.VMEM((128,2*W),bf16),
            pltpu.VMEM((KB,2*W),bf16),pltpu.VMEM((HEAD,W),f32)]),
        out_shape=[jax.ShapeDtypeStruct((experts*HEAD,tok),bf16),
          jax.ShapeDtypeStruct((keys,128),f32)],
        compiler_params=pltpu.CompilerParams(vmem_limit_bytes=60*2**20),
        name="attn_bwd",
    )(cidx,dct,q,ctx,lse,routesT,gatesT,qdoc,kaug,vaug,kt)


def dot(a,b,dims=NN): return lax.dot_general(a,b,dims,preferred_element_type=f32)

def ffn_kernel(cd_ref, wo_ref, tok_ref, cot_ref, g2_ref, s2_ref, up_ref, upb_ref, down_ref, downb_ref,
               out_ref, dmid_ref, dct_ref, gwo_ref, gup_ref, gub_ref, gdown_ref, gsm_ref,
               mid, xhat, rstd, act, actT, dffn, acc, da2):
    j=pl.program_id(0); n=pl.num_programs(0)
    @pl.when(j==0)
    def _():
        m=tok_ref[...]+dot(cd_ref[...],wo_ref[...],TN)
        mid[...]=m
        cen=m-jnp.mean(m,axis=-1,keepdims=True)
        rs=lax.rsqrt(jnp.mean(cen*cen,axis=-1,keepdims=True)+1e-5)
        xh=cen*rs
        xhat[...]=xh; rstd[...]=jnp.broadcast_to(rs,rstd.shape)
        a=(xh*g2_ref[...]+s2_ref[...])
        act[...]=a.astype(bf16)
        actT[...]=jnp.transpose(a).astype(bf16)
        dffn[...]=cot_ref[...].astype(bf16)
        acc[...]=jnp.zeros_like(acc); da2[...]=jnp.zeros_like(da2)
    up=up_ref[...].astype(bf16); down=down_ref[...].astype(bf16)
    pre=dot(act[...],up)+upb_ref[...]
    x2=pre*pre
    th=jnp.tanh(pre*(C0+C0*C1*x2))
    h=0.5*(1.0+th)
    hid=(pre*h).astype(bf16)
    gp=h+(0.5*pre)*(1.0-th*th)*(C0+3.0*C0*C1*x2)
    acc[...]+=dot(hid,down)
    gdown_ref[...]=dot(hid,dffn[...],TN).astype(gdown_ref.dtype)
    dp=dot(dffn[...],down,NT)*gp
    dpb=dp.astype(bf16)
    gub_ref[...]=jnp.sum(dpb.astype(f32),axis=0,keepdims=True)
    gup_ref[...]=dot(actT[...],dpb).astype(gup_ref.dtype)
    da2[...]+=dot(dpb,up,NT)
    @pl.when(j==n-1)
    def _():
        out_ref[...]=mid[...]+acc[...]+downb_ref[...]
        d=da2[...]; xh=xhat[...]
        gx=d*g2_ref[...]
        dm=cot_ref[...]+rstd[:,0:1]*(gx-jnp.mean(gx,axis=-1,keepdims=True)-xh*jnp.mean(gx*xh,axis=-1,keepdims=True))
        dmid_ref[...]=dm
        dmb=dm.astype(bf16)
        dct_ref[...]=dot(wo_ref[...],dmb,NT).astype(bf16)
        gwo_ref[...]=dot(cd_ref[...],dmb).astype(gwo_ref.dtype)
        gsm_ref[...]=jnp.concatenate([jnp.sum(d*xh,axis=0,keepdims=True),jnp.sum(d,axis=0,keepdims=True),
            jnp.sum(dffn[...].astype(f32),axis=0,keepdims=True),jnp.zeros((5,D),f32)],0)

def ffn(cd, wo, tokens, cot, g2, s2, up, upb, down, downb, FB=256, gdt=bf16):
    tok=tokens.shape[0]; FF=up.shape[1]; n=FF//FB; EH=wo.shape[0]
    full=lambda a: pl.BlockSpec(a.shape,lambda i:(0,)*a.ndim,pipeline_mode=pl.Buffered(1))
    fo=lambda *s: pl.BlockSpec(s,lambda i:(0,)*len(s))
    sd=jax.ShapeDtypeStruct
    return pl.pallas_call(ffn_kernel,grid=(n,),
        in_specs=[full(cd),full(wo),full(tokens),full(cot),full(g2),full(s2),
          pl.BlockSpec((D,FB),lambda i:(0,i)),pl.BlockSpec((1,FB),lambda i:(0,i)),
          pl.BlockSpec((FB,D),lambda i:(i,0)),full(downb)],
        out_specs=[fo(tok,D),fo(tok,D),fo(EH,tok),fo(EH,D),
          pl.BlockSpec((D,FB),lambda i:(0,i)),pl.BlockSpec((1,FB),lambda i:(0,i)),
          pl.BlockSpec((FB,D),lambda i:(i,0)),fo(8,D)],
        out_shape=[sd((tok,D),f32),sd((tok,D),f32),sd((EH,tok),bf16),sd((EH,D),gdt),
          sd((D,FF),gdt),sd((1,FF),f32),sd((FF,D),gdt),sd((8,D),f32)],
        scratch_shapes=[pltpu.VMEM((tok,D),f32),pltpu.VMEM((tok,D),f32),pltpu.VMEM((tok,128),f32),
          pltpu.VMEM((tok,D),bf16),pltpu.VMEM((D,tok),bf16),pltpu.VMEM((tok,D),bf16),
          pltpu.VMEM((tok,D),f32),pltpu.VMEM((tok,D),f32)],
        compiler_params=pltpu.CompilerParams(vmem_limit_bytes=60*2**20),
        name="ffn",
    )(cd,wo,tokens,cot,g2,s2,up,upb,down,downb)


def local(sizes, tokens, lengths, routes, route_gates, cotangent, gain_one, shift_one, kv_weight,
          query_weight, out_weight, gain_two, shift_two, up_weight, up_bias, down_weight, down_bias):
    x = tokens[0]
    tok = x.shape[0]
    ncx = sizes["ctx"]
    group = tok * ncx
    nexp = query_weight.shape[0]
    experts = nexp * sizes["exp"]
    cidx = lax.axis_index("ctx")
    wq_own = jnp.swapaxes(query_weight, 1, 2).reshape(nexp * HEAD, D).astype(bf16)
    wo_own = out_weight.reshape(nexp * HEAD, D).astype(bf16)
    wq = lax.all_gather(wq_own, "exp", axis=0, tiled=True)
    wo = lax.all_gather(wo_own, "exp", axis=0, tiled=True)
    cen = x - jnp.mean(x, axis=-1, keepdims=True)
    rs1 = lax.rsqrt(jnp.mean(cen * cen, axis=-1, keepdims=True) + 1e-5)
    xh1 = cen * rs1
    act = (xh1 * gain_one + shift_one).astype(bf16)
    kvw = kv_weight.astype(bf16)
    kv_own = dot(act, kvw).astype(bf16)
    kv = lax.all_gather(kv_own, "ctx", axis=0, tiled=True)
    keys, vals = kv[:, :HEAD], kv[:, HEAD:]
    kn = jnp.max(jnp.sum(jnp.square(keys.astype(f32)), axis=1)).reshape(1)
    pos = jnp.arange(group, dtype=jnp.int32)
    docs, end = jnp.zeros_like(pos), 0
    for d in range(lengths.shape[1] - 1):
        end = end + lengths[0, d]
        docs = docs + (pos >= end).astype(jnp.int32)
    hot = (docs[:, None] == jnp.arange(3)[None, :]).astype(bf16)
    one3 = jnp.ones((group, 3), bf16)
    kaug = jnp.concatenate([keys, hot, one3, jnp.zeros((group, HEAD - 6), bf16)], axis=1)
    vaug = jnp.concatenate([vals, one3, jnp.zeros((group, HEAD - 3), bf16)], axis=1)
    kt = keys.T
    vt = jnp.concatenate([vals.T, jnp.ones((1, group), bf16), jnp.zeros((15, group), bf16)], axis=0)
    qdocs = lax.dynamic_slice_in_dim(docs, cidx * tok, tok)
    slot = jnp.arange(8, dtype=jnp.int32)[:, None]
    qdoc = jnp.where((qdocs[None, :] == slot) | (slot > 2), 0.0, NEG).astype(f32)
    routes_t = routes[0].T
    gates_t = route_gates[0].T
    cvec = cidx.reshape(1).astype(jnp.int32)

    cd, q, ctx, lse = attn_fwd(cvec, act, wq, routes_t, gates_t, qdoc, kaug, vt, kn, KB=384)
    row = lambda v: v.reshape(1, -1)
    out, dmid, dct, gwo, gup, gub, gdown, gsm = ffn(
        cd, wo, x, cotangent[0], row(gain_two), row(shift_two), up_weight, row(up_bias),
        down_weight, row(down_bias), FB=512)
    dqd, dkv_part = attn_bwd(cvec, dct, q, ctx, lse, routes_t, gates_t, qdoc, kaug, vaug, kt, KB=384)
    dkv = lax.psum_scatter(dkv_part, "ctx", scatter_dimension=0, tiled=True).astype(bf16)
    gkv = dot(act, dkv, TN)
    gwq = dot(dqd, act).astype(bf16)
    da1 = dot(dqd, wq, TN) + dot(dkv, kvw, NT)
    gg1 = jnp.sum(da1 * xh1, axis=0)
    gs1 = jnp.sum(da1, axis=0)
    gx = da1 * gain_one
    dx = dmid + rs1 * (gx - jnp.mean(gx, axis=-1, keepdims=True) - xh1 * jnp.mean(gx * xh1, axis=-1, keepdims=True))

    gw = lax.psum_scatter(jnp.concatenate([gwq, gwo], axis=1), "exp", scatter_dimension=0, tiled=True)
    gw = lax.psum(gw, ("dp", "ctx")).astype(f32)
    gq = jnp.swapaxes(gw[:, :D].reshape(nexp, HEAD, D), 1, 2)
    go = gw[:, D:].reshape(nexp, HEAD, D)
    gup, gdown = lax.psum((gup, gdown), ("dp", "ctx", "exp"))
    gg1, gs1, gkv, gub, gsm = lax.psum((gg1, gs1, gkv, gub, gsm), ("dp", "ctx", "exp"))
    return (out[None], dx[None], gg1, gs1, gkv, gq, go, gsm[0], gsm[1], gup.astype(f32), gub[0],
            gdown.astype(f32), gsm[2])


def solution(mesh):
    tok3 = P(("dp", "exp"), "ctx", None)
    ex = P("exp", None, None)
    r = P()
    in_specs = (tok3, P(("dp", "exp"), None), tok3, tok3, tok3, r, r, r, ex, ex, r, r, r, r, r, r)
    out_specs = (tok3, tok3, r, r, r, ex, ex, r, r, r, r, r, r)
    fn = functools.partial(local, dict(mesh.shape))
    return jax.shard_map(fn, mesh=mesh, in_specs=in_specs, out_specs=out_specs, check_vma=False)
```

time: 908 us -> 518 us (0.57); the launches traced: 897 us -> 517 us
  local copies, waits for them, and re-layouts: 313 us -> 7.88 us
  matrix products: 274 us -> 12.9 us
  waiting for transfers between devices: 200 us -> 350 us
  Pallas kernels: 0 us -> 60.2 us
  other arithmetic: 41.2 us -> 19.8 us
    gather x10 -> x0, local copies, waits for them, and re-layouts: 191 us -> none  [the longest x4 107 us: from_slots(): slot_data.reshape(-1, row_width)[slot_index]]
    dot_general x76 -> x5, matrix products: 184 us -> 12.9 us  [dot(): return lax.dot_general(a, b, dims, preferred_element_type=f32)]
    psum x2 -> x3, waiting for transfers between devices: 200 us -> 309 us  [the longest x1 141 us: local(): gup, gdown = lax.psum((gup, gdown), ('dp', 'ctx', 'exp'))]
    sub x24 -> x0, matrix products: 90.9 us -> none  [block_probs(): return jax.nn.softmax(scores, axis=-1)]
    scatter x3 -> x0, local copies, waits for them, and re-layouts: 72.3 us -> none  [the longest x1 26.1 us: local(): jnp.zeros((experts_all * capacity,), jnp.bool_).at[slot_index].set(True)]
    pallas_call x0 -> x3, Pallas kernels: none -> 60.2 us  [the longest x1 25.6 us: ffn(): pl.pallas_call(ffn_kernel, grid=(n,), in_specs=[full(cd), full(wo), full(...]
    unnamed x129 -> x27, local copies, waits for them, and re-layouts: 23 us -> 1.73 us
    all_gather x2, waiting for transfers between devices: 0.02 us -> 20.4 us  [the longest x1 11.1 us: local(): wo = lax.all_gather(wo_own, 'exp', axis=0, tiled=True)]
  transfers between devices with their start and end apart: 7 -> 7, of which waited for: 2 -> 6; matrix products, arithmetic and copies ran while one was open for 39% -> 7% of each run, Pallas kernels for 0% -> 3%
where the time goes in v1:
time: 518 us; the launch traced here: 517 us
  waiting for transfers between devices  350 us (68%)
  Pallas kernels  60.2 us (12%)
  blocking collectives  50.5 us (10%)
  other arithmetic  19.8 us (4%)
  between operations  15.7 us (3%)
  matrix products  12.9 us (2%)
  local copies, waits for them, and re-layouts  7.88 us (2%)
    psum x1, waiting for transfers between devices, local(): gup, gdown = lax.psum((gup, gdown), ('dp', 'ctx', 'exp'))  141 us
    psum x1, waiting for transfers between devices, local(): lax.psum((gg1, gs1, gkv, gub, gsm), ('dp', 'ctx', 'exp'))  129 us
    psum x1, blocking collectives, local(): lax.psum((gg1, gs1, gkv, gub, gsm), ('dp', 'ctx', 'exp'))  42 us
    psum x1, waiting for transfers between devices, local(): gw = lax.psum(gw, ('dp', 'ctx')).astype(f32)  39.2 us
    pallas_call x1, Pallas kernels, ffn(): pl.pallas_call(ffn_kernel, grid=(n,), in_specs=[full(cd), full(wo), full(...  25.6 us
    reduce_scatter x1, waiting for transfers between devices, local(): lax.psum_scatter(dkv_part, 'ctx', scatter_dimension=0, tiled=True)  19.9 us
    pallas_call x1, Pallas kernels, attn_bwd(): pl.pallas_call(functools.partial(attn_bwd_kernel, experts=experts, tok=to...  19.1 us
    pallas_call x1, Pallas kernels, attn_fwd(): pl.pallas_call(functools.partial(attn_fwd_kernel, experts=experts, tok=to...  15.5 us
  transfers between devices with their start and end apart: 7, of which 6 were waited for; matrix products, arithmetic and copies ran while one was open for 7% of the time, Pallas kernels for 3%

profile of v1, /device:TPU:0, one launch (start us, length us, event | category | flops | bytes accessed | tf_op | source)
XLA Modules:
  0.0 517.3 jit_solution(2141767825188877208)
XLA Ops:
  7.2 1.8 convert_element_type.60
  9.1 0.0 all-gather.5.cloned.1.call-start
  9.1 1.7 convert_element_type.69
  10.8 0.0 reduce-scatter.3.cloned.1.call-start
  10.9 0.1 pad.6.clone
  11.0 0.1 pad.4.clone
  11.1 0.1 pad.7.clone
  11.1 0.1 pad.11.clone
  11.2 0.6 fusion.10
  11.8 0.2 reduce_sum.63
  12.0 0.3 multiply_reduce_fusion.2
  13.7 0.3 add_convert_fusion.act_ref
  14.1 0.7 convert_add_fusion
  14.7 0.1 dynamic_slice.3
  14.8 0.4 convolution_convert_fusion.1
  15.2 8.5 %all_gather.10 = bf16[1536,128]{0,1:T(8,128)(2,1)S(1)} all-gather(bf16[768,128]{0,1:T(8,128)(2,1)S(1)} %convolution_convert_fusion.1), channel_id=1, replica_groups=mesh['dp'=2,'ctx'=2,'exp'=8] {'ctx'}, dimensions={0}, use_global_device_ids=true | all-gather | bytes 589824 | tf_op jit(solution)/shard_map/all_gather | solution.py:310
  23.8 0.7 slice_bitcast_fusion.1
  24.5 0.2 maximum_maximum_fusion.1
  24.7 0.9 copy.32.vaug_ref
  25.6 0.9 copy.30.kaug_ref
  26.6 0.1 multiply_reduce_fusion.4
  26.6 0.6 reduce_max.9
  27.2 0.7 fusion.6.qdoc_ref
  27.9 0.8 maximum_maximum_fusion.2.vt_ref
  28.7 9.3 %all-gather.3.cloned.1.call-done.wq_ref = bf16[1536,512]{1,0:T(8,128)(2,1)} async-done(((bf16[192,512]{1,0:T(8,128)(2,1)}), bf16[1536,512]{1,0:T(8,128)(2,1)}) %all-gather.3.cloned.1.call-update) | async-done | bytes 1572880 | tf_op jit(solution)/shard_map/all_gather | solution.py:302
  38.0 15.5 %attn_fwd.1 = (bf16[1536,768]{1,0:T(8,128)(2,1)}, bf16[6,64,1024]{2,1,0:T(8,128)(2,1)}, f32[6,64,1024]{2,1,0:T(8,128)}, f32[6,1,1024]{2,1,0:T(1,128)}) custom-call(s32[1]{0:T(128)} %bitcast.cidx_ref, bf16[768,512]{1,0:T(8,128)(2,1)} %copy-done.2, bf16[1536,512]{1,0:T(8,128)(2,1)} %all-gather.3.cloned.1.call-done.wq_ref, s32[8,768]{1,0:T(8,128)} %bitcast.53, ...), custom_call_target="tpu_custom_call" | custom-call | tf_op jit(solution)/shard_map/attn_fwd/pallas_call | solution.py:111
  53.6 11.1 %all-gather.5.cloned.1.call-done.wo_ref = bf16[1536,512]{1,0:T(8,128)(2,1)} async-done(((bf16[192,512]{1,0:T(8,128)(2,1)}), bf16[1536,512]{1,0:T(8,128)(2,1)}) %all-gather.5.cloned.1.call-update) | async-done | bytes 1572880 | tf_op jit(solution)/shard_map/all_gather | solution.py:303
  64.7 25.6 %ffn.1 = (f32[768,512]{1,0:T(8,128)}, f32[768,512]{1,0:T(8,128)}, bf16[1536,768]{1,0:T(8,128)(2,1)}, bf16[1536,512]{1,0:T(8,128)(2,1)}, bf16[512,2048]{1,0:T(8,1...) custom-call(bf16[1536,768]{1,0:T(8,128)(2,1)} %get-tuple-element.27.cd_ref, ...), custom_call_target="tpu_custom_call" | custom-call | tf_op jit(solution)/shard_map/ffn/pallas_call | solution.py:274
  90.3 19.1 %attn_bwd.1 = (bf16[1536,768]{1,0:T(8,128)(2,1)}, f32[1536,128]{1,0:T(8,128)}) custom-call(s32[1]{0:T(128)} %bitcast.cidx_ref, bf16[1536,768]{1,0:T(8,128)(2,1)} %get-tuple-element.30.dct_ref, bf16[6,64,1024]{2,1,0:T(8,128)(2,1)} %get-tuple-element.31.q_ref, f32[6,64,1024]{2,1,0:T(8,128)} %get-tuple-element.32.ctx_ref, ...), custom_call_target="tpu_custom_call" | custom-call | tf_op jit(solution)/shard_map/attn_bwd/pallas_call | solution.py:205
  109.4 0.0 reduce-scatter.5.cloned.1.call-start
  109.4 3.2 convolution_convert_fusion
  112.6 2.1 pad_maximum_fusion
  114.7 0.0 all-reduce.10.cloned.1.call-start
  114.8 0.5 all-reduce.10.cloned.1.call-update
  115.4 4.8 fusion.11
  120.1 19.9 %reduce-scatter.3.cloned.1.call-done = f32[768,128]{1,0:T(8,128)} async-done(((f32[1536,128]{1,0:T(8,128)}), f32[768,128]{1,0:T(8,128)}) %reduce-scatter.3.cloned.1.call-update) | async-done | bytes 393232 | tf_op jit(solution)/shard_map/reduce_scatter | solution.py:337
  140.1 3.5 multiply_reduce_fusion
  143.6 42.0 %all-reduce = (f32[512]{0:T(512)}, f32[512]{0:T(512)}, f32[8,512]{1,0:T(8,128)S(1)}, f32[2048]{0:T(1024)}) all-reduce(f32[512]{0:T(512)S(1)} %get-tuple-element.41, f32[512]{0:T(512)S(1)} %get-tuple-element.44, f32[8,512]{1,0:T(8,128)S(1)} %copy-done.9, f32[2048]{0:T(1024)S(1)} %bitcast.58), channel_id=1, replica_groups=mesh['dp'=2,'ctx'=2,'exp'=8] {'dp','ctx','exp'}, use_global_device_ids=true, to_apply=%region_8.9 | all-reduce | flops 7168 | bytes 57344 | tf_op jit(solution)/shard_map/psum | solution.py:351
  185.6 0.6 fusion.9
  186.2 1.1 fusion
  187.4 3.5 add_bitcast_fusion
  190.9 140.8 %all-reduce.10.cloned.1.call-done = (bf16[512,2048]{1,0:T(8,128)(2,1)}, bf16[2048,512]{1,0:T(8,128)(2,1)}) async-done(((bf16[512,2048]{1,0:T(8,128)(2,1)}, bf16[2048,512]{1,0:T(8,128)(2,1)}), (bf16[512,2048]{1,0:T(8,128)(2,1)}, bf16[2048,512]{1,0:T(8,128)(2,1)})) %all-reduce.10.cloned.1.call-update) | async-done | bytes 4194320 | tf_op jit(solution)/shard_map/psum | solution.py:350
  331.7 4.3 convert_element_type.74
  335.9 2.6 convert_element_type.75
  338.6 39.2 %all-reduce.8.cloned.1.call-done = bf16[192,1024]{1,0:T(8,128)(2,1)} async-done(((bf16[192,1024]{1,0:T(8,128)(2,1)}), bf16[192,1024]{1,0:T(8,128)(2,1)}) %all-reduce.8.cloned.1.call-update) | async-done | bytes 393232 | tf_op jit(solution)/shard_map/psum | solution.py:347
  377.8 2.0 fusion.8
  379.8 129.1 %all-reduce.6.cloned.1.call-done = f32[512,128]{1,0:T(8,128)} async-done(((f32[512,128]{1,0:T(8,128)}), f32[512,128]{1,0:T(8,128)}) %all-reduce.6.cloned.1.call-update) | async-done | bytes 262160 | tf_op jit(solution)/shard_map/psum | solution.py:351
  508.8 1.7 copy.40
  (45 shorter events, 0.3 us)
Async XLA Ops:
  7.2 4.1 copy-start.12
  7.2 4.6 copy-start
  7.2 30.8 %all-gather.3.cloned.1.call-start = ((), (), s32[]{:S(2)}) async-start(), calls=%async_computation.2 | async-start | bytes 1769472 | tf_op jit(solution)/shard_map/all_gather | solution.py:302
  9.1 55.6 %all-gather.5.cloned.1.call-start = ((), (), s32[]{:S(2)}) async-start(), calls=%async_computation.3 | async-start | bytes 1769472 | tf_op jit(solution)/shard_map/all_gather | solution.py:303
  10.8 129.2 %reduce-scatter.3.cloned.1.call-start = ((), (), s32[]{:S(2)}) async-start(), calls=%async_computation.4 | async-start | bytes 1179648 | tf_op jit(solution)/shard_map/reduce_scatter | solution.py:337
  11.8 1.9 copy-start.8
  11.8 1.9 copy-start.11
  12.4 2.5 copy-start.7
  14.1 10.7 %copy-start.2 = (bf16[768,512]{1,0:T(8,128)(2,1)}, bf16[768,512]{1,0:T(8,128)(2,1)S(1)}, u32[]{:S(2)}) copy-start(bf16[768,512]{1,0:T(8,128)(2,1)S(1)} %add_convert_fusion.act_ref) | copy-start | bytes 2359300
  90.3 19.2 %copy-start.3 = (bf16[768,512]{1,0:T(8,128)(2,1)S(1)}, bf16[768,512]{1,0:T(8,128)(2,1)}, u32[]{:S(2)}) copy-start(bf16[768,512]{1,0:T(8,128)(2,1)} %copy-done.2) | copy-start | bytes 2359300
  109.4 76.2 %reduce-scatter.5.cloned.1.call-start = ((), (), s32[]{:S(2)}) async-start(), calls=%async_computation.6 | async-start | bytes 3538944 | tf_op jit(solution)/shard_map/reduce_scatter | solution.py:346
  109.4 3.2 copy-start.6
  114.7 216.9 %all-reduce.10.cloned.1.call-start = ((), (), s32[]{:S(2)}) async-start(), calls=%async_computation.8 | async-start | bytes 8388608 | tf_op jit(solution)/shard_map/psum | solution.py:350
  115.3 24.8 %copy-start.1 = (f32[1,768,512]{2,1,0:T(8,128)S(1)}, f32[1,768,512]{2,1,0:T(8,128)}, u32[]{:S(2)}) copy-start(f32[1,768,512]{2,1,0:T(8,128)} %param.16) | copy-start | bytes 4718596
  115.3 262.5 %all-reduce.8.cloned.1.call-start = ((), (), s32[]{:S(2)}) async-start(), calls=%async_computation.7 | async-start | bytes 786432 | tf_op jit(solution)/shard_map/psum | solution.py:347
  120.1 23.4 %copy-start.9 = (f32[8,512]{1,0:T(8,128)S(1)}, f32[8,512]{1,0:T(8,128)}, u32[]{:S(2)}) copy-start(f32[8,512]{1,0:T(8,128)} %get-tuple-element.37) | copy-start | bytes 49156
  120.1 23.4 %copy-start.10 = (f32[1,2048]{1,0:T(1,128)S(1)}, f32[1,2048]{1,0:T(1,128)}, u32[]{:S(2)}) copy-start(f32[1,2048]{1,0:T(1,128)} %get-tuple-element.39) | copy-start | bytes 24580
  140.1 46.1 %copy-start.5 = (f32[768,128]{1,0:T(8,128)S(1)}, f32[768,128]{1,0:T(8,128)}, u32[]{:S(2)}) copy-start(f32[768,128]{1,0:T(8,128)} %reduce-scatter.3.cloned.1.call-done) | copy-start | bytes 1179652
  185.6 323.2 %all-reduce.6.cloned.1.call-start = ((), (), s32[]{:S(2)}) async-start(), calls=%async_computation.5 | async-start | bytes 524288 | tf_op jit(solution)/shard_map/psum | solution.py:351
  331.7 4.3 copy-start.4
Sparse Core Ops, SparseCore 0:
  10.2 27.7 all-gather.2
  40.3 24.3 all-gather.4
  109.5 30.5 reduce-scatter.2
  142.9 41.3 reduce-scatter.4
  190.9 140.7 all-reduce.9
  334.8 42.9 all-reduce.7
  383.8 124.9 all-reduce.5

commit v2 on v1

--- a/solution.py
+++ b/solution.py
@@ -24,6 +24,8 @@
 TN = (((0,), (0,)), ((), ()))
 C0 = math.sqrt(2 / math.pi)
 C1 = 0.044715
+MESH = pl.DeviceIdType.MESH
+AXES = ("dp", "ctx", "exp")
 
 
 def attn_fwd_kernel(cidx_ref, act_ref, wq_ref, routes_ref, gates_ref, qdoc_ref, kaug_ref, vt_ref, kn_ref,
@@ -276,16 +278,205 @@
           pl.BlockSpec((D,FB),lambda i:(0,i)),pl.BlockSpec((1,FB),lambda i:(0,i)),
           pl.BlockSpec((FB,D),lambda i:(i,0)),full(downb)],
         out_specs=[fo(tok,D),fo(tok,D),fo(EH,tok),fo(EH,D),
-          pl.BlockSpec((D,FB),lambda i:(0,i)),pl.BlockSpec((1,FB),lambda i:(0,i)),
+          pl.BlockSpec((D,FB),lambda i:(i,0)),pl.BlockSpec((1,FB),lambda i:(0,i)),
           pl.BlockSpec((FB,D),lambda i:(i,0)),fo(8,D)],
         out_shape=[sd((tok,D),f32),sd((tok,D),f32),sd((EH,tok),bf16),sd((EH,D),gdt),
-          sd((D,FF),gdt),sd((1,FF),f32),sd((FF,D),gdt),sd((8,D),f32)],
+          sd((n*D,FB),gdt),sd((1,FF),f32),sd((FF,D),gdt),sd((8,D),f32)],
         scratch_shapes=[pltpu.VMEM((tok,D),f32),pltpu.VMEM((tok,D),f32),pltpu.VMEM((tok,128),f32),
           pltpu.VMEM((tok,D),bf16),pltpu.VMEM((D,tok),bf16),pltpu.VMEM((tok,D),bf16),
           pltpu.VMEM((tok,D),f32),pltpu.VMEM((tok,D),f32)],
         compiler_params=pltpu.CompilerParams(vmem_limit_bytes=60*2**20),
         name="ffn",
     )(cd,wo,tokens,cot,g2,s2,up,upb,down,downb)
+
+
+def partner(bit):
+    ax, m = bit
+    i = lax.axis_index(ax)
+    b = lax.rem(i // m, 2)
+    return {a: (i + m - 2 * m * b if a == ax else lax.axis_index(a)) for a in AXES}, b
+
+
+def mesh_bits(sizes):
+    return {a: [(a, 1 << i) for i in range(sizes[a].bit_length() - 1)] for a in AXES}
+
+
+def chain_orders(sizes):
+    b = mesh_bits(sizes)
+    e, d, c = b["exp"], b["dp"], b["ctx"]
+    late = e + d + c
+    if len(d) + len(c) > 2:
+        return [late, late, late]
+    return [e[:1] + d + c + e[1:], e[:1] + c + d + e[1:], late]
+
+
+def greet(bits):
+    bar = pltpu.get_barrier_semaphore()
+    for bit in bits:
+        pl.semaphore_signal(bar, inc=1, device_id=partner(bit)[0], device_id_type=MESH)
+    pl.semaphore_wait(bar, len(bits))
+
+
+def rows(ref, start, n):
+    return ref.at[pl.ds(pl.multiple_of(start, 16), n), :]
+
+
+def add_rows(dst, d0, a, a0, b, b0, n):
+    ch = math.gcd(n, 64)
+
+    @pl.loop(0, n // ch)
+    def _(t):
+        o = pl.multiple_of(t * ch, ch)
+        g = lambda r, s: r[pl.ds(pl.multiple_of(s + o, 16), ch), :].astype(f32)
+        dst[pl.ds(pl.multiple_of(d0 + o, 16), ch), :] = (g(a, a0) + g(b, b0)).astype(bf16)
+
+
+def chain_plan(n, order):
+    plan = []
+    for bit in order:
+        halve = n % 32 == 0
+        n = n // 2 if halve else n
+        plan.append((halve, bit, n))
+    return plan
+
+
+class Chain:
+    def __init__(self, src, work, final, base, n, order, fbase=None):
+        self.src, self.out, self.base, self.n, self.order = src, work, base, n, order
+        self.final, self.fbase = final, fbase
+        self.plan = chain_plan(n, order)
+        self.landed = sum(m for _, _, m in self.plan)
+        self.back = [i for i in reversed(range(len(order))) if self.plan[i][0] and (fbase is None or order[i][0] != "exp")]
+        if fbase is not None:
+            self.back.sort(key=lambda i: (order[i][0], order[i][1]), reverse=True)
+        self.nsem = len(self.plan) + len(self.back)
+        self.nsteps = self.nsem + 1
+        self.copies = {}
+
+    def place(self, land, lbase, ss, rs, sem):
+        self.land, self.ss, self.rs, self.sem = land, ss, rs, sem
+        self.lb, self.offs, off = [], [], self.base
+        for halve, bit, m in self.plan:
+            self.lb.append(lbase)
+            lbase += m
+            b = partner(bit)[1]
+            self.offs.append((off + b * m, off + (1 - b) * m) if halve else (off, off))
+            off = self.offs[-1][0]
+        self.last = off
+
+    def copy(self, i, src, dst, bit):
+        c = pltpu.make_async_remote_copy(
+            src_ref=src, dst_ref=dst, send_sem=self.ss.at[self.sem + i], recv_sem=self.rs.at[self.sem + i],
+            device_id=partner(bit)[0], device_id_type=MESH)
+        c.start()
+        self.copies[i] = c
+
+    def fold(self, i):
+        self.copies[i].wait()
+        d = self.offs[i][0]
+        last = i == len(self.plan) - 1
+        add_rows(self.final if last else self.out, self.final_range(0)[0] if last else d,
+                 self.src if i == 0 else self.out, d, self.land, self.lb[i], self.plan[i][2])
+
+    def final_range(self, j):
+        if self.fbase is None:
+            i = self.back[j] if j < len(self.back) else 0
+            return (self.offs[i][0], self.plan[i][2]) if j or self.plan[-1][0] else (self.last, self.plan[-1][2])
+        m = self.plan[-1][2]
+        off, size = self.fbase, m
+        for k, i in enumerate(self.back):
+            if k < j:
+                size *= 2
+        w = m
+        for k, i in enumerate(self.back):
+            if k >= j:
+                off = off + partner(self.order[i])[1] * w
+            w *= 2
+        return off, size
+
+    def step(self, k):
+        m = len(self.plan)
+        if k < m:
+            if k:
+                self.fold(k - 1)
+            _, bit, n = self.plan[k]
+            self.copy(k, rows(self.src if k == 0 else self.out, self.offs[k][1], n), rows(self.land, self.lb[k], n), bit)
+            return
+        j = k - m
+        if j == 0:
+            self.fold(m - 1)
+        else:
+            self.copies[k - 1].wait()
+        if j < len(self.back):
+            i = self.back[j]
+            r = rows(self.final, *self.final_range(j))
+            self.copy(k, r, r, self.order[i])
+
+
+def place_all(chains, land, ss, rs):
+    lb = sem = 0
+    for c in chains:
+        c.place(land, lb, ss, rs, sem)
+        lb += c.landed
+        sem += c.nsem
+
+
+def owner_rows(g, sizes, order):
+    n, width = g.shape
+    bits = [bit for halve, bit, _ in chain_plan(n, order) if halve]
+    own = [b for b in bits if b[0] == "exp"]
+    rest = sorted([b for b in bits if b[0] != "exp"])
+    nat = sorted(own, reverse=True) + rest
+    block = n >> len(nat)
+    y = g.reshape((2,) * len(nat) + (block, width))
+    y = y.transpose([nat.index(b) for b in bits] + [len(nat), len(nat) + 1])
+    return y.reshape(n, width)
+
+
+def dense_parts(n, orders):
+    a = n * 3 // 8 // 32 * 32
+    return [(0, a, orders[0]), (a, a, orders[1]), (2 * a, n - 2 * a, orders[2])]
+
+
+def make_chains(orders, gd, gu, go, gq, sm, gd_o, gu_o, sm_o, go_f, gq_f, gd_w, gu_w, sm_w, go_w, gq_w):
+    chains = []
+    for src, work, out in ((gd, gd_w, gd_o), (gu, gu_w, gu_o)):
+        chains += [Chain(src, work, out, b, n, o) for b, n, o in dense_parts(src.shape[0], orders)]
+    for src, work, fin in ((go, go_w, go_f), (gq, gq_w, gq_f)):
+        n = src.shape[0] // 3
+        chains += [Chain(src, work, fin, j * n, n, orders[j], j * HEAD) for j in range(3)]
+    chains.append(Chain(sm, sm_w, sm_o, 0, sm.shape[0], orders[0]))
+    return chains
+
+
+def reduce_kernel(sizes, *refs):
+    land, ss, rs = refs[-3:]
+    greet([b for a in AXES for b in mesh_bits(sizes)[a]])
+    chains = make_chains(chain_orders(sizes), *refs[:-3])
+    place_all(chains, land, ss, rs)
+    for t in range(max(c.nsteps for c in chains)):
+        for c in chains:
+            if t < c.nsteps:
+                c.step(t)
+
+
+def reduce_all(sizes, gd, gu, go, gq, sm):
+    shapes = [jax.ShapeDtypeStruct(v.shape, bf16) for v in (gd, gu, go, gq, sm)]
+    chains = make_chains(chain_orders(sizes), *shapes, *[None] * 10)
+    nsem = sum(c.nsem for c in chains)
+    land = sum(c.landed for c in chains)
+    v = pl.BlockSpec(memory_space=pltpu.VMEM)
+    fin = jax.ShapeDtypeStruct((go.shape[0] // sizes["exp"], go.shape[1]), bf16)
+    return pl.pallas_call(
+        functools.partial(reduce_kernel, sizes),
+        out_shape=[shapes[0], shapes[1], shapes[4], fin, fin],
+        in_specs=[v] * 5,
+        out_specs=[v] * 5,
+        scratch_shapes=[pltpu.VMEM(t.shape, bf16) for t in (gd, gu, sm, go, gq)]
+        + [pltpu.VMEM((land, D), bf16), pltpu.SemaphoreType.DMA((nsem,)), pltpu.SemaphoreType.DMA((nsem,))],
+        compiler_params=pltpu.CompilerParams(collective_id=0, has_side_effects=True, vmem_limit_bytes=60 * 2**20),
+        name="reduce_all",
+    )(gd, gu, go, gq, sm)
 
 
 def local(sizes, tokens, lengths, routes, route_gates, cotangent, gain_one, shift_one, kv_weight,
@@ -343,14 +534,26 @@
     gx = da1 * gain_one
     dx = dmid + rs1 * (gx - jnp.mean(gx, axis=-1, keepdims=True) - xh1 * jnp.mean(gx * xh1, axis=-1, keepdims=True))
 
-    gw = lax.psum_scatter(jnp.concatenate([gwq, gwo], axis=1), "exp", scatter_dimension=0, tiled=True)
-    gw = lax.psum(gw, ("dp", "ctx")).astype(f32)
-    gq = jnp.swapaxes(gw[:, :D].reshape(nexp, HEAD, D), 1, 2)
-    go = gw[:, D:].reshape(nexp, HEAD, D)
-    gup, gdown = lax.psum((gup, gdown), ("dp", "ctx", "exp"))
-    gg1, gs1, gkv, gub, gsm = lax.psum((gg1, gs1, gkv, gub, gsm), ("dp", "ctx", "exp"))
-    return (out[None], dx[None], gg1, gs1, gkv, gq, go, gsm[0], gsm[1], gup.astype(f32), gub[0],
-            gdown.astype(f32), gsm[2])
+    orders = chain_orders(sizes)
+
+    def parts(g):
+        g = g.reshape(sizes["exp"], nexp, HEAD, D)
+        return jnp.concatenate([owner_rows(g[:, j].reshape(-1, D), sizes, orders[j]) for j in range(nexp)], axis=0)
+
+    small = jnp.concatenate([gkv.reshape(-1, D), gub.reshape(-1, D), gsm[:3], row(gg1), row(gs1)], axis=0)
+    used = small.shape[0]
+    small = jnp.pad(small.astype(bf16), ((0, 256 - used), (0, 0)))
+    gdown, gup, small, go, gq = reduce_all(sizes, gdown, gup, parts(gwo), parts(gwq), small)
+    go = go.astype(f32).reshape(nexp, HEAD, D)
+    gq = jnp.swapaxes(gq.astype(f32).reshape(nexp, HEAD, D), 1, 2)
+    small = small[:used].astype(f32)
+    nkv, nub = gkv.size // D, gub.size // D
+    gkv = small[:nkv].reshape(gkv.shape)
+    gub = small[nkv:nkv + nub].reshape(-1)
+    tail = small[nkv + nub:]
+    gup = gup.astype(f32).reshape(-1, D, gup.shape[1]).transpose(1, 0, 2).reshape(D, -1)
+    return (out[None], dx[None], tail[3], tail[4], gkv, gq, go, tail[0], tail[1], gup, gub,
+            gdown.astype(f32), tail[2])
 
 
 def solution(mesh):

time: 518 us -> 243 us (0.47)
  waiting for transfers between devices: 350 us -> 38.4 us
  Pallas kernels: 60.2 us -> 133 us
  blocking collectives: 50.5 us -> 8.53 us
  local copies, waits for them, and re-layouts: 7.88 us -> 16.5 us
    psum x3 -> x0, waiting for transfers between devices: 309 us -> none  [the longest x1 141 us: local(): gup, gdown = lax.psum((gup, gdown), ('dp', 'ctx', 'exp'))]
    pallas_call x0 -> x1, Pallas kernels: none -> 72.5 us  [reduce_all(): pl.pallas_call(functools.partial(reduce_kernel, sizes), out_shape=[shapes...]
    psum x1 -> x0, blocking collectives: 42 us -> none  [local(): lax.psum((gg1, gs1, gkv, gub, gsm), ('dp', 'ctx', 'exp'))]
  transfers between devices with their start and end apart: 7 -> 3, of which waited for: 6 -> 3; matrix products, arithmetic and copies ran while one was open for 7% -> 8% of each run, Pallas kernels for 3% -> 6%
where the time goes in v2:
time: 243 us; the launch traced here: 242 us
  Pallas kernels  133 us (55%)
  waiting for transfers between devices  38.4 us (16%)
  other arithmetic  20 us (8%)
  local copies, waits for them, and re-layouts  16.5 us (7%)
  between operations  15.4 us (6%)
  matrix products  10.5 us (4%)
  blocking collectives  8.53 us (4%)
    pallas_call x1, Pallas kernels, reduce_all(): pl.pallas_call(functools.partial(reduce_kernel, sizes), out_shape=[shapes...  72.5 us
    pallas_call x1, Pallas kernels, ffn(): pl.pallas_call(ffn_kernel, grid=(n,), in_specs=[full(cd), full(wo), full(...  25.6 us
    pallas_call x1, Pallas kernels, attn_bwd(): pl.pallas_call(functools.partial(attn_bwd_kernel, experts=experts, tok=to...  19 us
    reduce_scatter x1, waiting for transfers between devices, local(): lax.psum_scatter(dkv_part, 'ctx', scatter_dimension=0, tiled=True)  18 us
    pallas_call x1, Pallas kernels, attn_fwd(): pl.pallas_call(functools.partial(attn_fwd_kernel, experts=experts, tok=to...  15.5 us
    all_gather x1, waiting for transfers between devices, local(): wo = lax.all_gather(wo_own, 'exp', axis=0, tiled=True)  11.1 us
    dot_general x5, matrix products, dot(): return lax.dot_general(a, b, dims, preferred_element_type=f32)  10.5 us
    all_gather x1, waiting for transfers between devices, local(): wq = lax.all_gather(wq_own, 'exp', axis=0, tiled=True)  9.32 us
  transfers between devices with their start and end apart: 3, of which 3 were waited for; matrix products, arithmetic and copies ran while one was open for 8% of the time, Pallas kernels for 6%

profile of v2, /device:TPU:0, one launch (start us, length us, event | category | flops | bytes accessed | tf_op | source)
XLA Modules:
  0.0 242.2 jit_solution(12175472029420797548)
XLA Ops:
  7.2 1.8 convert_element_type.63
  9.1 1.7 convert_element_type.72
  11.2 0.6 fusion.10
  11.8 0.2 reduce_sum.63
  12.0 0.3 multiply_reduce_fusion.2
  13.7 0.3 add_convert_fusion.act_ref
  14.1 0.7 convert_add_fusion
  14.7 0.1 dynamic_slice.3
  14.8 0.4 convolution_convert_fusion.1
  15.2 8.5 %all_gather.10 = bf16[1536,128]{0,1:T(8,128)(2,1)S(1)} all-gather(bf16[768,128]{0,1:T(8,128)(2,1)S(1)} %convolution_convert_fusion.1), channel_id=1, replica_groups=mesh['dp'=2,'ctx'=2,'exp'=8] {'ctx'}, dimensions={0}, use_global_device_ids=true | all-gather | bytes 589824 | tf_op jit(solution)/shard_map/all_gather | solution.py:501
  23.8 0.8 slice_bitcast_fusion.2
  24.6 0.2 maximum_maximum_fusion.1
  24.7 0.9 copy.37.vaug_ref
  25.7 0.9 copy.35.kaug_ref
  26.6 0.6 reduce_max.9
  27.2 0.7 fusion.5.qdoc_ref
  27.9 0.8 maximum_maximum_fusion.2.vt_ref
  28.7 9.3 %all-gather.3.cloned.1.call-done.wq_ref = bf16[1536,512]{1,0:T(8,128)(2,1)} async-done(((bf16[192,512]{1,0:T(8,128)(2,1)}), bf16[1536,512]{1,0:T(8,128)(2,1)}) %all-gather.3.cloned.1.call-update) | async-done | bytes 1572880 | tf_op jit(solution)/shard_map/all_gather | solution.py:493
  38.1 15.5 %attn_fwd.1 = (bf16[1536,768]{1,0:T(8,128)(2,1)}, bf16[6,64,1024]{2,1,0:T(8,128)(2,1)}, f32[6,64,1024]{2,1,0:T(8,128)}, f32[6,1,1024]{2,1,0:T(1,128)}) custom-call(s32[1]{0:T(128)} %bitcast.cidx_ref, bf16[768,512]{1,0:T(8,128)(2,1)} %copy-done.2, bf16[1536,512]{1,0:T(8,128)(2,1)} %all-gather.3.cloned.1.call-done.wq_ref, s32[8,768]{1,0:T(8,128)} %bitcast.119, ...), custom_call_target="tpu_custom_call" | custom-call | tf_op jit(solution)/shard_map/attn_fwd/pallas_call | solution.py:113
  53.6 11.1 %all-gather.5.cloned.1.call-done.wo_ref = bf16[1536,512]{1,0:T(8,128)(2,1)} async-done(((bf16[192,512]{1,0:T(8,128)(2,1)}), bf16[1536,512]{1,0:T(8,128)(2,1)}) %all-gather.5.cloned.1.call-update) | async-done | bytes 1572880 | tf_op jit(solution)/shard_map/all_gather | solution.py:494
  64.7 25.6 %ffn.1 = (f32[768,512]{1,0:T(8,128)}, f32[768,512]{1,0:T(8,128)}, bf16[1536,768]{1,0:T(8,128)(2,1)}, bf16[1536,512]{1,0:T(8,128)(2,1)}, bf16[2048,512]{1,0:T(8,1...) custom-call(bf16[1536,768]{1,0:T(8,128)(2,1)} %get-tuple-element.32.cd_ref, ...), custom_call_target="tpu_custom_call" | custom-call | tf_op jit(solution)/shard_map/ffn/pallas_call | solution.py:276
  90.3 19.0 %attn_bwd.1 = (bf16[1536,768]{1,0:T(8,128)(2,1)}, f32[1536,128]{1,0:T(8,128)}) custom-call(s32[1]{0:T(128)} %bitcast.cidx_ref, bf16[1536,768]{1,0:T(8,128)(2,1)} %get-tuple-element.35.dct_ref, bf16[6,64,1024]{2,1,0:T(8,128)(2,1)} %get-tuple-element.36.q_ref, f32[6,64,1024]{2,1,0:T(8,128)} %get-tuple-element.37.ctx_ref, ...), custom_call_target="tpu_custom_call" | custom-call | tf_op jit(solution)/shard_map/attn_bwd/pallas_call | solution.py:207
  109.3 3.1 %convolution_convert_fusion = bf16[1536,512]{1,0:T(8,128)(2,1)S(1)} fusion(bf16[1536,768]{1,0:T(8,128)(2,1)} %get-tuple-element.39, bf16[768,512]{1,0:T(8,128)(2,1)S(1)} %copy-done.3), kind=kOutput, calls=%fused_computation.1 | convolution fusion | flops 1208745984 | bytes 4718592 | tf_op jit(solution)/shard_map/dot_general | solution.py:225
  112.4 0.1 fusion.7
  112.6 0.6 copy-done.12
  113.2 1.3 slice.105
  114.6 1.5 fusion.8
  116.2 1.8 pad_maximum_fusion
  118.1 0.3 copy-done.6
  118.4 1.1 copy-done.15
  119.5 2.6 %fusion.11 = f32[768,512]{1,0:T(8,128)} fusion(bf16[1536,768]{1,0:T(8,128)(2,1)S(1)} %copy-done.15, bf16[1536,512]{1,0:T(8,128)(2,1)S(1)} %copy-done.6), kind=kOutput, calls=%fused_computation.46 | convolution fusion | flops 1207959552 | bytes 5505024 | tf_op jit(solution)/shard_map/dot_general | solution.py:225
  122.0 18.0 %reduce-scatter.2.cloned.1.call-done = f32[768,128]{1,0:T(8,128)} async-done(((f32[1536,128]{1,0:T(8,128)}), f32[768,128]{1,0:T(8,128)}) %reduce-scatter.2.cloned.1.call-update) | async-done | bytes 393232 | tf_op jit(solution)/shard_map/reduce_scatter | solution.py:528
  140.0 1.5 convolution_convert_fusion.2
  141.5 0.7 reshape.165
  142.3 3.0 %multiply_reduce_fusion = (bf16[512]{0:T(512)(128)(2,1)S(1)}, f32[768]{0:T(1024)}, f32[768]{0:T(1024)}, bf16[512]{0:T(512)(128)(2,1)S(1)}, f32[768,512]{1,0:T(8,128)S(1)}) fusion(f32[768]{0:T(1024)S(1)} %add_rsqrt_fusion, f32[768]{0:T(1024)S(1)} %broadcast_multiply_fusion.2, f32[1,768,512]{2,1,0:T(8,128)S(1)} %copy-done.1, f32[512]{0:T(512)S(1)} %copy-done.9, ...), kind=kOutput, calls=%fused_computation.4 | convolution fusion | flops 104756736 | bytes 5390336 | tf_op jit(solution)/shard_map/dot_general | solution.py:225
  145.3 1.6 concatenate.24
  146.9 0.7 pad.4.refs_4_
  147.6 72.5 %reduce_all.1 = (bf16[2048,512]{1,0:T(8,128)(2,1)}, bf16[2048,512]{1,0:T(8,128)(2,1)}, bf16[256,512]{1,0:T(8,128)(2,1)}, bf16[192,512]{1,0:T(8,128)(2,1)}, bf16[192,512]{1,0:T(8,128)(2,1)}) custom-call(bf16[2048,512]{1,0:T(8,128)(2,1)} %get-tuple-element.41.refs_0_, bf16[2048,512]{1,0:T(8,128)(2,1)} %get-tuple-element.42.refs_1_, ...), custom_call_target="tpu_custom_call" | custom-call | tf_op jit(solution)/shard_map/reduce_all/pallas_call | solution.py:470
  220.1 0.9 slice_convert_fusion
  221.1 0.6 fusion.9
  221.7 0.6 copy.59
  222.3 0.7 reshape.169
  223.0 1.7 convert_bitcast_fusion.1
  224.7 1.7 convert.32
  226.5 2.2 convert_bitcast_fusion
  228.6 2.7 %copy.58 = f32[4,64,8,512]{3,2,0,1:T(8,128)} copy(f32[4,64,8,512]{3,2,1,0:T(8,128)S(1)} %convert_bitcast_fusion) | data formatting | bytes 8388608 | tf_op jit(solution)/shard_map/reshape | solution.py:554
  231.3 2.6 %convert_element_type.77 = f32[2048,512]{1,0:T(8,128)} convert(bf16[2048,512]{1,0:T(8,128)(2,1)S(1)} %copy-done.4) | non-fusion elementwise | flops 1048576 | bytes 6291456 | tf_op jit(solution)/shard_map/convert_element_type | solution.py:556
  233.9 1.7 add_bitcast_fusion
  (61 shorter events, 0.9 us)
Async XLA Ops:
  7.2 4.1 %copy-start.14 = (s32[1,3]{1,0:T(1,128)S(1)}, s32[1,3]{1,0:T(1,128)}, u32[]{:S(2)}) copy-start(s32[1,3]{1,0:T(1,128)} %param.17) | copy-start | bytes 40
  7.2 4.6 %copy-start = (f32[1,768,512]{2,1,0:T(8,128)S(1)}, f32[1,768,512]{2,1,0:T(8,128)}, u32[]{:S(2)}) copy-start(f32[1,768,512]{2,1,0:T(8,128)} %param.16) | copy-start | bytes 4718596
  7.2 30.9 %all-gather.3.cloned.1.call-start = ((), (), s32[]{:S(2)}) async-start(), calls=%async_computation.1 | async-start | bytes 1769472 | tf_op jit(solution)/shard_map/all_gather | solution.py:493
  9.1 55.6 %all-gather.5.cloned.1.call-start = ((), (), s32[]{:S(2)}) async-start(), calls=%async_computation.2 | async-start | bytes 1769472 | tf_op jit(solution)/shard_map/all_gather | solution.py:494
  10.8 129.2 %reduce-scatter.2.cloned.1.call-start = ((), (), s32[]{:S(2)}) async-start(), calls=%async_computation.3 | async-start | bytes 1179648 | tf_op jit(solution)/shard_map/reduce_scatter | solution.py:528
  11.8 1.9 copy-start.9
  11.8 1.9 copy-start.13
  12.4 2.5 %copy-start.8 = (f32[512,128]{1,0:T(8,128)S(1)}, f32[512,128]{1,0:T(8,128)}, u32[]{:S(2)}) copy-start(f32[512,128]{1,0:T(8,128)} %param.23) | copy-start | bytes 786436
  14.1 10.7 %copy-start.2 = (bf16[768,512]{1,0:T(8,128)(2,1)}, bf16[768,512]{1,0:T(8,128)(2,1)S(1)}, u32[]{:S(2)}) copy-start(bf16[768,512]{1,0:T(8,128)(2,1)S(1)} %add_convert_fusion.act_ref) | copy-start | bytes 2359300
  90.2 19.1 %copy-start.3 = (bf16[768,512]{1,0:T(8,128)(2,1)S(1)}, bf16[768,512]{1,0:T(8,128)(2,1)}, u32[]{:S(2)}) copy-start(bf16[768,512]{1,0:T(8,128)(2,1)} %copy-done.2) | copy-start | bytes 2359300
  112.5 0.7 copy-start.12
  116.2 2.2 copy-start.6
  116.2 3.3 %copy-start.15 = (bf16[1536,768]{1,0:T(8,128)(2,1)S(1)}, bf16[1536,768]{1,0:T(8,128)(2,1)}, u32[]{:S(2)}) copy-start(bf16[1536,768]{1,0:T(8,128)(2,1)} %get-tuple-element.39) | copy-start | bytes 7077892
  119.5 22.8 %copy-start.1 = (f32[1,768,512]{2,1,0:T(8,128)S(1)}, f32[1,768,512]{2,1,0:T(8,128)}, u32[]{:S(2)}) copy-start(f32[1,768,512]{2,1,0:T(8,128)} %param.16) | copy-start | bytes 4718596
  140.0 2.2 copy-start.5
  228.6 2.7 %copy-start.4 = (bf16[2048,512]{1,0:T(8,128)(2,1)S(1)}, bf16[2048,512]{1,0:T(8,128)(2,1)}, u32[]{:S(2)}) copy-start(bf16[2048,512]{1,0:T(8,128)(2,1)} %get-tuple-element.50) | copy-start | bytes 6291460
  231.3 2.6 %copy-start.10 = (f32[768]{0:T(1024)S(1)}, f32[768]{0:T(1024)}, u32[]{:S(2)}) copy-start(f32[768]{0:T(1024)} %get-tuple-element.52) | copy-start | bytes 9220
  231.3 2.6 %copy-start.11 = (f32[768]{0:T(1024)S(1)}, f32[768]{0:T(1024)}, u32[]{:S(2)}) copy-start(f32[768]{0:T(1024)} %get-tuple-element.53) | copy-start | bytes 9220
  231.3 2.6 %copy-start.7 = (f32[768,512]{1,0:T(8,128)S(1)}, f32[768,512]{1,0:T(8,128)}, u32[]{:S(2)}) copy-start(f32[768,512]{1,0:T(8,128)} %get-tuple-element.34) | copy-start | bytes 4718596
Sparse Core Ops, SparseCore 0:
  10.2 27.7 all-gather.2
  40.3 24.3 all-gather.4
  109.4 30.5 reduce-scatter.1

commit v3 on v1

v3 whole, which is shorter than its diff:
```python
import functools
import math

import jax
import jax.numpy as jnp
from jax import lax
from jax.experimental import pallas as pl
from jax.experimental.pallas import tpu as pltpu
from jax.sharding import PartitionSpec as P

f32 = jnp.float32
bf16 = jnp.bfloat16
D = 512
HEAD = 64
TOP = 8
TB = 128
W = TOP * TB
NEG = -1e30
LOG2E = math.log2(math.e)
LN2 = math.log(2.0)
SMALL = 576
KBB = 384
STRIDE = 8
JOIN = 2
SAFE = 50.0
NN = (((1,), (0,)), ((), ()))
NT = (((1,), (1,)), ((), ()))
TN = (((0,), (0,)), ((), ()))
C0 = math.sqrt(2 / math.pi)
C1 = 0.044715
MESH = pl.DeviceIdType.MESH
AXES = ("dp", "ctx", "exp")


def attn_fwd_kernel(cidx_ref, act_ref, wq_ref, routes_ref, gates_ref, qdoc_ref, kaug_ref, vt_ref, kn_ref,
                    cd_ref, q_ref, ctx_ref, lse_ref,
                    qt, qaug, s, acc, *, experts, tok, KB):
    i=pl.program_id(0)
    c=cidx_ref[0]
    qt[...]=lax.dot_general(wq_ref[...], act_ref[...], NT, preferred_element_type=f32)*(0.125*LOG2E)
    n2=[]
    for k0 in range(0,TOP,4):
        r=[jnp.broadcast_to(routes_ref[k0+k:k0+k+1,:],(8,TB))[None] for k in range(4)]
        sel=[jnp.zeros((HEAD//8,8,TB),f32) for _ in range(4)]
        for e in range(experts):
            v=qt[e*HEAD:(e+1)*HEAD,:].reshape(HEAD//8,8,TB)
            sel=[jnp.where(r[k]==e,v,sel[k]) for k in range(4)]
        for k in range(4):
            sk=sel[k].reshape(HEAD,TB)
            n2.append(jnp.max(jnp.sum(sk*sk,axis=0,keepdims=True)))
            qaug[0:HEAD,(k0+k)*TB:(k0+k+1)*TB]=sk.astype(bf16)
    n2=functools.reduce(jnp.maximum,n2)*kn_ref[0]
    fast=n2<=SAFE*SAFE
    q_ref[0]=qaug[0:HEAD,:]
    qd=qdoc_ref[...]
    qaug[HEAD:HEAD+16,:]=jnp.concatenate([jnp.concatenate([qd,jnp.zeros_like(qd)],0)]*TOP,1).astype(bf16)
    qaug[HEAD+16:,:]=jnp.zeros((128-HEAD-16,W),bf16)
    q0=c*tok+i*TB
    nfull=q0//KB
    kd=pl.multiple_of(nfull*KB,KB)
    kp=lax.broadcasted_iota(jnp.int32,(KB,TB),0)+(kd-q0)
    tp=lax.broadcasted_iota(jnp.int32,(KB,TB),1)
    mask=kp<=tp
    acc[...]=jnp.zeros_like(acc)
    def scores(k0,n):
        return jnp.dot(kaug_ref[pl.ds(k0,n),:],qaug[...],preferred_element_type=f32)
    def masked(x):
        return jnp.concatenate([jnp.where(mask,x[:,k*TB:(k+1)*TB],NEG) for k in range(TOP)],1)
    def pv(k0,n,p):
        acc[...]+=jnp.dot(vt_ref[:,pl.ds(k0,n)],p,preferred_element_type=f32)
    def finish(m):
        l=acc[HEAD:HEAD+1,:]
        lse_ref[0]=m+jnp.log2(l)
        acc[0:HEAD,:]=acc[0:HEAD,:]*(1.0/l)
    @pl.when(fast)
    def _():
        def body(b,_):
            k0=pl.multiple_of(b*KB,KB)
            pv(k0,KB,jnp.exp2(scores(k0,KB)).astype(bf16))
            return 0
        lax.fori_loop(0,nfull,body,0)
        pv(kd,KB,jnp.exp2(masked(scores(kd,KB))).astype(bf16))
        finish(0.0)
    @pl.when(jnp.logical_not(fast))
    def _():
        def spass(b,m):
            k0=pl.multiple_of(b*KB,KB)
            x=scores(k0,KB)
            s[pl.ds(k0,KB),:]=x
            return jnp.maximum(m,jnp.max(x.reshape(KB//8,8,W),axis=0))
        m=lax.fori_loop(0,nfull,spass,jnp.full((8,W),NEG*2,f32))
        x=masked(scores(kd,KB))
        s[pl.ds(kd,KB),:]=x
        m=jnp.maximum(m,jnp.max(x.reshape(KB//8,8,W),axis=0))
        m=jnp.max(m,axis=0,keepdims=True)
        def ppass(b,_):
            k0=pl.multiple_of(b*KB,KB)
            pv(k0,KB,jnp.exp2(s[pl.ds(k0,KB),:]-m).astype(bf16))
            return 0
        lax.fori_loop(0,nfull+1,ppass,0)
        finish(m)
    ctx_ref[0]=acc[0:HEAD,:].astype(bf16)
    for k in range(TOP):
        acc[0:HEAD,k*TB:(k+1)*TB]*=gates_ref[k:k+1,:]
    r=[jnp.broadcast_to(routes_ref[k:k+1,:],(8,TB))[None] for k in range(TOP)]
    for h0 in range(0,HEAD,32):
        g=[acc[h0:h0+32,k*TB:(k+1)*TB].reshape(4,8,TB) for k in range(TOP)]
        for e in range(experts):
            o=jnp.zeros((4,8,TB),f32)
            for k in range(TOP):
                o=jnp.where(r[k]==e,g[k],o)
            cd_ref[e*HEAD+h0:e*HEAD+h0+32,:]=o.reshape(32,TB).astype(bf16)

def attn_fwd(cidx, act, wq, routesT, gatesT, qdoc, kaug, vt, kn, KB=256):
    tok=act.shape[0]; experts=wq.shape[0]//HEAD; keys=kaug.shape[0]; n=tok//TB; vr=vt.shape[0]
    full=lambda a: pl.BlockSpec(a.shape,lambda i,*_:(0,)*a.ndim)
    return pl.pallas_call(
        functools.partial(attn_fwd_kernel,experts=experts,tok=tok,KB=KB),
        grid_spec=pltpu.PrefetchScalarGridSpec(num_scalar_prefetch=1,grid=(n,),
          in_specs=[pl.BlockSpec((TB,D),lambda i,*_:(i,0)),full(wq),
            pl.BlockSpec((TOP,TB),lambda i,*_:(0,i)),pl.BlockSpec((TOP,TB),lambda i,*_:(0,i)),
            pl.BlockSpec((8,TB),lambda i,*_:(0,i)),full(kaug),full(vt),pl.BlockSpec(memory_space=pltpu.SMEM)],
          out_specs=[pl.BlockSpec((experts*HEAD,TB),lambda i,*_:(0,i)),
            pl.BlockSpec((1,HEAD,W),lambda i,*_:(i,0,0)),
            pl.BlockSpec((1,HEAD,W),lambda i,*_:(i,0,0)),
            pl.BlockSpec((1,1,W),lambda i,*_:(i,0,0))],
          scratch_shapes=[pltpu.VMEM((experts*HEAD,TB),f32),pltpu.VMEM((128,W),bf16),
            pltpu.VMEM((keys,W),f32),pltpu.VMEM((vr,W),f32)]),
        out_shape=[jax.ShapeDtypeStruct((experts*HEAD,tok),bf16),
          jax.ShapeDtypeStruct((n,HEAD,W),bf16),jax.ShapeDtypeStruct((n,HEAD,W),bf16),
          jax.ShapeDtypeStruct((n,1,W),f32)],
        compiler_params=pltpu.CompilerParams(vmem_limit_bytes=60*2**20),
        name="attn_fwd",
    )(cidx,act,wq,routesT,gatesT,qdoc,kaug,vt,kn)


def dot(a, b, dims=NN):
    return lax.dot_general(a, b, dims, preferred_element_type=f32)


def split3(x):
    hi = x.astype(bf16).astype(f32)
    r = x - hi
    mid = r.astype(bf16).astype(f32)
    return hi, mid, r - mid


class Here:
    def __init__(self, sizes):
        at = {a: lax.axis_index(a) for a in AXES}
        self.bit, self.dev = {}, {}
        for bits in mesh_bits(sizes).values():
            for ax, m in bits:
                b = lax.rem(at[ax] // m, 2)
                self.bit[ax, m] = b
                self.dev[ax, m] = tuple(at[a] + m - 2 * m * b if a == ax else at[a] for a in AXES)


def mesh_bits(sizes):
    return {a: [(a, 1 << i) for i in range(sizes[a].bit_length() - 1)] for a in AXES}


def chain_orders(sizes):
    b = mesh_bits(sizes)
    e, d, c = b["exp"], b["dp"], b["ctx"]
    late = e + d + c
    if len(d) + len(c) > 2:
        return [late, late, late]
    return [e[:1] + d + c + e[1:], e[:1] + c + d + e[1:], late]


def chain_plan(n, order):
    plan = []
    for bit in order:
        halve = n % 32 == 0
        n = n // 2 if halve else n
        plan.append((halve, bit, n))
    return plan


def rows(ref, start, n):
    return ref.at[pl.ds(pl.multiple_of(start, 16), n), :]


def add_rows(dst, d0, a, a0, b, b0, n):
    ch = math.gcd(n, 64)

    @pl.loop(0, n // ch)
    def _(t):
        o = pl.multiple_of(t * ch, ch)
        g = lambda r, s: r[pl.ds(pl.multiple_of(s + o, 16), ch), :]
        dst[pl.ds(pl.multiple_of(d0 + o, 16), ch), :] = g(a, a0) + g(b, b0)


def block_places(n, order, owner):
    bits = [bit for halve, bit, _ in chain_plan(n, order) if halve]
    own = sorted([b for b in bits if b[0] == owner], reverse=True)
    nat = own + sorted([b for b in bits if b[0] != owner])
    places = []
    for i in range(1 << len(nat)):
        v = {b: (i >> (len(nat) - 1 - k)) & 1 for k, b in enumerate(nat)}
        places.append(sum(v[b] << (len(bits) - 1 - k) for k, b in enumerate(bits)))
    return n >> len(nat), places


class Chain:
    def __init__(self, work, final, base, n, order, owner=None, fbase=0):
        self.work, self.final, self.base, self.n, self.order = work, final, base, n, order
        self.owner, self.fbase = owner, fbase
        self.plan = chain_plan(n, order)
        self.landed = sum(m for _, _, m in self.plan)
        self.back = [i for i in reversed(range(len(order))) if self.plan[i][0] and order[i][0] != owner]
        if owner:
            self.back.sort(key=lambda i: order[i], reverse=True)
        self.m = len(self.plan)
        self.nsem = self.m + len(self.back)
        self.nsteps = self.nsem + 1

    def place(self, here, land, lbase, ss, rs, sem):
        self.here, self.land, self.ss, self.rs, self.sem = here, land, ss, rs, sem
        self.lb = []
        for _, _, m in self.plan:
            self.lb.append(lbase)
            lbase += m
        self.offs = self.offsets()

    def offsets(self):
        offs, off = [], self.base
        for halve, bit, m in self.plan:
            b = self.here.bit[bit]
            offs.append((off + b * m, off + (1 - b) * m) if halve else (off, off))
            off = offs[-1][0]
        return offs

    def final_range(self, j):
        m = self.plan[-1][2]
        if self.owner is None:
            offs = self.offs
            if j == 0:
                return offs[-1][0], m
            i = self.back[j]
            return offs[i][0], self.plan[i][2]
        off, w = self.fbase, m
        for k, i in enumerate(self.back):
            if k >= j:
                off = off + self.here.bit[self.order[i]] * w
            w *= 2
        return off, m << j

    def copy(self, k):
        if k < self.m:
            _, bit, n = self.plan[k]
            src, dst = rows(self.work, self.offs[k][1], n), rows(self.land, self.lb[k], n)
        else:
            bit = self.order[self.back[k - self.m]]
            src = dst = rows(self.final, *self.final_range(k - self.m))
        return pltpu.make_async_remote_copy(
            src_ref=src, dst_ref=dst, send_sem=self.ss.at[self.sem + k], recv_sem=self.rs.at[self.sem + k],
            device_id=self.here.dev[bit], device_id_type=MESH)

    def step(self, k):
        if k:
            self.copy(k - 1).wait()
            if k <= self.m:
                i = k - 1
                last = i == self.m - 1
                d = self.offs[i][0]
                add_rows(self.final if last else self.work, self.final_range(0)[0] if last else d,
                         self.work, d, self.land, self.lb[i], self.plan[i][2])
        if k < self.nsem:
            self.copy(k).start()


def greet(here):
    bar = pltpu.get_barrier_semaphore()
    for dev in here.dev.values():
        pl.semaphore_signal(bar, inc=1, device_id=dev, device_id_type=MESH)
    pl.semaphore_wait(bar, len(here.dev))


def dense_parts(n, orders):
    a = n * 3 // 8 // 32 * 32
    return [(0, a, orders[0]), (a, a, orders[1]), (2 * a, n - 2 * a, orders[2])]


def make_chains(sizes, steps, part, nexp, keys, dsrc, fin, osrc, go, qsrc, gq, ksrc, kfin, ssrc, sfin):
    orders = chain_orders(sizes)
    n = sizes["exp"] * HEAD
    kbits = mesh_bits(sizes)["ctx"][::-1]
    part = part * JOIN
    dense = [[Chain(dsrc, fin, j * part + b, m, o) for b, m, o in dense_parts(part, orders)] for j in range(steps // JOIN)]
    return dict(
        dense=dense,
        o=[Chain(osrc, go, j * n, n, orders[j % 3], "exp", j * HEAD) for j in range(nexp)],
        q=[Chain(qsrc, gq, j * n, n, orders[j % 3], "exp", j * HEAD) for j in range(nexp)],
        k=[Chain(ksrc, kfin, 0, keys, kbits, "ctx", 0)],
        s=[Chain(ssrc, sfin, 0, SMALL, orders[0])],
    )


def flat(chains):
    wide = [c for g in chains["dense"] for c in g] + chains["o"] + chains["q"]
    return wide, chains["k"] + chains["s"]


def place_all(here, chains, land, nland, ss, rs):
    sem = 0
    for group, buf in zip(flat(chains), (land, nland)):
        lb = 0
        for c in group:
            c.place(here, buf, lb, ss, rs, sem)
            lb += c.landed
            sem += c.nsem


def mega_kernel(sizes, nf, nb, nexp, fb,
                cd, wo, tok, cot, g2, s2, up_ref, upb, down_ref, downb, q_ref, ctx_ref, lse_ref, routes_ref, gates_ref,
                qdoc_ref, kaug_ref, vaug_ref, kt_ref, act1, wq, kvw, g1,
                out, dx, fin_o, go_o, gq_o, sm_o,
                mid, rstd, act, actT, dffn, dct, dqd, gub, gsm,
                qaug, daug, rhs, pds, dq, dkv,
                dsrc, fin, osrc, go, qsrc, gq, ksrc, kfin, ssrc, sfin, land, nland, ss, rs, lsem):
    s = pl.program_id(0)
    experts = cd.shape[0] // HEAD
    ntok, keys = tok.shape[0], kaug_ref.shape[0]
    part = 2 * fb
    chains = make_chains(sizes, nf, part, nexp, keys, dsrc, fin, osrc, go, qsrc, gq, ksrc, kfin, ssrc, sfin)
    here = Here(sizes)
    place_all(here, chains, land, nland, ss, rs)
    ticks = [(j, p) for j in range(nf) for p in range(3)] + [(nf + i, p) for i in range(nb) for p in range(4)]
    ticks += [(nf + nb, p) for p in range(4)]
    table, late = {}, []
    for j, group in enumerate(chains["dense"] + [chains["o"]]):
        t0 = ticks.index((j * JOIN + JOIN - 1, 2)) if j < nf // JOIN else ticks.index((nf, 0))
        for k in range(max(c.nsteps for c in group)):
            todo = [(c, k) for c in group if k < c.nsteps]
            if t0 + STRIDE * k // 2 < len(ticks):
                table.setdefault(ticks[t0 + STRIDE * k // 2], []).extend(todo)
            else:
                late.extend(todo)

    def tick(step, pos):
        for at, todo in table.items():
            if at[1] != pos or step != ("f" if at[0] < nf else "b" if at[0] < nf + nb else "t"):
                continue
            if step == "t":
                for c, k in todo:
                    c.step(k)
                continue

            @pl.when(s == at[0])
            def _():
                for c, k in todo:
                    c.step(k)

    def put_owner(src_rows, value, e, order_of):
        for j in range(nexp):
            c = order_of[j]
            block, places = block_places(c.n, c.order, "exp")
            per = HEAD // block
            for b in range(per):
                at = c.base + places[e * per + b] * block
                src_rows[at:at + block, :] = value[j * HEAD + b * block:j * HEAD + (b + 1) * block, :]

    @pl.when(s == 0)
    def _():
        m = tok[...] + dot(cd[...], wo[...], TN)
        mid[...] = m
        cen = m - jnp.mean(m, axis=-1, keepdims=True)
        r = lax.rsqrt(jnp.mean(cen * cen, axis=-1, keepdims=True) + 1e-5)
        xh = cen * r
        rstd[...] = jnp.broadcast_to(r, rstd.shape)
        a = xh * g2[...] + s2[...]
        act[...] = a.astype(bf16)
        actT[...] = jnp.transpose(a).astype(bf16)
        dffn[...] = cot[...].astype(bf16)
        out[...] = m + downb[...]
        dx[...] = jnp.zeros_like(dx)
        greet(here)

    @pl.when(s < nf)
    def _():
        up, down = up_ref[...], down_ref[...]
        pre = dot(act[...], up) + upb[...]
        x2 = pre * pre
        th = jnp.tanh(pre * (C0 + C0 * C1 * x2))
        h = 0.5 * (1.0 + th)
        hid = (pre * h).astype(bf16)
        gp = h + (0.5 * pre) * (1.0 - th * th) * (C0 + 3.0 * C0 * C1 * x2)
        out[...] += dot(hid, down)
        tick("f", 0)
        r0 = pl.multiple_of(s * part, part)
        dsrc[pl.ds(r0, fb), :] = dot(hid, dffn[...], TN).astype(bf16)
        tick("f", 1)
        dpb = (dot(dffn[...], down, NT) * gp).astype(bf16)
        gub[pl.ds(s, 1), :] = jnp.sum(dpb.astype(f32), axis=0, keepdims=True)
        dsrc[pl.ds(pl.multiple_of(r0 + fb, fb), fb), :] = dot(actT[...], dpb).astype(bf16)
        dx[...] += dot(dpb, up, NT)
        tick("f", 2)

    @pl.when(s == nf - 1)
    def _():
        d = dx[...]
        m = mid[...]
        xh = (m - jnp.mean(m, axis=-1, keepdims=True)) * rstd[:, 0:1]
        gx = d * g2[...]
        dm = cot[...] + rstd[:, 0:1] * (gx - jnp.mean(gx, axis=-1, keepdims=True)
                                        - xh * jnp.mean(gx * xh, axis=-1, keepdims=True))
        mid[...] = dm
        gsm[...] = jnp.concatenate([jnp.sum(d * xh, axis=0, keepdims=True), jnp.sum(d, axis=0, keepdims=True),
                                    jnp.sum(dffn[...].astype(f32), axis=0, keepdims=True)], axis=0)
        dmb = dm.astype(bf16)
        act[...] = dmb
        dct[...] = dot(wo[...], dmb, NT).astype(bf16)
        w = nexp * HEAD
        for e in range(sizes["exp"]):
            put_owner(osrc, dot(cd[e * w:(e + 1) * w, :], dmb).astype(bf16), e, chains["o"])

    @pl.when(s == nf)
    def _():
        dkv[...] = jnp.zeros_like(dkv)
        rhs[...] = jnp.zeros_like(rhs)

    @pl.when((s >= nf) & (s < nf + nb))
    def _():
        i = s - nf
        lanes = pl.ds(pl.multiple_of(i * TB, TB), TB)
        q = q_ref[0]
        qaug[0:HEAD, :] = q
        rhs[0:HEAD, 0:W] = q
        hi, md, lo = split3(-lse_ref[0])
        qd = qdoc_ref[...]
        qaug[HEAD:HEAD + 16, :] = jnp.concatenate(
            [jnp.concatenate([qd[0:3, :]] * TOP, 1), hi, md, lo, jnp.zeros((10, W), f32)], 0).astype(bf16)
        qaug[HEAD + 16:, :] = jnp.zeros((128 - HEAD - 16, W), bf16)
        r = [jnp.broadcast_to(routes_ref[k:k + 1, :], (8, TB))[None] for k in range(TOP)]
        for k0 in range(0, TOP, 4):
            sel = [jnp.zeros((HEAD // 8, 8, TB), f32) for _ in range(4)]
            for e in range(experts):
                v = dct[e * HEAD:(e + 1) * HEAD, lanes].astype(f32).reshape(HEAD // 8, 8, TB)
                sel = [jnp.where(r[k0 + k] == e, v, sel[k]) for k in range(4)]
            for k in range(4):
                sl = slice((k0 + k) * TB, (k0 + k + 1) * TB)
                dc = (sel[k].reshape(HEAD, TB) * gates_ref[k0 + k:k0 + k + 1, :]).astype(bf16)
                daug[0:HEAD, sl] = dc
                rhs[HEAD:, W + (k0 + k) * TB:W + (k0 + k + 1) * TB] = dc
                dq[0:1, sl] = jnp.sum(dc.astype(f32) * ctx_ref[0, :, sl].astype(f32), axis=0, keepdims=True)
        hi, md, lo = split3(-dq[0:1, :])
        daug[HEAD:HEAD + 16, :] = jnp.concatenate([hi, md, lo, jnp.zeros((13, W), f32)], 0).astype(bf16)
        daug[HEAD + 16:, :] = jnp.zeros((128 - HEAD - 16, W), bf16)
        dq[...] = jnp.zeros_like(dq)
        q0 = lax.axis_index("ctx") * ntok + i * TB
        nfull = q0 // KBB
        kd = pl.multiple_of(nfull * KBB, KBB)

        def block(k0, mask):
            p = jnp.exp2(dot(kaug_ref[pl.ds(k0, KBB), :], qaug[...]))
            if mask is not None:
                p = jnp.concatenate([jnp.where(mask, p[:, k * TB:(k + 1) * TB], 0.0) for k in range(TOP)], 1)
            dp = dot(vaug_ref[pl.ds(k0, KBB), :], daug[...])
            pds[:, W:] = p.astype(bf16)
            pds[:, :W] = (p * dp).astype(bf16)
            dq[...] += dot(kt_ref[:, pl.ds(k0, KBB)], pds[:, :W])
            dkv[pl.ds(k0, KBB), :] += dot(pds[...], rhs[...], NT)

        def body(b, _):
            block(pl.multiple_of(b * KBB, KBB), None)
            return 0

        tick("b", 0)
        lax.fori_loop(0, nfull, body, 0)
        tick("b", 1)
        kp = lax.broadcasted_iota(jnp.int32, (KBB, TB), 0) + (kd - q0)
        tp = lax.broadcasted_iota(jnp.int32, (KBB, TB), 1)
        block(kd, kp <= tp)
        tick("b", 2)
        dq[...] *= 0.125
        for h0 in range(0, HEAD, 32):
            g = [dq[h0:h0 + 32, k * TB:(k + 1) * TB].reshape(4, 8, TB) for k in range(TOP)]
            for e in range(experts):
                o = jnp.zeros((4, 8, TB), f32)
                for k in range(TOP):
                    o = jnp.where(r[k] == e, g[k], o)
                dqd[e * HEAD + h0:e * HEAD + h0 + 32, lanes] = o.reshape(32, TB).astype(bf16)
        tick("b", 3)

    @pl.when(s == nf + nb)
    def _():
        lane = lax.broadcasted_iota(jnp.int32, (1, 128), 1)
        ksrc[...] = (dkv[...] * jnp.where(lane < HEAD, LN2, 1.0)).astype(bf16)
        kc, sc = chains["k"][0], chains["s"][0]
        kc.step(0)
        tick("t", 0)
        w = nexp * HEAD
        for e in range(sizes["exp"]):
            put_owner(qsrc, dot(dqd[e * w:(e + 1) * w, :], act1[...]).astype(bf16), e, chains["q"])
        for c in chains["q"]:
            c.step(0)
        tick("t", 1)
        for k in range(1, kc.nsteps):
            kc.step(k)
        da = dot(dqd[...], wq[...], TN) + dot(kfin[...], kvw[...], NT)
        for c in chains["q"]:
            c.step(1)
        tick("t", 2)
        x = tok[...]
        cen = x - jnp.mean(x, axis=-1, keepdims=True)
        r1 = lax.rsqrt(jnp.mean(cen * cen, axis=-1, keepdims=True) + 1e-5)
        xh = cen * r1
        gg1, gs1 = jnp.sum(da * xh, axis=0, keepdims=True), jnp.sum(da, axis=0, keepdims=True)
        gx = da * g1[...]
        dx[...] = mid[...] + r1 * (gx - jnp.mean(gx, axis=-1, keepdims=True)
                                   - xh * jnp.mean(gx * xh, axis=-1, keepdims=True))
        ssrc[0:D, :] = dot(act1[...], kfin[...], TN).astype(bf16)
        vecs = [gsm[0:1, :], gsm[1:2, :], gsm[2:3, :], gg1, gs1] + [gub[j:j + 1, :] for j in range(nf)]
        vecs = [v[:, o:o + 128] for v in vecs for o in range(0, v.shape[1], 128)]
        vecs.append(jnp.zeros((SMALL - D - len(vecs), 128), f32))
        ssrc[D:SMALL, :] = jnp.concatenate(vecs, 0).astype(bf16)
        tick("t", 3)
        tail = [[(c, k + 2) for c in chains["q"] if k + 2 < c.nsteps] + ([(sc, k)] if k < sc.nsteps else []) for k in range(20)]
        for k in range(20):
            for c, n in tail[k]:
                c.step(n)
            for c, n in late[k * len(late) // 6:(k + 1) * len(late) // 6]:
                c.step(n)
            if k == 6:
                moved = pltpu.make_async_copy(fin, fin_o, lsem.at[0])
                moved.start()
        qg = pltpu.make_async_copy(gq, gq_o, lsem.at[2])
        qg.start()
        og = pltpu.make_async_copy(go, go_o, lsem.at[1])
        og.start()
        sg = pltpu.make_async_copy(sfin, sm_o, lsem.at[3])
        sg.start()
        for c in (moved, og, qg, sg):
            c.wait()


def mega(sizes, nexp, cd, wo, tok, cot, g2, s2, up, upb, down, downb, q, ctx, lse, routes, gates, qdoc, kaug, vaug, kt,
         act1, wq, kvw, g1, fb=512):
    ntok, keys, ff, eh = tok.shape[0], kaug.shape[0], up.shape[1], wo.shape[0]
    nf, nb = ff // fb, ntok // TB
    part = 2 * fb
    sd = jax.ShapeDtypeStruct
    z = [None] * 10
    chains = make_chains(sizes, nf, part, nexp, keys, *z)
    wide, narrow = flat(chains)
    land, nland = sum(c.landed for c in wide), sum(c.landed for c in narrow)
    nsem = sum(c.nsem for c in wide + narrow)
    once = pl.Buffered(1)
    full = lambda a: pl.BlockSpec(a.shape, lambda s: (0,) * a.ndim, pipeline_mode=once)
    fo = lambda *sh: pl.BlockSpec(sh, lambda s: (0,) * len(sh), pipeline_mode=once)
    fj = lambda s: jnp.minimum(s, nf - 1)
    bi = lambda s: jnp.clip(s - nf, 0, nb - 1)
    blk = lambda r: pl.BlockSpec((r, TB), lambda s: (0, bi(s)))
    b3 = lambda a: pl.BlockSpec((1,) + a.shape[1:], lambda s: (bi(s), 0, 0))
    any_ = pl.BlockSpec(memory_space=pl.ANY)
    v = pltpu.VMEM
    return pl.pallas_call(
        functools.partial(mega_kernel, sizes, nf, nb, nexp, fb),
        grid=(nf + nb + 1,),
        in_specs=[full(cd), full(wo), full(tok), full(cot), full(g2), full(s2),
                  pl.BlockSpec((D, fb), lambda s: (0, fj(s))), pl.BlockSpec((1, fb), lambda s: (0, fj(s))),
                  pl.BlockSpec((fb, D), lambda s: (fj(s), 0)), full(downb), b3(q), b3(ctx), b3(lse),
                  blk(TOP), blk(TOP), blk(8), full(kaug), full(vaug), full(kt), full(act1), full(wq), full(kvw), full(g1)],
        out_specs=[fo(ntok, D), fo(ntok, D), any_, any_, any_, any_],
        out_shape=[sd((ntok, D), f32), sd((ntok, D), f32), sd((nf * part, D), bf16), sd((nexp * HEAD, D), bf16),
                   sd((nexp * HEAD, D), bf16), sd((SMALL, 128), bf16)],
        scratch_shapes=[
            v((ntok, D), f32), v((ntok, 128), f32), v((ntok, D), bf16), v((D, ntok), bf16),
            v((ntok, D), bf16), v((eh, ntok), bf16), v((eh, ntok), bf16), v((nf, fb), f32), v((3, D), f32),
            v((128, W), bf16), v((128, W), bf16), v((128, 2 * W), bf16), v((KBB, 2 * W), bf16), v((HEAD, W), f32),
            v((keys, 128), f32),
            v((nf * part, D), bf16), v((nf * part, D), bf16), v((eh, D), bf16), v((nexp * HEAD, D), bf16),
            v((eh, D), bf16), v((nexp * HEAD, D), bf16), v((keys, 128), bf16), v((ntok, 128), bf16),
            v((SMALL, 128), bf16), v((SMALL, 128), bf16), v((land, D), bf16), v((nland, 128), bf16),
            pltpu.SemaphoreType.DMA((nsem,)), pltpu.SemaphoreType.DMA((nsem,)), pltpu.SemaphoreType.DMA((4,))],
        compiler_params=pltpu.CompilerParams(collective_id=0, has_side_effects=True, vmem_limit_bytes=62 * 2**20),
        name="mega",
    )(cd, wo, tok, cot, g2, s2, up, upb, down, downb, q, ctx, lse, routes, gates, qdoc, kaug, vaug, kt, act1, wq, kvw, g1)


def local(sizes, tokens, lengths, routes, route_gates, cotangent, gain_one, shift_one, kv_weight,
          query_weight, out_weight, gain_two, shift_two, up_weight, up_bias, down_weight, down_bias):
    x = tokens[0]
    tok = x.shape[0]
    ncx = sizes["ctx"]
    group = tok * ncx
    nexp = query_weight.shape[0]
    experts = nexp * sizes["exp"]
    cidx = lax.axis_index("ctx")
    wq_own = jnp.swapaxes(query_weight, 1, 2).reshape(nexp * HEAD, D).astype(bf16)
    wo_own = out_weight.reshape(nexp * HEAD, D).astype(bf16)
    wq = lax.all_gather(wq_own, "exp", axis=0, tiled=True)
    wo = lax.all_gather(wo_own, "exp", axis=0, tiled=True)
    cen = x - jnp.mean(x, axis=-1, keepdims=True)
    rs1 = lax.rsqrt(jnp.mean(cen * cen, axis=-1, keepdims=True) + 1e-5)
    xh1 = cen * rs1
    act = (xh1 * gain_one + shift_one).astype(bf16)
    kvw = kv_weight.astype(bf16)
    kv_own = dot(act, kvw).astype(bf16)
    kv = lax.all_gather(kv_own, "ctx", axis=0, tiled=True)
    keys, vals = kv[:, :HEAD], kv[:, HEAD:]
    kn = jnp.max(jnp.sum(jnp.square(keys.astype(f32)), axis=1)).reshape(1)
    pos = jnp.arange(group, dtype=jnp.int32)
    docs, end = jnp.zeros_like(pos), 0
    for d in range(lengths.shape[1] - 1):
        end = end + lengths[0, d]
        docs = docs + (pos >= end).astype(jnp.int32)
    hot = (docs[:, None] == jnp.arange(3)[None, :]).astype(bf16)
    one3 = jnp.ones((group, 3), bf16)
    kaug = jnp.concatenate([keys, hot, one3, jnp.zeros((group, HEAD - 6), bf16)], axis=1)
    vaug = jnp.concatenate([vals, one3, jnp.zeros((group, HEAD - 3), bf16)], axis=1)
    kt = keys.T
    vt = jnp.concatenate([vals.T, jnp.ones((1, group), bf16), jnp.zeros((15, group), bf16)], axis=0)
    qdocs = lax.dynamic_slice_in_dim(docs, cidx * tok, tok)
    slot = jnp.arange(8, dtype=jnp.int32)[:, None]
    qdoc = jnp.where((qdocs[None, :] == slot) | (slot > 2), 0.0, NEG).astype(f32)
    routes_t = routes[0].T
    gates_t = route_gates[0].T
    cvec = cidx.reshape(1).astype(jnp.int32)

    cd, q, ctx, lse = attn_fwd(cvec, act, wq, routes_t, gates_t, qdoc, kaug, vt, kn, KB=384)
    row = lambda v: v.reshape(1, -1)
    out, dx, dense, go, gq, small = mega(
        sizes, nexp, cd, wo, x, cotangent[0], row(gain_two), row(shift_two), up_weight.astype(bf16),
        row(up_bias), down_weight.astype(bf16), row(down_bias), q, ctx, lse, routes_t, gates_t, qdoc, kaug, vaug, kt, act, wq, kvw, row(gain_one))
    go = go.astype(f32).reshape(nexp, HEAD, D)
    gq = jnp.swapaxes(gq.astype(f32).reshape(nexp, HEAD, D), 1, 2)
    dense = dense.reshape(-1, 2, D, D)
    gdown = dense[:, 0].astype(f32).reshape(-1, D)
    gup = dense[:, 1].astype(f32).transpose(1, 0, 2).reshape(D, -1)
    small = small.astype(f32)
    vec = small[D:].reshape(-1)
    v = lambda i: vec[i * D:(i + 1) * D]
    return (out[None], dx[None], v(3), v(4), small[:D], gq, go, v(0), v(1), gup, vec[5 * D:5 * D + up_bias.shape[0]],
            gdown, v(2))


def solution(mesh):
    tok3 = P(("dp", "exp"), "ctx", None)
    ex = P("exp", None, None)
    r = P()
    in_specs = (tok3, P(("dp", "exp"), None), tok3, tok3, tok3, r, r, r, ex, ex, r, r, r, r, r, r)
    out_specs = (tok3, tok3, r, r, r, ex, ex, r, r, r, r, r, r)
    fn = functools.partial(local, dict(mesh.shape))
    return jax.shard_map(fn, mesh=mesh, in_specs=in_specs, out_specs=out_specs, check_vma=False)
```

time: 518 us -> 199 us (0.38)
  waiting for transfers between devices: 350 us -> 14.1 us
  Pallas kernels: 60.2 us -> 125 us
  blocking collectives: 50.5 us -> 8.53 us
  matrix products: 12.9 us -> 0.4 us
    psum x3 -> x0, waiting for transfers between devices: 309 us -> none  [the longest x1 141 us: local(): gup, gdown = lax.psum((gup, gdown), ('dp', 'ctx', 'exp'))]
    pallas_call x2 -> x1, Pallas kernels: 44.7 us -> 110 us  [mega(): pl.pallas_call(functools.partial(mega_kernel, sizes, nf, nb, nexp, fb), g...]
    psum x1 -> x0, blocking collectives: 42 us -> none  [local(): lax.psum((gg1, gs1, gkv, gub, gsm), ('dp', 'ctx', 'exp'))]
    reduce_scatter x2 -> x0, waiting for transfers between devices: 19.9 us -> none  [the longest x1 19.9 us: local(): lax.psum_scatter(dkv_part, 'ctx', scatter_dimension=0, tiled=True)]
    dot_general x5 -> x1, matrix products: 12.9 us -> 0.4 us  [dot(): return lax.dot_general(a, b, dims, preferred_element_type=f32)]
    all_gather x1, waiting for transfers between devices: 9.32 us -> 3.38 us  [local(): wq = lax.all_gather(wq_own, 'exp', axis=0, tiled=True)]
  transfers between devices with their start and end apart: 7 -> 2, of which waited for: 6 -> 2; matrix products, arithmetic and copies ran while one was open for 7% -> 8% of each run, Pallas kernels for 3% -> 8%
where the time goes in v3:
time: 199 us
  Pallas kernels  125 us (63%)
  other arithmetic  22.1 us (11%)
  between operations  15.5 us (8%)
  waiting for transfers between devices  14.1 us (7%)
  local copies, waits for them, and re-layouts  12.5 us (6%)
  blocking collectives  8.53 us (4%)
    pallas_call x1, Pallas kernels, mega(): pl.pallas_call(functools.partial(mega_kernel, sizes, nf, nb, nexp, fb), g...  110 us
    pallas_call x1, Pallas kernels, attn_fwd(): pl.pallas_call(functools.partial(attn_fwd_kernel, experts=experts, tok=to...  15.5 us
    all_gather x1, waiting for transfers between devices, local(): wo = lax.all_gather(wo_own, 'exp', axis=0, tiled=True)  10.7 us
    all_gather x1, blocking collectives, local(): kv = lax.all_gather(kv_own, 'ctx', axis=0, tiled=True)  8.53 us
    convert_element_type x1, other arithmetic, local(): up_weight.astype(bf16)  4.02 us
  transfers between devices with their start and end apart: 2, of which 2 were waited for; matrix products, arithmetic and copies ran while one was open for 8% of the time, Pallas kernels for 8%

profile of v3, /device:TPU:0, one launch (start us, length us, event | category | flops | bytes accessed | tf_op | source)
XLA Modules:
  0.0 198.5 jit_solution(9527645947642722590)
XLA Ops:
  7.2 0.0 copy-start
  7.2 0.0 all-gather.3.cloned.1.call-start
  7.2 1.8 convert_element_type.67
  9.1 0.0 all-gather.3.cloned.1.call-update
  9.1 0.0 all-gather.5.cloned.1.call-start
  9.1 1.7 convert_element_type.76
  10.8 0.0 all-gather.5.cloned.1.call-update
  10.9 0.1 pad.4.clone
  10.9 0.1 pad.2.clone
  11.0 0.1 pad.5.clone
  11.1 0.1 pad.9.clone
  11.2 0.6 fusion.4
  11.8 0.0 copy-start.9
  11.8 0.2 reduce_sum.27
  12.0 0.3 multiply_reduce_fusion
  12.3 0.4 copy-done.6
  14.1 0.3 add_convert_fusion.act_ref.act1
  14.4 0.0 copy-start.1
  14.4 0.7 convert_add_fusion
  15.1 0.1 dynamic_slice.3
  15.2 0.4 convolution_convert_fusion
  15.6 8.5 %all_gather.10 = bf16[1536,128]{0,1:T(8,128)(2,1)S(1)} all-gather(bf16[768,128]{0,1:T(8,128)(2,1)S(1)} %convolution_convert_fusion), channel_id=1, replica_groups=mesh['dp'=2,'ctx'=2,'exp'=8] {'ctx'}, dimensions={0}, use_global_device_ids=true | all-gather | bytes 589824 | tf_op jit(solution)/shard_map/all_gather | solution.py:602
  24.1 0.7 slice_bitcast_fusion.8
  24.9 0.2 maximum_maximum_fusion.1
  25.0 0.9 copy.32.vaug_ref
  26.0 0.9 copy.30.kaug_ref
  26.9 4.0 %convert_element_type.78.up_ref = bf16[512,2048]{1,0:T(8,128)(2,1)} convert(f32[512,2048]{1,0:T(8,128)} %param.28) | non-fusion elementwise | flops 1048576 | bytes 6291456 | tf_op jit(solution)/shard_map/convert_element_type | solution.py:626
  30.9 1.6 convert_element_type.79.down_ref
  32.5 0.1 multiply_reduce_fusion.1
  32.5 0.6 reduce_max.9
  33.1 0.7 fusion.1.qdoc_ref
  33.8 0.8 maximum_maximum_fusion.2.vt_ref
  34.7 3.4 %all-gather.3.cloned.1.call-done.wq_ref.wq = bf16[1536,512]{1,0:T(8,128)(2,1)} async-done(((bf16[192,512]{1,0:T(8,128)(2,1)}), bf16[1536,512]{1,0:T(8,128)(2,1)}) %all-gather.3.cloned.1.call-update) | async-done | bytes 1572880 | tf_op jit(solution)/shard_map/all_gather | solution.py:594
  38.0 15.5 %attn_fwd.1 = (bf16[1536,768]{1,0:T(8,128)(2,1)}, bf16[6,64,1024]{2,1,0:T(8,128)(2,1)}, bf16[6,64,1024]{2,1,0:T(8,128)(2,1)}, f32[6,1,1024]{2,1,0:T(1,128)}) custom-call(s32[1]{0:T(128)} %bitcast.cidx_ref, bf16[768,512]{1,0:T(8,128)(2,1)} %copy-done.1, bf16[1536,512]{1,0:T(8,128)(2,1)} %all-gather.3.cloned.1.call-done.wq_ref.wq, s32[8,768]{1,0:T(8,128)} %bitcast.73, ...), custom_call_target="tpu_custom_call" | custom-call | tf_op jit(solution)/shard_map/attn_fwd/pallas_call | solution.py:117
  53.6 10.7 %all-gather.5.cloned.1.call-done.wo = bf16[1536,512]{1,0:T(8,128)(2,1)} async-done(((bf16[192,512]{1,0:T(8,128)(2,1)}), bf16[1536,512]{1,0:T(8,128)(2,1)}) %all-gather.5.cloned.1.call-update) | async-done | bytes 1572880 | tf_op jit(solution)/shard_map/all_gather | solution.py:595
  64.3 109.8 %mega.1 = (f32[768,512]{1,0:T(8,128)}, f32[768,512]{1,0:T(8,128)}, bf16[4096,512]{1,0:T(8,128)(2,1)}, bf16[192,512]{1,0:T(8,128)(2,1)}, bf16[192,512]{1,0:T(8,128)(2,1)}, /*index=5*/bf16[576,128]{1,0:T(8,128)(2,1)}) custom-call(bf16[1536,768]{1,0:T(8,128)(2,1)} %get-tuple-element.23.cd, bf16[1536,512]{1,0:T(8,128)(2,1)} %all-gather.5.cloned.1.call-done.wo, ...), custom_call_target="tpu_custom_call" | custom-call | tf_op jit(solution)/shard_map/mega/pallas_call | solution.py:559
  174.1 1.7 slice.87
  175.7 0.9 convert_element_type.80
  176.7 0.6 slice_bitcast_fusion.1
  177.3 0.6 slice_bitcast_fusion.2
  177.9 1.7 convert_bitcast_fusion.1
  179.6 0.8 convert.8
  180.4 2.9 %fusion.3 = (bf16[4,1,512,512]{3,2,1,0:T(8,128)(2,1)S(1)}, f32[4,64,8,512]{3,2,1,0:T(8,128)S(1)}) fusion(bf16[4,2,512,512]{3,2,1,0:T(8,128)(2,1)} %bitcast.64), kind=kLoop, calls=%fused_computation.30 | loop fusion | flops 1048576 | bytes 10485760 | tf_op jit(solution)/shard_map/slice | solution.py:631
  183.3 2.7 %bitcast_convert_fusion = f32[2048,512]{1,0:T(8,128)} fusion(bf16[4,1,512,512]{3,2,1,0:T(8,128)(2,1)S(1)} %get-tuple-element.33), kind=kLoop, calls=%fused_computation.2 | loop fusion | flops 1048576 | bytes 6291456 | tf_op jit(solution)/shard_map/convert_element_type | solution.py:631
  186.1 2.5 %copy.35 = f32[4,64,8,512]{3,2,0,1:T(8,128)} copy(f32[4,64,8,512]{3,2,1,0:T(8,128)S(1)} %get-tuple-element.34) | data formatting | bytes 8388608 | tf_op jit(solution)/shard_map/reshape | solution.py:632
  188.6 1.1 copy.38
  189.7 0.8 copy-done.3
  190.5 1.1 copy.39
  (26 shorter events, 0.1 us)
Async XLA Ops:
  7.2 4.0 %copy-start.10 = (s32[1,3]{1,0:T(1,128)S(1)}, s32[1,3]{1,0:T(1,128)}, u32[]{:S(2)}) copy-start(s32[1,3]{1,0:T(1,128)} %param.17) | copy-start | bytes 40
  7.2 4.6 %copy-start = (f32[1,768,512]{2,1,0:T(8,128)S(1)}, f32[1,768,512]{2,1,0:T(8,128)}, u32[]{:S(2)}) copy-start(f32[1,768,512]{2,1,0:T(8,128)} %param.16) | copy-start | bytes 4718596
  7.2 30.8 %all-gather.3.cloned.1.call-start = ((), (), s32[]{:S(2)}) async-start(), calls=%async_computation | async-start | bytes 1769472 | tf_op jit(solution)/shard_map/all_gather | solution.py:594
  9.1 55.2 %all-gather.5.cloned.1.call-start = ((), (), s32[]{:S(2)}) async-start(), calls=%async_computation.1 | async-start | bytes 1769472 | tf_op jit(solution)/shard_map/all_gather | solution.py:595
  11.8 1.0 copy-start.6
  11.8 2.3 %copy-start.8 = (f32[512]{0:T(512)S(1)}, f32[512]{0:T(512)}, u32[]{:S(2)}) copy-start(f32[512]{0:T(512)} %param.21) | copy-start | bytes 6148
  11.8 2.3 %copy-start.9 = (f32[512]{0:T(512)S(1)}, f32[512]{0:T(512)}, u32[]{:S(2)}) copy-start(f32[512]{0:T(512)} %param.22) | copy-start | bytes 6148
  12.7 2.8 %copy-start.5 = (bf16[512,128]{1,0:T(8,128)(2,1)}, bf16[512,128]{1,0:T(8,128)(2,1)S(1)}, u32[]{:S(2)}) copy-start(bf16[512,128]{1,0:T(8,128)(2,1)S(1)} %convert_element_type.72.kvw) | copy-start | bytes 393220
  14.4 10.6 %copy-start.1 = (bf16[768,512]{1,0:T(8,128)(2,1)}, bf16[768,512]{1,0:T(8,128)(2,1)S(1)}, u32[]{:S(2)}) copy-start(bf16[768,512]{1,0:T(8,128)(2,1)S(1)} %add_convert_fusion.act_ref.act1) | copy-start | bytes 2359300
  26.9 4.0 %copy-start.2 = (f32[2048,512]{1,0:T(8,128)S(1)}, f32[2048,512]{1,0:T(8,128)}, u32[]{:S(2)}) copy-start(f32[2048,512]{1,0:T(8,128)} %param.30) | copy-start | bytes 12582916
  174.1 5.5 %copy-start.7 = (bf16[192,512]{1,0:T(8,128)(2,1)S(1)}, bf16[192,512]{1,0:T(8,128)(2,1)}, u32[]{:S(2)}) copy-start(bf16[192,512]{1,0:T(8,128)(2,1)} %get-tuple-element.31) | copy-start | bytes 589828
  186.1 2.5 %copy-start.4 = (f32[768,512]{1,0:T(8,128)S(1)}, f32[768,512]{1,0:T(8,128)}, u32[]{:S(2)}) copy-start(f32[768,512]{1,0:T(8,128)} %get-tuple-element.27) | copy-start | bytes 4718596
  188.6 2.0 copy-start.3
Sparse Core Ops, SparseCore 0:
  10.2 27.7 all-gather.2
  39.7 24.5 all-gather.4

commit v4 on v3

--- a/solution.py
+++ b/solution.py
@@ -32,11 +32,16 @@
 AXES = ("dp", "ctx", "exp")
 
 
-def attn_fwd_kernel(cidx_ref, act_ref, wq_ref, routes_ref, gates_ref, qdoc_ref, kaug_ref, vt_ref, kn_ref,
+def attn_fwd_kernel(act_ref, wq_ref, routes_ref, gates_ref, qdoc_ref, kaug_ref, vt_ref,
                     cd_ref, q_ref, ctx_ref, lse_ref,
-                    qt, qaug, s, acc, *, experts, tok, KB):
+                    qt, qaug, s, acc, kn_ref, *, experts, tok, KB):
     i=pl.program_id(0)
-    c=cidx_ref[0]
+    c=lax.axis_index("ctx")
+    @pl.when(i==0)
+    def _():
+        kk=kaug_ref[...].astype(f32)
+        kk=jnp.where(lax.broadcasted_iota(jnp.int32,kk.shape,1)<HEAD,kk*kk,0.0)
+        kn_ref[0]=jnp.max(jnp.sum(kk,axis=1,keepdims=True))
     qt[...]=lax.dot_general(wq_ref[...], act_ref[...], NT, preferred_element_type=f32)*(0.125*LOG2E)
     n2=[]
     for k0 in range(0,TOP,4):
@@ -111,27 +116,27 @@
                 o=jnp.where(r[k]==e,g[k],o)
             cd_ref[e*HEAD+h0:e*HEAD+h0+32,:]=o.reshape(32,TB).astype(bf16)
 
-def attn_fwd(cidx, act, wq, routesT, gatesT, qdoc, kaug, vt, kn, KB=256):
+def attn_fwd(act, wq, routesT, gatesT, qdoc, kaug, vt, KB=256):
     tok=act.shape[0]; experts=wq.shape[0]//HEAD; keys=kaug.shape[0]; n=tok//TB; vr=vt.shape[0]
     full=lambda a: pl.BlockSpec(a.shape,lambda i,*_:(0,)*a.ndim)
     return pl.pallas_call(
         functools.partial(attn_fwd_kernel,experts=experts,tok=tok,KB=KB),
-        grid_spec=pltpu.PrefetchScalarGridSpec(num_scalar_prefetch=1,grid=(n,),
+        grid_spec=pltpu.PrefetchScalarGridSpec(num_scalar_prefetch=0,grid=(n,),
           in_specs=[pl.BlockSpec((TB,D),lambda i,*_:(i,0)),full(wq),
             pl.BlockSpec((TOP,TB),lambda i,*_:(0,i)),pl.BlockSpec((TOP,TB),lambda i,*_:(0,i)),
-            pl.BlockSpec((8,TB),lambda i,*_:(0,i)),full(kaug),full(vt),pl.BlockSpec(memory_space=pltpu.SMEM)],
+            pl.BlockSpec((8,TB),lambda i,*_:(0,i)),full(kaug),full(vt)],
           out_specs=[pl.BlockSpec((experts*HEAD,TB),lambda i,*_:(0,i)),
             pl.BlockSpec((1,HEAD,W),lambda i,*_:(i,0,0)),
             pl.BlockSpec((1,HEAD,W),lambda i,*_:(i,0,0)),
             pl.BlockSpec((1,1,W),lambda i,*_:(i,0,0))],
           scratch_shapes=[pltpu.VMEM((experts*HEAD,TB),f32),pltpu.VMEM((128,W),bf16),
-            pltpu.VMEM((keys,W),f32),pltpu.VMEM((vr,W),f32)]),
+            pltpu.VMEM((keys,W),f32),pltpu.VMEM((vr,W),f32),pltpu.SMEM((1,),f32)]),
         out_shape=[jax.ShapeDtypeStruct((experts*HEAD,tok),bf16),
           jax.ShapeDtypeStruct((n,HEAD,W),bf16),jax.ShapeDtypeStruct((n,HEAD,W),bf16),
           jax.ShapeDtypeStruct((n,1,W),f32)],
         compiler_params=pltpu.CompilerParams(vmem_limit_bytes=60*2**20),
         name="attn_fwd",
-    )(cidx,act,wq,routesT,gatesT,qdoc,kaug,vt,kn)
+    )(act,wq,routesT,gatesT,qdoc,kaug,vt)
 
 
 def dot(a, b, dims=NN):
@@ -316,7 +321,7 @@
 def mega_kernel(sizes, nf, nb, nexp, fb,
                 cd, wo, tok, cot, g2, s2, up_ref, upb, down_ref, downb, q_ref, ctx_ref, lse_ref, routes_ref, gates_ref,
                 qdoc_ref, kaug_ref, vaug_ref, kt_ref, act1, wq, kvw, g1,
-                out, dx, fin_o, go_o, gq_o, sm_o,
+                out, dx, go_o, gq_o, gkv_o, sm_o, gd_o, gu_o,
                 mid, rstd, act, actT, dffn, dct, dqd, gub, gsm,
                 qaug, daug, rhs, pds, dq, dkv,
                 dsrc, fin, osrc, go, qsrc, gq, ksrc, kfin, ssrc, sfin, land, nland, ss, rs, lsem):
@@ -497,12 +502,13 @@
         for c in chains["q"]:
             c.step(0)
         tick("t", 1)
-        for k in range(1, kc.nsteps):
-            kc.step(k)
-        da = dot(dqd[...], wq[...], TN) + dot(kfin[...], kvw[...], NT)
+        dx[...] = dot(dqd[...], wq[...], TN)
         for c in chains["q"]:
             c.step(1)
         tick("t", 2)
+        for k in range(1, kc.nsteps):
+            kc.step(k)
+        da = dx[...] + dot(kfin[...], kvw[...].astype(bf16), NT)
         x = tok[...]
         cen = x - jnp.mean(x, axis=-1, keepdims=True)
         r1 = lax.rsqrt(jnp.mean(cen * cen, axis=-1, keepdims=True) + 1e-5)
@@ -524,15 +530,20 @@
             for c, n in late[k * len(late) // 6:(k + 1) * len(late) // 6]:
                 c.step(n)
             if k == 6:
-                moved = pltpu.make_async_copy(fin, fin_o, lsem.at[0])
-                moved.start()
-        qg = pltpu.make_async_copy(gq, gq_o, lsem.at[2])
-        qg.start()
-        og = pltpu.make_async_copy(go, go_o, lsem.at[1])
-        og.start()
-        sg = pltpu.make_async_copy(sfin, sm_o, lsem.at[3])
-        sg.start()
-        for c in (moved, og, qg, sg):
+                moved = []
+                for j in range(nf):
+                    r0 = j * part
+                    moved.append(pltpu.make_async_copy(
+                        fin.at[r0:r0 + fb, :], gd_o.at[j * fb:(j + 1) * fb, :], lsem.at[2 * j]))
+                    moved.append(pltpu.make_async_copy(
+                        fin.at[r0 + fb:r0 + part, :], gu_o.at[:, j * fb:(j + 1) * fb], lsem.at[2 * j + 1]))
+                for c in moved:
+                    c.start()
+        go_o[...] = go[...].astype(f32)
+        gq_o[...] = gq[...].astype(f32)
+        gkv_o[...] = sfin[0:D, :].astype(f32)
+        sm_o[...] = sfin[D:SMALL, :].astype(f32)
+        for c in moved:
             c.wait()
 
 
@@ -563,9 +574,9 @@
                   pl.BlockSpec((D, fb), lambda s: (0, fj(s))), pl.BlockSpec((1, fb), lambda s: (0, fj(s))),
                   pl.BlockSpec((fb, D), lambda s: (fj(s), 0)), full(downb), b3(q), b3(ctx), b3(lse),
                   blk(TOP), blk(TOP), blk(8), full(kaug), full(vaug), full(kt), full(act1), full(wq), full(kvw), full(g1)],
-        out_specs=[fo(ntok, D), fo(ntok, D), any_, any_, any_, any_],
-        out_shape=[sd((ntok, D), f32), sd((ntok, D), f32), sd((nf * part, D), bf16), sd((nexp * HEAD, D), bf16),
-                   sd((nexp * HEAD, D), bf16), sd((SMALL, 128), bf16)],
+        out_specs=[fo(ntok, D), fo(ntok, D), fo(nexp * HEAD, D), fo(nexp * HEAD, D), fo(D, 128), fo(SMALL - D, 128), any_, any_],
+        out_shape=[sd((ntok, D), f32), sd((ntok, D), f32), sd((nexp * HEAD, D), f32), sd((nexp * HEAD, D), f32),
+                   sd((D, 128), f32), sd((SMALL - D, 128), f32), sd((ff, D), bf16), sd((D, ff), bf16)],
         scratch_shapes=[
             v((ntok, D), f32), v((ntok, 128), f32), v((ntok, D), bf16), v((D, ntok), bf16),
             v((ntok, D), bf16), v((eh, ntok), bf16), v((eh, ntok), bf16), v((nf, fb), f32), v((3, D), f32),
@@ -574,67 +585,187 @@
             v((nf * part, D), bf16), v((nf * part, D), bf16), v((eh, D), bf16), v((nexp * HEAD, D), bf16),
             v((eh, D), bf16), v((nexp * HEAD, D), bf16), v((keys, 128), bf16), v((ntok, 128), bf16),
             v((SMALL, 128), bf16), v((SMALL, 128), bf16), v((land, D), bf16), v((nland, 128), bf16),
-            pltpu.SemaphoreType.DMA((nsem,)), pltpu.SemaphoreType.DMA((nsem,)), pltpu.SemaphoreType.DMA((4,))],
+            pltpu.SemaphoreType.DMA((nsem,)), pltpu.SemaphoreType.DMA((nsem,)), pltpu.SemaphoreType.DMA((2 * nf,))],
         compiler_params=pltpu.CompilerParams(collective_id=0, has_side_effects=True, vmem_limit_bytes=62 * 2**20),
         name="mega",
     )(cd, wo, tok, cot, g2, s2, up, upb, down, downb, q, ctx, lse, routes, gates, qdoc, kaug, vaug, kt, act1, wq, kvw, g1)
 
 
+def gather_stages(sizes, here, shard):
+    e = lax.axis_index("exp")
+    if (sizes["dp"], sizes["ctx"], sizes["exp"]) != (2, 2, 8) or shard % 64:
+        stages = []
+        for i, bit in enumerate(mesh_bits(sizes)["exp"]):
+            stages.append([((e >> i << i) * shard, shard << i, bit)])
+        return stages, []
+    core, zl, zh, x, y = ("exp", 1), ("exp", 2), ("exp", 4), ("dp", 1), ("ctx", 1)
+    quarter = shard // 4
+    flip = lambda bit, n=1: n * (1 - 2 * here.bit[bit])
+    at = lambda dz: e + (dz & 1) * flip(zl, 2) + (dz >> 1) * flip(zh, 4)
+    q = here.bit[x] * 2 + here.bit[y]
+    row = lambda dz, dq: at(dz) * shard + (q + (dq & 1) * flip(y) + (dq >> 1) * flip(x, 2)) * quarter
+    gx = lambda dq: [(row(1, dq), quarter), (row(3, dq), 16)]
+    gy = lambda dq: [(row(2, dq), quarter), (row(3, dq) + 16, quarter - 16)]
+    stages = [
+        [(row(0, 0), quarter, zh)],
+        [(row(0, 0), quarter, zl), (row(2, 0), quarter, zl)],
+        [m + (x,) for m in gx(0)] + [m + (y,) for m in gy(0)],
+        [m + (y,) for m in gx(0) + gx(2)] + [m + (x,) for m in gy(0) + gy(1)],
+        [(at(d) * shard, shard, core) for d in (1, 2, 3)],
+    ]
+    return stages, [(e * shard, shard, core)]
+
+
+def head_kernel(sizes, nexp, nsem, tok, g1, s1, kvw, wq3, wo3, lens, up_h, down_h,
+                act, kaug, vaug, kt, vt, qdoc, wq_o, wo_o, up_o, down_o,
+                wqs, wos, kv, upf, downf, upb, downb, ss, rs, ls):
+    here = Here(sizes)
+    ntok, keys, shard = tok.shape[0], kv.shape[0], nexp * HEAD
+    fetch = [pltpu.make_async_copy(up_h, upf, ls.at[0]), pltpu.make_async_copy(down_h, downf, ls.at[1])]
+    for c in fetch:
+        c.start()
+    mine = lax.axis_index("exp") * shard
+    for j in range(nexp):
+        r = pl.ds(pl.multiple_of(mine + j * HEAD, HEAD), HEAD)
+        wqs[r, :] = wq3[j].astype(bf16)
+        wos[r, :] = wo3[j].astype(bf16)
+    greet(here)
+    count = [0]
+
+    def send(buf, moves):
+        out = []
+        for start, n, bit in moves:
+            r = rows(buf, start, n)
+            k = count[0]
+            count[0] += 1
+            c = pltpu.make_async_remote_copy(src_ref=r, dst_ref=r, send_sem=ss.at[k], recv_sem=rs.at[k],
+                                             device_id=here.dev[bit], device_id_type=MESH)
+            c.start()
+            out.append(c)
+        return out
+
+    def wait(copies):
+        for c in copies:
+            c.wait()
+
+    stages, early = gather_stages(sizes, here, shard)
+    work = []
+
+    def run(k):
+        for buf, lag in ((wqs, 0), (wos, 0)):
+            i = k - lag
+            if 0 < i <= len(stages):
+                wait(flying[buf is wos])
+            if 0 <= i < len(stages):
+                flying[buf is wos] = send(buf, stages[i])
+
+    flying = [[], []]
+    run(0)
+    own = send(wqs, early) + send(wos, early)
+    x = tok[...]
+    cen = x - jnp.mean(x, axis=-1, keepdims=True)
+    a = (cen * lax.rsqrt(jnp.mean(cen * cen, axis=-1, keepdims=True) + 1e-5) * g1[...] + s1[...]).astype(bf16)
+    act[...] = a
+    ctx = lax.axis_index("ctx")
+    kv[pl.ds(pl.multiple_of(ctx * ntok, ntok), ntok), :] = dot(a, kvw[...].astype(bf16)).astype(bf16)
+    cbits = mesh_bits(sizes)["ctx"]
+    share = lambda i: send(kv, [((ctx >> i << i) * ntok, ntok << i, cbits[i])])
+    swap = share(0)
+    run(1)
+    put = []
+
+    def cast(k, src, dst, o):
+        fetch[k].wait()
+
+        @pl.loop(0, src.shape[0] // 64)
+        def _(t):
+            r = pl.ds(pl.multiple_of(t * 64, 64), 64)
+            dst[r, :] = src[r, :].astype(bf16)
+
+        c = pltpu.make_async_copy(dst, o, ls.at[2 + k])
+        c.start()
+        put.append(c)
+
+    def ends(pos):
+        d, end = jnp.zeros(pos.shape, jnp.int32), 0
+        for j in range(lens.shape[0] - 1):
+            end = end + lens[j]
+            d = d + (pos >= end).astype(jnp.int32)
+        return d
+
+    cast(0, upf, upb, up_o)
+    slot = lax.broadcasted_iota(jnp.int32, (8, ntok), 0)
+    qpos = ends(lax.broadcasted_iota(jnp.int32, (8, ntok), 1) + ctx * ntok)
+    qdoc[...] = jnp.where((qpos == slot) | (slot > 2), 0.0, NEG)
+    run(2)
+    wait(swap)
+    for i in range(1, len(cbits)):
+        wait(share(i))
+    cast(1, downf, downb, down_o)
+    run(3)
+    lane = lax.broadcasted_iota(jnp.int32, (keys, 128), 1)
+    doc = ends(lax.broadcasted_iota(jnp.int32, (keys, 128), 0))
+    full = kv[...].astype(f32)
+    extra = jnp.where((lane == doc + HEAD) | ((lane > HEAD + 2) & (lane < HEAD + 6)), 1.0, 0.0)
+    kaug[...] = jnp.where(lane < HEAD, full, extra).astype(bf16)
+    flipped = jnp.concatenate([full[:, HEAD:], full[:, :HEAD]], axis=1)
+    vaug[...] = jnp.where(lane < HEAD, flipped, jnp.where(lane < HEAD + 3, 1.0, 0.0)).astype(bf16)
+    both = jnp.transpose(full)
+    kt[...] = both[:HEAD].astype(bf16)
+    vt[...] = jnp.concatenate([both[HEAD:], jnp.ones((1, keys), f32), jnp.zeros((15, keys), f32)], 0).astype(bf16)
+    run(4)
+    for k in range(5, len(stages) + 1):
+        run(k)
+    wait(own)
+    for k, (src, o) in enumerate(((wqs, wq_o), (wos, wo_o))):
+        c = pltpu.make_async_copy(src, o, ls.at[4 + k])
+        c.start()
+        put.append(c)
+    for c in put:
+        c.wait()
+
+
+def head(sizes, nexp, tok, g1, s1, kvw, wq3, wo3, lens, up, down):
+    ntok, keys, experts = tok.shape[0], tok.shape[0] * sizes["ctx"], nexp * sizes["exp"]
+    vm, any_ = pl.BlockSpec(memory_space=pltpu.VMEM), pl.BlockSpec(memory_space=pl.ANY)
+    sd, v = jax.ShapeDtypeStruct, pltpu.VMEM
+    nsem = 64
+    wide = (experts * HEAD, D)
+    return pl.pallas_call(
+        functools.partial(head_kernel, sizes, nexp, nsem),
+        in_specs=[vm] * 6 + [pl.BlockSpec(memory_space=pltpu.SMEM), any_, any_],
+        out_specs=[vm] * 6 + [any_] * 4,
+        out_shape=[sd((ntok, D), bf16), sd((keys, 128), bf16), sd((keys, 128), bf16), sd((HEAD, keys), bf16),
+                   sd((HEAD + 16, keys), bf16), sd((8, ntok), f32), sd(wide, bf16), sd(wide, bf16),
+                   sd(up.shape, bf16), sd(down.shape, bf16)],
+        scratch_shapes=[v(wide, bf16), v(wide, bf16), v((keys, 128), bf16), v(up.shape, f32), v(down.shape, f32),
+                        v(up.shape, bf16), v(down.shape, bf16), pltpu.SemaphoreType.DMA((nsem,)),
+                        pltpu.SemaphoreType.DMA((nsem,)), pltpu.SemaphoreType.DMA((6,))],
+        compiler_params=pltpu.CompilerParams(collective_id=1, has_side_effects=True, vmem_limit_bytes=60 * 2**20),
+        name="head",
+    )(tok, g1, s1, kvw, wq3, wo3, lens, up, down)
+
+
 def local(sizes, tokens, lengths, routes, route_gates, cotangent, gain_one, shift_one, kv_weight,
           query_weight, out_weight, gain_two, shift_two, up_weight, up_bias, down_weight, down_bias):
     x = tokens[0]
-    tok = x.shape[0]
-    ncx = sizes["ctx"]
-    group = tok * ncx
     nexp = query_weight.shape[0]
-    experts = nexp * sizes["exp"]
-    cidx = lax.axis_index("ctx")
-    wq_own = jnp.swapaxes(query_weight, 1, 2).reshape(nexp * HEAD, D).astype(bf16)
-    wo_own = out_weight.reshape(nexp * HEAD, D).astype(bf16)
-    wq = lax.all_gather(wq_own, "exp", axis=0, tiled=True)
-    wo = lax.all_gather(wo_own, "exp", axis=0, tiled=True)
-    cen = x - jnp.mean(x, axis=-1, keepdims=True)
-    rs1 = lax.rsqrt(jnp.mean(cen * cen, axis=-1, keepdims=True) + 1e-5)
-    xh1 = cen * rs1
-    act = (xh1 * gain_one + shift_one).astype(bf16)
-    kvw = kv_weight.astype(bf16)
-    kv_own = dot(act, kvw).astype(bf16)
-    kv = lax.all_gather(kv_own, "ctx", axis=0, tiled=True)
-    keys, vals = kv[:, :HEAD], kv[:, HEAD:]
-    kn = jnp.max(jnp.sum(jnp.square(keys.astype(f32)), axis=1)).reshape(1)
-    pos = jnp.arange(group, dtype=jnp.int32)
-    docs, end = jnp.zeros_like(pos), 0
-    for d in range(lengths.shape[1] - 1):
-        end = end + lengths[0, d]
-        docs = docs + (pos >= end).astype(jnp.int32)
-    hot = (docs[:, None] == jnp.arange(3)[None, :]).astype(bf16)
-    one3 = jnp.ones((group, 3), bf16)
-    kaug = jnp.concatenate([keys, hot, one3, jnp.zeros((group, HEAD - 6), bf16)], axis=1)
-    vaug = jnp.concatenate([vals, one3, jnp.zeros((group, HEAD - 3), bf16)], axis=1)
-    kt = keys.T
-    vt = jnp.concatenate([vals.T, jnp.ones((1, group), bf16), jnp.zeros((15, group), bf16)], axis=0)
-    qdocs = lax.dynamic_slice_in_dim(docs, cidx * tok, tok)
-    slot = jnp.arange(8, dtype=jnp.int32)[:, None]
-    qdoc = jnp.where((qdocs[None, :] == slot) | (slot > 2), 0.0, NEG).astype(f32)
+    row = lambda v: v.reshape(1, -1)
+    act, kaug, vaug, kt, vt, qdoc, wq, wo, up, down = head(
+        sizes, nexp, x, row(gain_one), row(shift_one), kv_weight, jnp.swapaxes(query_weight, 1, 2), out_weight, lengths[0], up_weight,
+        down_weight)
     routes_t = routes[0].T
     gates_t = route_gates[0].T
-    cvec = cidx.reshape(1).astype(jnp.int32)
-
-    cd, q, ctx, lse = attn_fwd(cvec, act, wq, routes_t, gates_t, qdoc, kaug, vt, kn, KB=384)
-    row = lambda v: v.reshape(1, -1)
-    out, dx, dense, go, gq, small = mega(
-        sizes, nexp, cd, wo, x, cotangent[0], row(gain_two), row(shift_two), up_weight.astype(bf16),
-        row(up_bias), down_weight.astype(bf16), row(down_bias), q, ctx, lse, routes_t, gates_t, qdoc, kaug, vaug, kt, act, wq, kvw, row(gain_one))
-    go = go.astype(f32).reshape(nexp, HEAD, D)
-    gq = jnp.swapaxes(gq.astype(f32).reshape(nexp, HEAD, D), 1, 2)
-    dense = dense.reshape(-1, 2, D, D)
-    gdown = dense[:, 0].astype(f32).reshape(-1, D)
-    gup = dense[:, 1].astype(f32).transpose(1, 0, 2).reshape(D, -1)
-    small = small.astype(f32)
-    vec = small[D:].reshape(-1)
+    cd, q, ctx, lse = attn_fwd(act, wq, routes_t, gates_t, qdoc, kaug, vt, KB=384)
+    out, dx, go, gq, gkv, small, gdown, gup = mega(
+        sizes, nexp, cd, wo, x, cotangent[0], row(gain_two), row(shift_two), up, row(up_bias), down, row(down_bias), q,
+        ctx, lse, routes_t, gates_t, qdoc, kaug, vaug, kt, act, wq, kv_weight, row(gain_one))
+    go = go.reshape(nexp, HEAD, D)
+    gq = jnp.swapaxes(gq.reshape(nexp, HEAD, D), 1, 2)
+    vec = small.reshape(-1)
     v = lambda i: vec[i * D:(i + 1) * D]
-    return (out[None], dx[None], v(3), v(4), small[:D], gq, go, v(0), v(1), gup, vec[5 * D:5 * D + up_bias.shape[0]],
-            gdown, v(2))
+    return (out[None], dx[None], v(3), v(4), gkv, gq, go, v(0), v(1), gup.astype(f32),
+            vec[5 * D:5 * D + up_bias.shape[0]], gdown.astype(f32), v(2))
 
 
 def solution(mesh):

time: 199 us -> 179 us (0.90)
  Pallas kernels: 125 us -> 163 us
  other arithmetic: 22.1 us -> 6.89 us
  between operations: 15.5 us -> 0.68 us
  waiting for transfers between devices: 14.1 us -> 0 us
  blocking collectives: 8.53 us -> 0 us
  local copies, waits for them, and re-layouts: 12.5 us -> 8 us
    pallas_call x0 -> x1, Pallas kernels: none -> 33 us  [head(): pl.pallas_call(functools.partial(head_kernel, sizes, nexp, nsem), in_spec...]
    all_gather x2 -> x0, waiting for transfers between devices: 14.1 us -> none  [the longest x1 10.7 us: local(): wo = lax.all_gather(wo_own, 'exp', axis=0, tiled=True)]
    all_gather x1 -> x0, blocking collectives: 8.53 us -> none  [local(): kv = lax.all_gather(kv_own, 'ctx', axis=0, tiled=True)]
    convert_element_type x9 -> x2, other arithmetic: 13.1 us -> 6.89 us  [the longest x1 4.28 us: local(): gup.astype(f32)]
    pallas_call x1, Pallas kernels: 110 us -> 115 us  [mega(): pl.pallas_call(functools.partial(mega_kernel, sizes, nf, nb, nexp, fb), g...]
    slice x1 -> x0, other arithmetic: 2.93 us -> none  [local(): gdown = dense[:, 0].astype(f32).reshape(-1, D)]
    reshape x1 -> x0, local copies, waits for them, and re-layouts: 2.5 us -> none  [local(): gup = dense[:, 1].astype(f32).transpose(1, 0, 2).reshape(D, -1)]
    slice x2 -> x0, local copies, waits for them, and re-layouts: 2.25 us -> none  [the longest x1 1.66 us: local(): small[:D]]
  transfers between devices with their start and end apart: 2 -> 0, of which waited for: 2 -> 0; matrix products, arithmetic and copies ran while one was open for 8% -> 0% of each run, Pallas kernels for 8% -> 0%
where the time goes in v4:
time: 179 us
  Pallas kernels  163 us (91%)
  local copies, waits for them, and re-layouts  8 us (4%)
  other arithmetic  6.89 us (4%)
    pallas_call x1, Pallas kernels, mega(): pl.pallas_call(functools.partial(mega_kernel, sizes, nf, nb, nexp, fb), g...  115 us
    pallas_call x1, Pallas kernels, head(): pl.pallas_call(functools.partial(head_kernel, sizes, nexp, nsem), in_spec...  33 us
    pallas_call x1, Pallas kernels, attn_fwd(): pl.pallas_call(functools.partial(attn_fwd_kernel, experts=experts, tok=to...  15.1 us
    unnamed x17, local copies, waits for them, and re-layouts  5.33 us
    convert_element_type x1, other arithmetic, local(): gup.astype(f32)  4.28 us

profile of v4, /device:TPU:0, one launch (start us, length us, event | category | flops | bytes accessed | tf_op | source)
XLA Modules:
  0.0 178.7 jit_solution(13634560292981967711)
XLA Ops:
  0.6 33.0 %head.1 = (bf16[768,512]{1,0:T(8,128)(2,1)}, bf16[1536,128]{1,0:T(8,128)(2,1)}, bf16[1536,128]{1,0:T(8,128)(2,1)}, bf16[64,1536]{1,0:T(8,128)(2,1)}, bf16[80,153...) custom-call(f32[768,512]{1,0:T(8,128)} %bitcast.34, ...), custom_call_target="tpu_custom_call" | custom-call | tf_op jit(solution)/shard_map/head/pallas_call | solution.py:734
  33.6 15.1 %attn_fwd.1 = (bf16[1536,768]{1,0:T(8,128)(2,1)}, bf16[6,64,1024]{2,1,0:T(8,128)(2,1)}, bf16[6,64,1024]{2,1,0:T(8,128)(2,1)}, f32[6,1,1024]{2,1,0:T(1,128)}) custom-call(bf16[768,512]{1,0:T(8,128)(2,1)} %get-tuple-element.35.act_ref.act1, bf16[1536,512]{1,0:T(8,128)(2,1)} %get-tuple-element.36.wq_ref.wq, s32[8,768]{1,0:T(8,128)} %bitcast.42, ...), custom_call_target="tpu_custom_call" | custom-call | tf_op jit(solution)/shard_map/attn_fwd/pallas_call | solution.py:122
  48.7 115.1 %mega.1 = (f32[768,512]{1,0:T(8,128)}, f32[768,512]{1,0:T(8,128)}, f32[192,512]{1,0:T(8,128)}, f32[192,512]{1,0:T(8,128)}, f32[512,128]{1,0:T(8,128)}, /*index=5...) custom-call(bf16[1536,768]{1,0:T(8,128)(2,1)} %get-tuple-element.40.cd, ...), custom_call_target="tpu_custom_call" | custom-call | tf_op jit(solution)/shard_map/mega/pallas_call | solution.py:570
  163.8 1.3 slice_bitcast_fusion
  165.1 1.4 slice_bitcast_fusion.1
  166.5 0.0 copy-start
  166.5 4.3 %convert_element_type.6 = f32[512,2048]{1,0:T(8,128)} convert(bf16[512,2048]{1,0:T(8,128)(2,1)} %get-tuple-element.55) | non-fusion elementwise | flops 1048576 | bytes 6291456 | tf_op jit(solution)/shard_map/convert_element_type | solution.py:767
  170.8 0.0 copy-done
  170.8 0.0 copy-start.2
  170.8 2.6 %convert_element_type.7 = f32[2048,512]{1,0:T(8,128)} convert(bf16[2048,512]{1,0:T(8,128)(2,1)S(1)} %copy-done) | non-fusion elementwise | flops 1048576 | bytes 6291456 | tf_op jit(solution)/shard_map/convert_element_type | solution.py:768
  173.4 0.0 copy-done.2
  173.4 0.0 copy-start.1
  173.4 1.1 copy.34
  174.5 0.8 copy-done.1
  175.4 0.0 copy-start.5
  175.4 0.0 copy-start.4
  175.4 0.0 copy-start.3
  175.4 1.1 copy.35
  176.5 0.0 copy-done.5
  176.5 0.7 copy.36
  177.2 0.0 copy-done.4
  177.2 0.7 copy.37
  178.0 0.0 copy-done.3
  178.0 0.7 copy.38
Async XLA Ops:
  166.5 4.3 %copy-start = (bf16[2048,512]{1,0:T(8,128)(2,1)S(1)}, bf16[2048,512]{1,0:T(8,128)(2,1)}, u32[]{:S(2)}) copy-start(bf16[2048,512]{1,0:T(8,128)(2,1)} %get-tuple-element.56) | copy-start | bytes 6291460
  170.8 2.6 %copy-start.2 = (f32[768,512]{1,0:T(8,128)S(1)}, f32[768,512]{1,0:T(8,128)}, u32[]{:S(2)}) copy-start(f32[768,512]{1,0:T(8,128)} %get-tuple-element.49) | copy-start | bytes 4718596
  173.4 2.0 %copy-start.1 = (f32[768,512]{1,0:T(8,128)S(1)}, f32[768,512]{1,0:T(8,128)}, u32[]{:S(2)}) copy-start(f32[768,512]{1,0:T(8,128)} %get-tuple-element.50) | copy-start | bytes 4718596
  175.4 1.2 copy-start.5
  175.4 1.9 %copy-start.4 = (f32[192,512]{1,0:T(8,128)S(1)}, f32[192,512]{1,0:T(8,128)}, u32[]{:S(2)}) copy-start(f32[192,512]{1,0:T(8,128)} %get-tuple-element.53) | copy-start | bytes 1179652
  175.4 2.6 %copy-start.3 = (f32[192,512]{1,0:T(8,128)S(1)}, f32[192,512]{1,0:T(8,128)}, u32[]{:S(2)}) copy-start(f32[192,512]{1,0:T(8,128)} %get-tuple-element.54) | copy-start | bytes 1179652

commit v5 on v4

--- a/solution.py
+++ b/solution.py
@@ -20,7 +20,7 @@
 LN2 = math.log(2.0)
 SMALL = 576
 KBB = 384
-STRIDE = 8
+STRIDE = 7
 JOIN = 2
 SAFE = 50.0
 NN = (((1,), (0,)), ((), ()))
@@ -152,34 +152,51 @@
 
 class Here:
     def __init__(self, sizes):
-        at = {a: lax.axis_index(a) for a in AXES}
-        self.bit, self.dev = {}, {}
-        for bits in mesh_bits(sizes).values():
+        self.at = {a: lax.axis_index(a) for a in AXES}
+        self.bit = {(ax, m): lax.rem(self.at[ax] // m, 2) for bits in mesh_bits(sizes).values() for ax, m in bits}
+        self.known = {}
+
+    def across(self, bits):
+        bits = tuple(sorted(bits))
+        if bits not in self.known:
+            at = dict(self.at)
             for ax, m in bits:
-                b = lax.rem(at[ax] // m, 2)
-                self.bit[ax, m] = b
-                self.dev[ax, m] = tuple(at[a] + m - 2 * m * b if a == ax else at[a] for a in AXES)
+                at[ax] = at[ax] + m - 2 * m * self.bit[ax, m]
+            self.known[bits] = tuple(at[a] for a in AXES)
+        return self.known[bits]
+
+
+def subsets(group):
+    return [[b for i, b in enumerate(group) if d >> i & 1] for d in range(1, 1 << len(group))]
 
 
 def mesh_bits(sizes):
     return {a: [(a, 1 << i) for i in range(sizes[a].bit_length() - 1)] for a in AXES}
+
+
+def small_mesh(sizes):
+    return sizes["dp"] == sizes["ctx"] == 2 and sizes["exp"] == 8
 
 
 def chain_orders(sizes):
     b = mesh_bits(sizes)
     e, d, c = b["exp"], b["dp"], b["ctx"]
-    late = e + d + c
-    if len(d) + len(c) > 2:
-        return [late, late, late]
-    return [e[:1] + d + c + e[1:], e[:1] + c + d + e[1:], late]
+    one = lambda bits: [(x,) for x in bits]
+    late = one(e + d + c)
+    if not small_mesh(sizes):
+        return [late] * 3, late
+    dense = [one(e[:1] + d + c + e[1:]), one(e[:1] + c + d + e[1:]), late]
+    fast = [tuple(e[:1]), tuple(d + c), tuple(e[1:])]
+    return dense, fast
 
 
 def chain_plan(n, order):
     plan = []
-    for bit in order:
-        halve = n % 32 == 0
-        n = n // 2 if halve else n
-        plan.append((halve, bit, n))
+    for group in order:
+        ways = 1 << len(group)
+        halve = n % (16 * ways) == 0
+        n = n // ways if halve else n
+        plan.append((halve, group, n))
     return plan
 
 
@@ -187,18 +204,19 @@
     return ref.at[pl.ds(pl.multiple_of(start, 16), n), :]
 
 
-def add_rows(dst, d0, a, a0, b, b0, n):
+def add_rows(dst, d0, parts, n):
     ch = math.gcd(n, 64)
 
     @pl.loop(0, n // ch)
     def _(t):
         o = pl.multiple_of(t * ch, ch)
-        g = lambda r, s: r[pl.ds(pl.multiple_of(s + o, 16), ch), :]
-        dst[pl.ds(pl.multiple_of(d0 + o, 16), ch), :] = g(a, a0) + g(b, b0)
+        g = [r[pl.ds(pl.multiple_of(s + o, 16), ch), :] for r, s in parts]
+        total = g[0] + g[1] if len(g) == 2 else functools.reduce(jnp.add, [v.astype(f32) for v in g]).astype(bf16)
+        dst[pl.ds(pl.multiple_of(d0 + o, 16), ch), :] = total
 
 
 def block_places(n, order, owner):
-    bits = [bit for halve, bit, _ in chain_plan(n, order) if halve]
+    bits = [bit for halve, group, _ in chain_plan(n, order) if halve for bit in group]
     own = sorted([b for b in bits if b[0] == owner], reverse=True)
     nat = own + sorted([b for b in bits if b[0] != owner])
     places = []
@@ -213,74 +231,91 @@
         self.work, self.final, self.base, self.n, self.order = work, final, base, n, order
         self.owner, self.fbase = owner, fbase
         self.plan = chain_plan(n, order)
-        self.landed = sum(m for _, _, m in self.plan)
-        self.back = [i for i in reversed(range(len(order))) if self.plan[i][0] and order[i][0] != owner]
+        self.landed = sum(m * ((1 << len(g)) - 1) for _, g, m in self.plan)
+        self.back = [i for i in reversed(range(len(order))) if self.plan[i][0] and order[i][0][0] != owner]
         if owner:
             self.back.sort(key=lambda i: order[i], reverse=True)
         self.m = len(self.plan)
-        self.nsem = self.m + len(self.back)
-        self.nsteps = self.nsem + 1
+        self.groups = [g for _, g, _ in self.plan] + [order[i] for i in self.back]
+        self.nsem = sum((1 << len(g)) - 1 for g in self.groups)
+        self.nsteps = len(self.groups) + 1
 
     def place(self, here, land, lbase, ss, rs, sem):
-        self.here, self.land, self.ss, self.rs, self.sem = here, land, ss, rs, sem
-        self.lb = []
-        for _, _, m in self.plan:
+        self.here, self.land, self.ss, self.rs = here, land, ss, rs
+        self.lb, self.sem = [], []
+        for _, g, m in self.plan:
             self.lb.append(lbase)
-            lbase += m
-        self.offs = self.offsets()
-
-    def offsets(self):
-        offs, off = [], self.base
-        for halve, bit, m in self.plan:
-            b = self.here.bit[bit]
-            offs.append((off + b * m, off + (1 - b) * m) if halve else (off, off))
-            off = offs[-1][0]
-        return offs
+            lbase += m * ((1 << len(g)) - 1)
+        for g in self.groups:
+            for f in subsets(g):
+                here.across(f)
+            self.sem.append(sem)
+            sem += (1 << len(g)) - 1
+        self.offs, off = [], self.base
+        for halve, g, m in self.plan:
+            self.offs.append(off)
+            if halve:
+                off = off + self.index(g, []) * m
+        self.last = off
+
+    def index(self, group, flipped):
+        v = 0
+        for b in group:
+            w = self.here.bit[b]
+            v = 2 * v + (1 - w if b in flipped else w)
+        return v
 
     def final_range(self, j):
         m = self.plan[-1][2]
         if self.owner is None:
-            offs = self.offs
             if j == 0:
-                return offs[-1][0], m
-            i = self.back[j]
-            return offs[i][0], self.plan[i][2]
-        off, w = self.fbase, m
-        for k, i in enumerate(self.back):
-            if k >= j:
-                off = off + self.here.bit[self.order[i]] * w
-            w *= 2
-        return off, m << j
-
-    def copy(self, k):
-        if k < self.m:
-            _, bit, n = self.plan[k]
-            src, dst = rows(self.work, self.offs[k][1], n), rows(self.land, self.lb[k], n)
-        else:
-            bit = self.order[self.back[k - self.m]]
-            src = dst = rows(self.final, *self.final_range(k - self.m))
-        return pltpu.make_async_remote_copy(
-            src_ref=src, dst_ref=dst, send_sem=self.ss.at[self.sem + k], recv_sem=self.rs.at[self.sem + k],
-            device_id=self.here.dev[bit], device_id_type=MESH)
+                return self.last, m
+            i = self.back[j - 1]
+            return self.offs[i], self.plan[i][2] << len(self.order[i])
+        rest = sorted(b for i in self.back for b in self.order[i])
+        done = [b for i in self.back[:j] for b in self.order[i]]
+        off = self.fbase
+        for k, b in enumerate(rest):
+            if b not in done:
+                off = off + self.here.bit[b] * (m << (len(rest) - 1 - k))
+        return off, m << len(done)
+
+    def copies(self, k):
+        out, g = [], self.groups[k]
+        for d, flipped in enumerate(subsets(g)):
+            if k < self.m:
+                halve, _, n = self.plan[k]
+                start = self.offs[k] + self.index(g, flipped) * n if halve else self.offs[k]
+                src, dst = rows(self.work, start, n), rows(self.land, self.lb[k] + d * n, n)
+            else:
+                src = dst = rows(self.final, *self.final_range(k - self.m))
+            out.append(pltpu.make_async_remote_copy(
+                src_ref=src, dst_ref=dst, send_sem=self.ss.at[self.sem[k] + d], recv_sem=self.rs.at[self.sem[k] + d],
+                device_id=self.here.across(flipped), device_id_type=MESH))
+        return out
 
     def step(self, k):
         if k:
-            self.copy(k - 1).wait()
+            for c in self.copies(k - 1):
+                c.wait()
             if k <= self.m:
                 i = k - 1
+                halve, g, n = self.plan[i]
                 last = i == self.m - 1
-                d = self.offs[i][0]
-                add_rows(self.final if last else self.work, self.final_range(0)[0] if last else d,
-                         self.work, d, self.land, self.lb[i], self.plan[i][2])
-        if k < self.nsem:
-            self.copy(k).start()
-
-
-def greet(here):
+                d = self.offs[i] + self.index(g, []) * n if halve else self.offs[i]
+                parts = [(self.work, d)] + [(self.land, self.lb[i] + j * n) for j in range((1 << len(g)) - 1)]
+                add_rows(self.final if last else self.work, self.final_range(0)[0] if last else d, parts, n)
+        if k < len(self.groups):
+            for c in self.copies(k):
+                c.start()
+
+
+def greet(here, groups):
+    devices = {tuple(sorted(f)) for g in groups for f in subsets(g)}
     bar = pltpu.get_barrier_semaphore()
-    for dev in here.dev.values():
-        pl.semaphore_signal(bar, inc=1, device_id=dev, device_id_type=MESH)
-    pl.semaphore_wait(bar, len(here.dev))
+    for f in sorted(devices):
+        pl.semaphore_signal(bar, inc=1, device_id=here.across(f), device_id_type=MESH)
+    pl.semaphore_wait(bar, len(devices))
 
 
 def dense_parts(n, orders):
@@ -289,9 +324,9 @@
 
 
 def make_chains(sizes, steps, part, nexp, keys, dsrc, fin, osrc, go, qsrc, gq, ksrc, kfin, ssrc, sfin):
-    orders = chain_orders(sizes)
+    orders, small = chain_orders(sizes)
     n = sizes["exp"] * HEAD
-    kbits = mesh_bits(sizes)["ctx"][::-1]
+    kbits = [(b,) for b in mesh_bits(sizes)["ctx"][::-1]]
     part = part * JOIN
     dense = [[Chain(dsrc, fin, j * part + b, m, o) for b, m, o in dense_parts(part, orders)] for j in range(steps // JOIN)]
     return dict(
@@ -299,13 +334,14 @@
         o=[Chain(osrc, go, j * n, n, orders[j % 3], "exp", j * HEAD) for j in range(nexp)],
         q=[Chain(qsrc, gq, j * n, n, orders[j % 3], "exp", j * HEAD) for j in range(nexp)],
         k=[Chain(ksrc, kfin, 0, keys, kbits, "ctx", 0)],
-        s=[Chain(ssrc, sfin, 0, SMALL, orders[0])],
+        g=[Chain(ssrc, sfin, 0, D, small)],
+        s=[Chain(ssrc, sfin, D, SMALL - D, small)],
     )
 
 
 def flat(chains):
     wide = [c for g in chains["dense"] for c in g] + chains["o"] + chains["q"]
-    return wide, chains["k"] + chains["s"]
+    return wide, chains["k"] + chains["g"] + chains["s"]
 
 
 def place_all(here, chains, land, nland, ss, rs):
@@ -381,7 +417,7 @@
         dffn[...] = cot[...].astype(bf16)
         out[...] = m + downb[...]
         dx[...] = jnp.zeros_like(dx)
-        greet(here)
+        greet(here, [g for group in flat(chains) for c in group for g in c.groups])
 
     @pl.when(s < nf)
     def _():
@@ -493,7 +529,7 @@
     def _():
         lane = lax.broadcasted_iota(jnp.int32, (1, 128), 1)
         ksrc[...] = (dkv[...] * jnp.where(lane < HEAD, LN2, 1.0)).astype(bf16)
-        kc, sc = chains["k"][0], chains["s"][0]
+        kc, gc, sc = chains["k"][0], chains["g"][0], chains["s"][0]
         kc.step(0)
         tick("t", 0)
         w = nexp * HEAD
@@ -501,35 +537,42 @@
             put_owner(qsrc, dot(dqd[e * w:(e + 1) * w, :], act1[...]).astype(bf16), e, chains["q"])
         for c in chains["q"]:
             c.step(0)
+        for k in range(1, kc.nsteps):
+            kc.step(k)
+        ssrc[0:D, :] = dot(act1[...], kfin[...], TN).astype(bf16)
+        gc.step(0)
         tick("t", 1)
-        dx[...] = dot(dqd[...], wq[...], TN)
         for c in chains["q"]:
             c.step(1)
+        da = dot(dqd[...], wq[...], TN) + dot(kfin[...], kvw[...].astype(bf16), NT)
+        gc.step(1)
         tick("t", 2)
-        for k in range(1, kc.nsteps):
-            kc.step(k)
-        da = dx[...] + dot(kfin[...], kvw[...].astype(bf16), NT)
         x = tok[...]
         cen = x - jnp.mean(x, axis=-1, keepdims=True)
         r1 = lax.rsqrt(jnp.mean(cen * cen, axis=-1, keepdims=True) + 1e-5)
         xh = cen * r1
         gg1, gs1 = jnp.sum(da * xh, axis=0, keepdims=True), jnp.sum(da, axis=0, keepdims=True)
-        gx = da * g1[...]
-        dx[...] = mid[...] + r1 * (gx - jnp.mean(gx, axis=-1, keepdims=True)
-                                   - xh * jnp.mean(gx * xh, axis=-1, keepdims=True))
-        ssrc[0:D, :] = dot(act1[...], kfin[...], TN).astype(bf16)
         vecs = [gsm[0:1, :], gsm[1:2, :], gsm[2:3, :], gg1, gs1] + [gub[j:j + 1, :] for j in range(nf)]
         vecs = [v[:, o:o + 128] for v in vecs for o in range(0, v.shape[1], 128)]
         vecs.append(jnp.zeros((SMALL - D - len(vecs), 128), f32))
         ssrc[D:SMALL, :] = jnp.concatenate(vecs, 0).astype(bf16)
+        sc.step(0)
+        for c in chains["q"]:
+            c.step(2)
+        gc.step(2)
+        gx = da * g1[...]
+        dx[...] = mid[...] + r1 * (gx - jnp.mean(gx, axis=-1, keepdims=True)
+                                   - xh * jnp.mean(gx * xh, axis=-1, keepdims=True))
         tick("t", 3)
-        tail = [[(c, k + 2) for c in chains["q"] if k + 2 < c.nsteps] + ([(sc, k)] if k < sc.nsteps else []) for k in range(20)]
-        for k in range(20):
-            for c, n in tail[k]:
+        rounds = max(c.nsteps for c in (gc, sc, *chains["q"]))
+        for k in range(1, rounds):
+            for c, lag in [(c, 2) for c in chains["q"]] + [(gc, 2), (sc, 0)]:
+                if k + lag < c.nsteps:
+                    c.step(k + lag)
+            share = -(-len(late) // 3)
+            for c, n in late[(k - 1) * share:k * share]:
                 c.step(n)
-            for c, n in late[k * len(late) // 6:(k + 1) * len(late) // 6]:
-                c.step(n)
-            if k == 6:
+            if k == 3:
                 moved = []
                 for j in range(nf):
                     r0 = j * part
@@ -593,27 +636,22 @@
 
 def gather_stages(sizes, here, shard):
     e = lax.axis_index("exp")
-    if (sizes["dp"], sizes["ctx"], sizes["exp"]) != (2, 2, 8) or shard % 64:
+    if not small_mesh(sizes) or shard % 64:
         stages = []
         for i, bit in enumerate(mesh_bits(sizes)["exp"]):
-            stages.append([((e >> i << i) * shard, shard << i, bit)])
+            stages.append([((e >> i << i) * shard, shard << i, [bit])])
         return stages, []
     core, zl, zh, x, y = ("exp", 1), ("exp", 2), ("exp", 4), ("dp", 1), ("ctx", 1)
     quarter = shard // 4
-    flip = lambda bit, n=1: n * (1 - 2 * here.bit[bit])
+    flip = lambda bit, n: n * (1 - 2 * here.bit[bit])
     at = lambda dz: e + (dz & 1) * flip(zl, 2) + (dz >> 1) * flip(zh, 4)
-    q = here.bit[x] * 2 + here.bit[y]
-    row = lambda dz, dq: at(dz) * shard + (q + (dq & 1) * flip(y) + (dq >> 1) * flip(x, 2)) * quarter
-    gx = lambda dq: [(row(1, dq), quarter), (row(3, dq), 16)]
-    gy = lambda dq: [(row(2, dq), quarter), (row(3, dq) + 16, quarter - 16)]
+    row = lambda dz: at(dz) * shard + (here.bit[x] * 2 + here.bit[y]) * quarter
     stages = [
-        [(row(0, 0), quarter, zh)],
-        [(row(0, 0), quarter, zl), (row(2, 0), quarter, zl)],
-        [m + (x,) for m in gx(0)] + [m + (y,) for m in gy(0)],
-        [m + (y,) for m in gx(0) + gx(2)] + [m + (x,) for m in gy(0) + gy(1)],
-        [(at(d) * shard, shard, core) for d in (1, 2, 3)],
+        [(row(0), quarter, f) for f in subsets((zl, zh))],
+        [(row(d), quarter, f) for d in (1, 2, 3) for f in subsets((x, y))],
+        [(at(d) * shard, shard, [core]) for d in (1, 2, 3)],
     ]
-    return stages, [(e * shard, shard, core)]
+    return stages, [(e * shard, shard, [core])]
 
 
 def head_kernel(sizes, nexp, nsem, tok, g1, s1, kvw, wq3, wo3, lens, up_h, down_h,
@@ -629,17 +667,19 @@
         r = pl.ds(pl.multiple_of(mine + j * HEAD, HEAD), HEAD)
         wqs[r, :] = wq3[j].astype(bf16)
         wos[r, :] = wo3[j].astype(bf16)
-    greet(here)
+    b = mesh_bits(sizes)
+    exact = [tuple(b["exp"][1:]), tuple(b["dp"] + b["ctx"])] if small_mesh(sizes) else []
+    greet(here, [(x,) for a in AXES for x in b[a]] + exact)
     count = [0]
 
     def send(buf, moves):
         out = []
-        for start, n, bit in moves:
+        for start, n, bits in moves:
             r = rows(buf, start, n)
             k = count[0]
             count[0] += 1
             c = pltpu.make_async_remote_copy(src_ref=r, dst_ref=r, send_sem=ss.at[k], recv_sem=rs.at[k],
-                                             device_id=here.dev[bit], device_id_type=MESH)
+                                             device_id=here.across(bits), device_id_type=MESH)
             c.start()
             out.append(c)
         return out
@@ -652,7 +692,7 @@
     work = []
 
     def run(k):
-        for buf, lag in ((wqs, 0), (wos, 0)):
+        for buf, lag in ((wqs, 0), (wos, 1)):
             i = k - lag
             if 0 < i <= len(stages):
                 wait(flying[buf is wos])
@@ -669,7 +709,7 @@
     ctx = lax.axis_index("ctx")
     kv[pl.ds(pl.multiple_of(ctx * ntok, ntok), ntok), :] = dot(a, kvw[...].astype(bf16)).astype(bf16)
     cbits = mesh_bits(sizes)["ctx"]
-    share = lambda i: send(kv, [((ctx >> i << i) * ntok, ntok << i, cbits[i])])
+    share = lambda i: send(kv, [((ctx >> i << i) * ntok, ntok << i, [cbits[i]])])
     swap = share(0)
     run(1)
     put = []
@@ -714,7 +754,7 @@
     kt[...] = both[:HEAD].astype(bf16)
     vt[...] = jnp.concatenate([both[HEAD:], jnp.ones((1, keys), f32), jnp.zeros((15, keys), f32)], 0).astype(bf16)
     run(4)
-    for k in range(5, len(stages) + 1):
+    for k in range(5, len(stages) + 2):
         run(k)
     wait(own)
     for k, (src, o) in enumerate(((wqs, wq_o), (wos, wo_o))):
@@ -746,6 +786,54 @@
     )(tok, g1, s1, kvw, wq3, wo3, lens, up, down)
 
 
+def finish_kernel(nc, sm, gd, gu, *refs):
+    moves, wide_o, moved, vec_o = refs[:5], refs[5:7], refs[7:12], refs[12:18]
+    lows, wides, vias, si, so = refs[18:20], refs[20:22], refs[22:27], refs[27], refs[28]
+    ins, outs, parts = [], [], []
+    for i, src in enumerate((gd, gu)):
+        n = src.shape[0] // nc
+        for j in range(nc):
+            r = slice(j * n, (j + 1) * n)
+            ins.append(pltpu.make_async_copy(src.at[r, :], lows[i].at[r, :], si.at[i * nc + j]))
+            outs.append(pltpu.make_async_copy(wides[i].at[r, :], wide_o[i].at[r, :], so.at[i * nc + j]))
+            parts.append((i, r))
+    for k, (a, via, b) in enumerate(zip(moves, vias, moved)):
+        ins.append(pltpu.make_async_copy(a, via, si.at[2 * nc + k]))
+        outs.append(pltpu.make_async_copy(via, b, so.at[2 * nc + k]))
+        parts.append(None)
+    for c in ins:
+        c.start()
+    at = 0
+    for o in vec_o:
+        n = o.shape[1] // 128
+        o[...] = jnp.concatenate([sm[j:j + 1, :] for j in range(at, at + n)], 1)
+        at += n
+    for k, part in enumerate(parts):
+        ins[k].wait()
+        if part:
+            i, r = part
+            wides[i][r, :] = lows[i][r, :].astype(f32)
+        outs[k].start()
+    for c in outs:
+        c.wait()
+
+
+def finish(sm, gd, gu, others, nub, nc=4):
+    any_, vm = pl.BlockSpec(memory_space=pl.ANY), pl.BlockSpec(memory_space=pltpu.VMEM)
+    sd, v = jax.ShapeDtypeStruct, pltpu.VMEM
+    sem = pltpu.SemaphoreType.DMA
+    return pl.pallas_call(
+        functools.partial(finish_kernel, nc),
+        in_specs=[vm] + [any_] * 7, out_specs=[any_] * 7 + [vm] * 6,
+        out_shape=[sd(gd.shape, f32), sd(gu.shape, f32)] + [sd(o.shape, o.dtype) for o in others]
+        + [sd((1, D), f32)] * 5 + [sd((1, nub), f32)],
+        scratch_shapes=[v(gd.shape, bf16), v(gu.shape, bf16), v(gd.shape, f32), v(gu.shape, f32)]
+        + [v(o.shape, o.dtype) for o in others] + [sem((2 * nc + 5,)), sem((2 * nc + 5,))],
+        compiler_params=pltpu.CompilerParams(vmem_limit_bytes=62 * 2**20),
+        name="post",
+    )(sm, gd, gu, *others)
+
+
 def local(sizes, tokens, lengths, routes, route_gates, cotangent, gain_one, shift_one, kv_weight,
           query_weight, out_weight, gain_two, shift_two, up_weight, up_bias, down_weight, down_bias):
     x = tokens[0]
@@ -760,12 +848,11 @@
     out, dx, go, gq, gkv, small, gdown, gup = mega(
         sizes, nexp, cd, wo, x, cotangent[0], row(gain_two), row(shift_two), up, row(up_bias), down, row(down_bias), q,
         ctx, lse, routes_t, gates_t, qdoc, kaug, vaug, kt, act, wq, kv_weight, row(gain_one))
+    gdown, gup, out, dx, go, gq, gkv, *vecs = finish(small, gdown, gup, (out, dx, go, gq, gkv), up_bias.shape[0])
     go = go.reshape(nexp, HEAD, D)
     gq = jnp.swapaxes(gq.reshape(nexp, HEAD, D), 1, 2)
-    vec = small.reshape(-1)
-    v = lambda i: vec[i * D:(i + 1) * D]
-    return (out[None], dx[None], v(3), v(4), gkv, gq, go, v(0), v(1), gup.astype(f32),
-            vec[5 * D:5 * D + up_bias.shape[0]], gdown.astype(f32), v(2))
+    gg2, gs2, gdb, gg1, gs1, gub = [v.reshape(-1) for v in vecs]
+    return (out[None], dx[None], gg1, gs1, gkv, gq, go, gg2, gs2, gup, gub, gdown, gdb)
 
 
 def solution(mesh):

time: 179 us -> 171 us (0.955)
  local copies, waits for them, and re-layouts: 8 us -> 0 us
  Pallas kernels: 163 us -> 170 us
  other arithmetic: 6.89 us -> 0 us
    pallas_call x0 -> x1, Pallas kernels: none -> 8.88 us  [finish(): pl.pallas_call(functools.partial(finish_kernel, nc), in_specs=[vm] + [any...]
    convert_element_type x2 -> x0, other arithmetic: 6.89 us -> none  [the longest x1 4.28 us: local(): gup.astype(f32)]
    unnamed x17 -> x0, local copies, waits for them, and re-layouts: 5.33 us -> none
    slice x2 -> x0, local copies, waits for them, and re-layouts: 2.67 us -> none  [the longest x1 1.36 us: local(): v = lambda i: vec[i * D:(i + 1) * D]]
    pallas_call x1, Pallas kernels: 115 us -> 113 us  [mega(): pl.pallas_call(functools.partial(mega_kernel, sizes, nf, nb, nexp, fb), g...]
where the time goes in v5:
time: 171 us
  Pallas kernels  170 us (99%)
    pallas_call x1, Pallas kernels, mega(): pl.pallas_call(functools.partial(mega_kernel, sizes, nf, nb, nexp, fb), g...  113 us
    pallas_call x1, Pallas kernels, head(): pl.pallas_call(functools.partial(head_kernel, sizes, nexp, nsem), in_spec...  33.2 us
    pallas_call x1, Pallas kernels, attn_fwd(): pl.pallas_call(functools.partial(attn_fwd_kernel, experts=experts, tok=to...  15 us
    pallas_call x1, Pallas kernels, finish(): pl.pallas_call(functools.partial(finish_kernel, nc), in_specs=[vm] + [any...  8.88 us

profile of v5, /device:TPU:0, one launch (start us, length us, event | category | flops | bytes accessed | tf_op | source)
XLA Modules:
  0.0 170.9 jit_solution(15580451754855801212)
XLA Ops:
  0.6 33.2 %head.1 = (bf16[768,512]{1,0:T(8,128)(2,1)}, bf16[1536,128]{1,0:T(8,128)(2,1)}, bf16[1536,128]{1,0:T(8,128)(2,1)}, bf16[64,1536]{1,0:T(8,128)(2,1)}, bf16[80,153...) custom-call(f32[768,512]{1,0:T(8,128)} %bitcast.28, ...), custom_call_target="tpu_custom_call" | custom-call | tf_op jit(solution)/shard_map/head/pallas_call | solution.py:774
  33.9 15.0 %attn_fwd.1 = (bf16[1536,768]{1,0:T(8,128)(2,1)}, bf16[6,64,1024]{2,1,0:T(8,128)(2,1)}, bf16[6,64,1024]{2,1,0:T(8,128)(2,1)}, f32[6,1,1024]{2,1,0:T(1,128)}) custom-call(bf16[768,512]{1,0:T(8,128)(2,1)} %get-tuple-element.48.act_ref.act1, bf16[1536,512]{1,0:T(8,128)(2,1)} %get-tuple-element.49.wq_ref.wq, s32[8,768]{1,0:T(8,128)} %bitcast.32, ...), custom_call_target="tpu_custom_call" | custom-call | tf_op jit(solution)/shard_map/attn_fwd/pallas_call | solution.py:122
  48.9 113.0 %mega.1 = (f32[768,512]{1,0:T(8,128)}, f32[768,512]{1,0:T(8,128)}, f32[192,512]{1,0:T(8,128)}, f32[192,512]{1,0:T(8,128)}, f32[512,128]{1,0:T(8,128)}, /*index=5...) custom-call(bf16[1536,768]{1,0:T(8,128)(2,1)} %get-tuple-element.53.cd, ...), custom_call_target="tpu_custom_call" | custom-call | tf_op jit(solution)/shard_map/mega/pallas_call | solution.py:613
  161.9 8.9 %post.1 = (f32[2048,512]{1,0:T(8,128)}, f32[512,2048]{1,0:T(8,128)}, f32[768,512]{1,0:T(8,128)}, f32[768,512]{1,0:T(8,128)}, f32[192,512]{1,0:T(8,128)}, /*index...) custom-call(f32[64,128]{1,0:T(8,128)} %get-tuple-element.62.sm, ...), custom_call_target="tpu_custom_call" | custom-call | tf_op jit(solution)/shard_map/post/pallas_call | solution.py:825

commit v6 on v5

--- a/solution.py
+++ b/solution.py
@@ -20,7 +20,7 @@
 LN2 = math.log(2.0)
 SMALL = 576
 KBB = 384
-STRIDE = 7
+STRIDE = 8
 JOIN = 2
 SAFE = 50.0
 NN = (((1,), (0,)), ((), ()))
@@ -310,12 +310,12 @@
                 c.start()
 
 
-def greet(here, groups):
-    devices = {tuple(sorted(f)) for g in groups for f in subsets(g)}
+def meet(here, groups):
+    devices = sorted({tuple(sorted(f)) for g in groups for f in subsets(g)})
     bar = pltpu.get_barrier_semaphore()
-    for f in sorted(devices):
+    for f in devices:
         pl.semaphore_signal(bar, inc=1, device_id=here.across(f), device_id_type=MESH)
-    pl.semaphore_wait(bar, len(devices))
+    return lambda: pl.semaphore_wait(bar, len(devices))
 
 
 def dense_parts(n, orders):
@@ -375,8 +375,9 @@
         t0 = ticks.index((j * JOIN + JOIN - 1, 2)) if j < nf // JOIN else ticks.index((nf, 0))
         for k in range(max(c.nsteps for c in group)):
             todo = [(c, k) for c in group if k < c.nsteps]
-            if t0 + STRIDE * k // 2 < len(ticks):
-                table.setdefault(ticks[t0 + STRIDE * k // 2], []).extend(todo)
+            at = t0 + (1 + STRIDE * (k - 1) // 2 if k else 0)
+            if at < len(ticks):
+                table.setdefault(ticks[at], []).extend(todo)
             else:
                 late.extend(todo)
 
@@ -405,6 +406,7 @@
 
     @pl.when(s == 0)
     def _():
+        met = meet(here, [g for group in flat(chains) for c in group for g in c.groups])
         m = tok[...] + dot(cd[...], wo[...], TN)
         mid[...] = m
         cen = m - jnp.mean(m, axis=-1, keepdims=True)
@@ -417,7 +419,7 @@
         dffn[...] = cot[...].astype(bf16)
         out[...] = m + downb[...]
         dx[...] = jnp.zeros_like(dx)
-        greet(here, [g for group in flat(chains) for c in group for g in c.groups])
+        met()
 
     @pl.when(s < nf)
     def _():
@@ -662,14 +664,15 @@
     fetch = [pltpu.make_async_copy(up_h, upf, ls.at[0]), pltpu.make_async_copy(down_h, downf, ls.at[1])]
     for c in fetch:
         c.start()
+    b = mesh_bits(sizes)
+    exact = [tuple(b["exp"][1:]), tuple(b["dp"] + b["ctx"])] if small_mesh(sizes) else []
+    met = meet(here, [(x,) for a in AXES for x in b[a]] + exact)
     mine = lax.axis_index("exp") * shard
     for j in range(nexp):
         r = pl.ds(pl.multiple_of(mine + j * HEAD, HEAD), HEAD)
         wqs[r, :] = wq3[j].astype(bf16)
         wos[r, :] = wo3[j].astype(bf16)
-    b = mesh_bits(sizes)
-    exact = [tuple(b["exp"][1:]), tuple(b["dp"] + b["ctx"])] if small_mesh(sizes) else []
-    greet(here, [(x,) for a in AXES for x in b[a]] + exact)
+    met()
     count = [0]
 
     def send(buf, moves):
@@ -844,7 +847,7 @@
         down_weight)
     routes_t = routes[0].T
     gates_t = route_gates[0].T
-    cd, q, ctx, lse = attn_fwd(act, wq, routes_t, gates_t, qdoc, kaug, vt, KB=384)
+    cd, q, ctx, lse = attn_fwd(act, wq, routes_t, gates_t, qdoc, kaug, vt, KB=768)
     out, dx, go, gq, gkv, small, gdown, gup = mega(
         sizes, nexp, cd, wo, x, cotangent[0], row(gain_two), row(shift_two), up, row(up_bias), down, row(down_bias), q,
         ctx, lse, routes_t, gates_t, qdoc, kaug, vaug, kt, act, wq, kv_weight, row(gain_one))

time: 171 us -> 168 us (0.982)
  Pallas kernels: 170 us -> 167 us
    pallas_call x1, Pallas kernels: 113 us -> 109 us  [mega(): pl.pallas_call(functools.partial(mega_kernel, sizes, nf, nb, nexp, fb), g...]
where the time goes in v6:
time: 168 us; the launch traced here: 167 us
  Pallas kernels  167 us (99%)
    pallas_call x1, Pallas kernels, mega(): pl.pallas_call(functools.partial(mega_kernel, sizes, nf, nb, nexp, fb), g...  109 us
    pallas_call x1, Pallas kernels, head(): pl.pallas_call(functools.partial(head_kernel, sizes, nexp, nsem), in_spec...  33.2 us
    pallas_call x1, Pallas kernels, attn_fwd(): pl.pallas_call(functools.partial(attn_fwd_kernel, experts=experts, tok=to...  15.6 us
    pallas_call x1, Pallas kernels, finish(): pl.pallas_call(functools.partial(finish_kernel, nc), in_specs=[vm] + [any...  8.88 us

profile of v6, /device:TPU:0, one launch (start us, length us, event | category | flops | bytes accessed | tf_op | source)
XLA Modules:
  0.0 167.4 jit_solution(2105695833709963075)
XLA Ops:
  0.6 33.2 %head.1 = (bf16[768,512]{1,0:T(8,128)(2,1)}, bf16[1536,128]{1,0:T(8,128)(2,1)}, bf16[1536,128]{1,0:T(8,128)(2,1)}, bf16[64,1536]{1,0:T(8,128)(2,1)}, bf16[80,153...) custom-call(f32[768,512]{1,0:T(8,128)} %bitcast.28, ...), custom_call_target="tpu_custom_call" | custom-call | tf_op jit(solution)/shard_map/head/pallas_call | solution.py:777
  33.9 15.6 %attn_fwd.1 = (bf16[1536,768]{1,0:T(8,128)(2,1)}, bf16[6,64,1024]{2,1,0:T(8,128)(2,1)}, bf16[6,64,1024]{2,1,0:T(8,128)(2,1)}, f32[6,1,1024]{2,1,0:T(1,128)}) custom-call(bf16[768,512]{1,0:T(8,128)(2,1)} %get-tuple-element.48.act_ref.act1, bf16[1536,512]{1,0:T(8,128)(2,1)} %get-tuple-element.49.wq_ref.wq, s32[8,768]{1,0:T(8,128)} %bitcast.32, ...), custom_call_target="tpu_custom_call" | custom-call | tf_op jit(solution)/shard_map/attn_fwd/pallas_call | solution.py:122
  49.4 108.9 %mega.1 = (f32[768,512]{1,0:T(8,128)}, f32[768,512]{1,0:T(8,128)}, f32[192,512]{1,0:T(8,128)}, f32[192,512]{1,0:T(8,128)}, f32[512,128]{1,0:T(8,128)}, /*index=5...) custom-call(bf16[1536,768]{1,0:T(8,128)(2,1)} %get-tuple-element.53.cd, ...), custom_call_target="tpu_custom_call" | custom-call | tf_op jit(solution)/shard_map/mega/pallas_call | solution.py:615
  158.4 8.9 %post.1 = (f32[2048,512]{1,0:T(8,128)}, f32[512,2048]{1,0:T(8,128)}, f32[768,512]{1,0:T(8,128)}, f32[768,512]{1,0:T(8,128)}, f32[192,512]{1,0:T(8,128)}, /*index...) custom-call(f32[64,128]{1,0:T(8,128)} %get-tuple-element.62.sm, ...), custom_call_target="tpu_custom_call" | custom-call | tf_op jit(solution)/shard_map/post/pallas_call | solution.py:828

commit v7 on v6

--- a/solution.py
+++ b/solution.py
@@ -793,6 +793,10 @@
     moves, wide_o, moved, vec_o = refs[:5], refs[5:7], refs[7:12], refs[12:18]
     lows, wides, vias, si, so = refs[18:20], refs[20:22], refs[22:27], refs[27], refs[28]
     ins, outs, parts = [], [], []
+    for k, (a, via, b) in enumerate(zip(moves, vias, moved)):
+        ins.append(pltpu.make_async_copy(a, via, si.at[2 * nc + k]))
+        outs.append(pltpu.make_async_copy(via, b, so.at[2 * nc + k]))
+        parts.append(None)
     for i, src in enumerate((gd, gu)):
         n = src.shape[0] // nc
         for j in range(nc):
@@ -800,10 +804,6 @@
             ins.append(pltpu.make_async_copy(src.at[r, :], lows[i].at[r, :], si.at[i * nc + j]))
             outs.append(pltpu.make_async_copy(wides[i].at[r, :], wide_o[i].at[r, :], so.at[i * nc + j]))
             parts.append((i, r))
-    for k, (a, via, b) in enumerate(zip(moves, vias, moved)):
-        ins.append(pltpu.make_async_copy(a, via, si.at[2 * nc + k]))
-        outs.append(pltpu.make_async_copy(via, b, so.at[2 * nc + k]))
-        parts.append(None)
     for c in ins:
         c.start()
     at = 0
@@ -821,7 +821,7 @@
         c.wait()
 
 
-def finish(sm, gd, gu, others, nub, nc=4):
+def finish(sm, gd, gu, others, nub, nc=8):
     any_, vm = pl.BlockSpec(memory_space=pl.ANY), pl.BlockSpec(memory_space=pltpu.VMEM)
     sd, v = jax.ShapeDtypeStruct, pltpu.VMEM
     sem = pltpu.SemaphoreType.DMA

time: 168 us -> 167 us (level)
  no operation moved by 1% of the time
where the time goes in v7:
time: 167 us
  Pallas kernels  166 us (99%)
    pallas_call x1, Pallas kernels, mega(): pl.pallas_call(functools.partial(mega_kernel, sizes, nf, nb, nexp, fb), g...  109 us
    pallas_call x1, Pallas kernels, head(): pl.pallas_call(functools.partial(head_kernel, sizes, nexp, nsem), in_spec...  33.2 us
    pallas_call x1, Pallas kernels, attn_fwd(): pl.pallas_call(functools.partial(attn_fwd_kernel, experts=experts, tok=to...  15.6 us
    pallas_call x1, Pallas kernels, finish(): pl.pallas_call(functools.partial(finish_kernel, nc), in_specs=[vm] + [any...  8.49 us

profile of v7, /device:TPU:0, one launch (start us, length us, event | category | flops | bytes accessed | tf_op | source)
XLA Modules:
  0.0 167.0 jit_solution(11464471515357355765)
XLA Ops:
  0.6 33.2 %head.1 = (bf16[768,512]{1,0:T(8,128)(2,1)}, bf16[1536,128]{1,0:T(8,128)(2,1)}, bf16[1536,128]{1,0:T(8,128)(2,1)}, bf16[64,1536]{1,0:T(8,128)(2,1)}, bf16[80,153...) custom-call(f32[768,512]{1,0:T(8,128)} %bitcast.28, ...), custom_call_target="tpu_custom_call" | custom-call | tf_op jit(solution)/shard_map/head/pallas_call | solution.py:777
  33.9 15.6 %attn_fwd.1 = (bf16[1536,768]{1,0:T(8,128)(2,1)}, bf16[6,64,1024]{2,1,0:T(8,128)(2,1)}, bf16[6,64,1024]{2,1,0:T(8,128)(2,1)}, f32[6,1,1024]{2,1,0:T(1,128)}) custom-call(bf16[768,512]{1,0:T(8,128)(2,1)} %get-tuple-element.48.act_ref.act1, bf16[1536,512]{1,0:T(8,128)(2,1)} %get-tuple-element.49.wq_ref.wq, s32[8,768]{1,0:T(8,128)} %bitcast.32, ...), custom_call_target="tpu_custom_call" | custom-call | tf_op jit(solution)/shard_map/attn_fwd/pallas_call | solution.py:122
  49.4 108.9 %mega.1 = (f32[768,512]{1,0:T(8,128)}, f32[768,512]{1,0:T(8,128)}, f32[192,512]{1,0:T(8,128)}, f32[192,512]{1,0:T(8,128)}, f32[512,128]{1,0:T(8,128)}, /*index=5...) custom-call(bf16[1536,768]{1,0:T(8,128)(2,1)} %get-tuple-element.53.cd, ...), custom_call_target="tpu_custom_call" | custom-call | tf_op jit(solution)/shard_map/mega/pallas_call | solution.py:615
  158.4 8.5 %post.1 = (f32[2048,512]{1,0:T(8,128)}, f32[512,2048]{1,0:T(8,128)}, f32[768,512]{1,0:T(8,128)}, f32[768,512]{1,0:T(8,128)}, f32[192,512]{1,0:T(8,128)}, /*index...) custom-call(f32[64,128]{1,0:T(8,128)} %get-tuple-element.62.sm, ...), custom_call_target="tpu_custom_call" | custom-call | tf_op jit(solution)/shard_map/post/pallas_call | solution.py:828
